TPU v7x, 32 devices: a whole 2x2x4 slice. The times are simulated.
32 devices in a mesh: dp: 8 (over y, x, core), tensor: 4 (over z).
Axes of the slice: x: 2, y: 2, z: 4, core: 2. Of those that a mesh axis runs over, the one named last changes fastest.
Arguments:
- tokens: bfloat16 [32, 1024, 512], P(('dp', 'tensor')), may hold values from -6 to 6
- timestep: int32 [32], P(('dp', 'tensor')), may hold values from 0 to 999
- segment_ids: int32 [32, 1024], P('dp'), may hold values from 0 to 7, never falling along the last dimension, each value on 1 to 512 neighbouring positions
- span_lengths: int32 [32], P('dp'), may hold values from 512 to 1024
- w_qkv: float32 [3, 512, 512], P(None, 'dp', 'tensor'), may hold values from -0.25 to 0.25
- w_out_t: float32 [512, 512], P('dp', 'tensor'), may hold values from -1.5 to 1.5
- w_up: float32 [512, 2048], P('dp', 'tensor'), may hold values from -0.25 to 0.25
- w_down_t: float32 [512, 2048], P('dp', 'tensor'), may hold values from -0.125 to 0.125
- w_time: float32 [512, 512], replicated, may hold values from -0.25 to 0.25
- b_time: float32 [512], replicated, may hold values from -3 to 3
- ln1_gain: float32 [512], replicated, may hold values from 0.1 to 1.9
- ln1_bias: float32 [512], replicated, may hold values from -3 to 3
- ln2_gain: float32 [512], replicated, may hold values from 0.1 to 1.9
- ln2_bias: float32 [512], replicated, may hold values from -3 to 3
- b_up: float32 [2048], replicated, may hold values from -3 to 3
- b_down: float32 [512], replicated, may hold values from -3 to 3
- cotangent: bfloat16 [32, 1024, 512], P(('dp', 'tensor')), may hold values from -6 to 6
Outputs:
- layer_out: bfloat16 [32, 1024, 512], P(('dp', 'tensor'))
- grad_tokens: float32 [32, 1024, 512], P(('dp', 'tensor'))
- grad_w_qkv: float32 [3, 512, 512], P(None, 'dp', 'tensor')
- grad_w_out_t: float32 [512, 512], P('dp', 'tensor')
- grad_w_up: float32 [512, 2048], P('dp', 'tensor')
- grad_w_down_t: float32 [512, 2048], P('dp', 'tensor')
- grad_w_time: float32 [512, 512], replicated
- grad_b_time: float32 [512], replicated
- grad_ln1_gain: float32 [512], replicated
- grad_ln1_bias: float32 [512], replicated
- grad_ln2_gain: float32 [512], replicated
- grad_ln2_bias: float32 [512], replicated
- grad_b_up: float32 [2048], replicated
- grad_b_down: float32 [512], replicated
Inputs may be any that keep to these rules, and one draw needn't show every extreme that they name: `segment_ids`: never falls along a row; each document has 1 to 512 positions and one has exactly that many.
All inputs are finite; a program needn't handle non-finite values.
Results may differ from a plain program's by a relative error of at most 0.013.
Values may be sent and summed in bfloat16 or wider, within the bound.
A program may use at most 192 MiB of HBM per device.

v0:
```python
import math

import jax
import jax.numpy as jnp
from jax import lax
from jax.sharding import PartitionSpec as P

HS = 64
FF = 2048


highest = lax.Precision.HIGHEST
epsilon = 1e-05
masked_score = -1e30


def split_up(value, dim, count):
    before, after = (value.shape[:dim], value.shape[dim + 1 :])
    return jnp.moveaxis(value.reshape(*before, count, -1, *after), dim, 0)


def sent_and_summed(value, axis, dim):
    count = lax.axis_size(axis)
    parts = lax.all_to_all(split_up(value, dim, count), axis, 0, 0, tiled=True)
    return jnp.sum(parts.astype(jnp.float32), axis=0)


def side_by_side(arrays, axis, dim, along):
    ends, at = ([], 0)
    for a in arrays[:-1]:
        at += a.shape[along]
        ends.append(at)
    both = jnp.concatenate(arrays, axis=along)
    return tuple(jnp.split(sent_and_summed(both, axis, dim), ends, axis=along))


def norm_layer(values, gain_vec, shift_vec):
    row_mean = jnp.mean(values, axis=-1, keepdims=True)
    centred = values - row_mean
    variance = jnp.mean(centred * centred, axis=-1, keepdims=True)
    return centred * lax.rsqrt(variance + epsilon) * gain_vec + shift_vec


def time_features(timestep, features):
    half_width = features // 2
    frequency = jnp.exp(-math.log(10000.0) * jnp.arange(half_width, dtype=jnp.float32) / half_width)
    angles = timestep.astype(jnp.float32)[:, None] * frequency[None, :]
    return jnp.concatenate([jnp.sin(angles), jnp.cos(angles)], axis=1)


def allowed_keys(segment, length):
    places = jnp.arange(segment.shape[0], dtype=jnp.int32)
    same_doc = segment[:, None] == segment[None, :]
    is_valid = (places < length)[None, :] | (places[:, None] == places[None, :])
    return same_doc & is_valid


def gelu_tanh(values):
    return jax.nn.gelu(values, approximate=True)


def split_heads(values):
    return values.reshape(values.shape[0], values.shape[1] // HS, HS)


def head_scores(query_heads, key_heads, allowed):
    scores = jnp.einsum(
        "qhe,khe->hqk", query_heads, key_heads, preferred_element_type=jnp.float32
    ) * (1.0 / math.sqrt(HS))
    return jnp.where(allowed[None], scores, masked_score)


def attend_forward(packed):
    query_heads = split_heads(packed[0])
    key_heads = split_heads(packed[1])
    value_heads = split_heads(packed[2])
    scores = head_scores(query_heads, key_heads, allowed_keys(packed[3], packed[4]))
    row_max = jnp.max(scores, axis=-1, keepdims=True)
    raised = jnp.exp(scores - row_max)
    row_total = jnp.sum(raised, axis=-1, keepdims=True)
    probs_low = (raised / row_total).astype(jnp.bfloat16)
    mixed = jnp.einsum("hqk,khe->qhe", probs_low, value_heads, preferred_element_type=jnp.float32)
    return (mixed.reshape(packed[0].shape).astype(jnp.bfloat16), row_max + jnp.log(row_total))


def attend_backward(packed):
    query_heads = split_heads(packed[0])
    key_heads = split_heads(packed[1])
    value_heads = split_heads(packed[2])
    grad_heads = split_heads(packed[3])
    scores = head_scores(query_heads, key_heads, allowed_keys(packed[5], packed[6]))
    attn_probs = jnp.exp(scores - packed[4])
    probs_low = attn_probs.astype(jnp.bfloat16)
    grad_values = jnp.einsum(
        "hqk,qhe->khe", probs_low, grad_heads, preferred_element_type=jnp.float32
    )
    grad_probs = jnp.einsum(
        "qhe,khe->hqk", grad_heads, value_heads, preferred_element_type=jnp.float32
    )
    row_delta = jnp.sum(attn_probs * grad_probs, axis=-1, keepdims=True)
    grad_scores = (attn_probs * (grad_probs - row_delta)).astype(jnp.bfloat16)
    score_scale = 1.0 / math.sqrt(HS)
    grad_queries = (
        jnp.einsum("hqk,khe->qhe", grad_scores, key_heads, preferred_element_type=jnp.float32)
        * score_scale
    )
    grad_keys = (
        jnp.einsum("hqk,qhe->khe", grad_scores, query_heads, preferred_element_type=jnp.float32)
        * score_scale
    )
    shape_rows = packed[0].shape
    return jnp.stack(
        [
            grad_queries.reshape(shape_rows),
            grad_keys.reshape(shape_rows),
            grad_values.reshape(shape_rows),
        ]
    ).astype(jnp.bfloat16)


def shards(
    tokens,
    timestep,
    segment_ids,
    span_lengths,
    w_qkv,
    w_out_t,
    w_up,
    w_down_t,
    w_time,
    b_time,
    ln1_gain,
    ln1_bias,
    ln2_gain,
    ln2_bias,
    b_up,
    b_down,
    cotangent,
):
    tensor_place = lax.axis_index("tensor")
    qkv_copy, out_copy, up_copy, down_copy = (
        lax.all_gather(w_qkv.astype(jnp.bfloat16), "dp", axis=1, tiled=True),
        lax.all_gather(w_out_t.astype(jnp.bfloat16), "dp", axis=0, tiled=True),
        lax.all_gather(w_up.astype(jnp.bfloat16), "dp", axis=0, tiled=True),
        lax.all_gather(w_down_t.astype(jnp.bfloat16), "dp", axis=0, tiled=True),
    )
    bias_up_cols = lax.dynamic_slice_in_dim(
        b_up, tensor_place * up_copy.shape[1], up_copy.shape[1], 0
    )
    ff_cols = up_copy.shape[1]
    time_emb = time_features(timestep, tokens.shape[2])
    time_proj = jnp.dot(time_emb, w_time, precision=highest) + b_time
    start = tokens.astype(jnp.float32) + time_proj[:, None, :]
    normed_one = norm_layer(start, ln1_gain, ln1_bias).astype(jnp.bfloat16)
    normed_all = lax.all_gather(normed_one, "tensor", axis=0, tiled=True)
    qkv_act = jnp.einsum(
        "nsd,cde->cnse", normed_all, qkv_copy, preferred_element_type=jnp.float32
    ).astype(jnp.bfloat16)
    mixed, log_total = lax.map(
        attend_forward, (qkv_act[0], qkv_act[1], qkv_act[2], segment_ids, span_lengths)
    )
    part_rows = mixed
    attn_out = lax.psum_scatter(
        jnp.einsum("nse,de->nsd", part_rows, out_copy, preferred_element_type=jnp.float32),
        "tensor",
        scatter_dimension=0,
        tiled=True,
    )
    middle = start + attn_out
    normed_two = norm_layer(middle, ln2_gain, ln2_bias).astype(jnp.bfloat16)
    second_all = lax.all_gather(normed_two, "tensor", axis=0, tiled=True)
    upper = (
        jnp.einsum("nsd,df->nsf", second_all, up_copy, preferred_element_type=jnp.float32)
        + bias_up_cols
    )
    activated = gelu_tanh(upper).astype(jnp.bfloat16)
    part_rows = activated
    ffn_out = lax.psum_scatter(
        jnp.einsum("nsf,df->nsd", part_rows, down_copy, preferred_element_type=jnp.float32).astype(
            jnp.bfloat16
        ),
        "tensor",
        scatter_dimension=0,
        tiled=True,
    ).astype(jnp.float32)
    layer_out = (middle + ffn_out + b_down).astype(jnp.bfloat16)
    grad_b_down = jnp.sum(cotangent.astype(jnp.float32), axis=(0, 1))
    grad_out_all = lax.all_gather(cotangent, "tensor", axis=0, tiled=True)
    grad_down = jnp.einsum(
        "nsd,nsf->df", grad_out_all, activated, preferred_element_type=jnp.float32
    )
    grad_act = jnp.einsum(
        "nsd,df->nsf", grad_out_all, down_copy, preferred_element_type=jnp.float32
    )
    gelu_value, gelu_pull = jax.vjp(gelu_tanh, upper)
    grad_upper = gelu_pull(grad_act)[0].astype(jnp.bfloat16)
    grad_bias_cols = jnp.sum(grad_upper.astype(jnp.float32), axis=(0, 1))
    grad_up = jnp.einsum("nsd,nsf->df", second_all, grad_upper, preferred_element_type=jnp.float32)
    part_rows = grad_upper
    grad_normed_two = lax.psum_scatter(
        jnp.einsum("nsf,df->nsd", part_rows, up_copy, preferred_element_type=jnp.float32).astype(
            jnp.bfloat16
        ),
        "tensor",
        scatter_dimension=0,
        tiled=True,
    ).astype(jnp.float32)
    norm_two_value, norm_two_pull = jax.vjp(norm_layer, middle, ln2_gain, ln2_bias)
    grad_middle_norm, grad_gain_two, grad_bias_two = norm_two_pull(grad_normed_two)
    grad_middle = cotangent.astype(jnp.float32) + grad_middle_norm
    grad_attn = grad_middle.astype(jnp.bfloat16)
    grad_attn_all = lax.all_gather(grad_attn, "tensor", axis=0, tiled=True)
    grad_out_w = jnp.einsum("nsd,nse->de", grad_attn_all, mixed, preferred_element_type=jnp.float32)
    grad_mixed = jnp.einsum(
        "nsd,de->nse", grad_attn_all, out_copy, preferred_element_type=jnp.float32
    ).astype(jnp.bfloat16)
    grad_qkv_act = lax.map(
        attend_backward,
        (qkv_act[0], qkv_act[1], qkv_act[2], grad_mixed, log_total, segment_ids, span_lengths),
    )
    grad_qkv_w = jnp.einsum(
        "nsd,ncse->cde", normed_all, grad_qkv_act, preferred_element_type=jnp.float32
    )
    part_rows = grad_qkv_act
    grad_normed_one = lax.psum_scatter(
        jnp.einsum("ncse,cde->nsd", part_rows, qkv_copy, preferred_element_type=jnp.float32).astype(
            jnp.bfloat16
        ),
        "tensor",
        scatter_dimension=0,
        tiled=True,
    ).astype(jnp.float32)
    norm_one_value, norm_one_pull = jax.vjp(norm_layer, start, ln1_gain, ln1_bias)
    grad_start_norm, grad_gain_one, grad_bias_one = norm_one_pull(grad_normed_one)
    grad_tokens = grad_middle + grad_start_norm
    grad_time_rows = jnp.sum(grad_tokens, axis=1)
    grad_time_w = jnp.dot(time_emb.T, grad_time_rows, precision=highest)
    grad_time_bias = jnp.sum(grad_time_rows, axis=0)
    grad_bias_up = lax.dynamic_update_slice_in_dim(
        jnp.zeros((FF,), jnp.float32), grad_bias_cols, tensor_place * ff_cols, 0
    )
    shard_qkv, shard_out, shard_up, shard_down = (
        sent_and_summed(grad_qkv_w.astype(jnp.bfloat16), "dp", 1),
        *side_by_side(
            (
                grad_out_w.astype(jnp.bfloat16),
                grad_up.astype(jnp.bfloat16),
                grad_down.astype(jnp.bfloat16),
            ),
            "dp",
            0,
            1,
        ),
    )
    summed = lax.psum(
        (
            grad_time_w,
            grad_time_bias,
            grad_gain_one,
            grad_bias_one,
            grad_gain_two,
            grad_bias_two,
            grad_bias_up,
            grad_b_down,
        ),
        ("dp", "tensor"),
    )
    return (
        layer_out,
        grad_tokens,
        shard_qkv,
        shard_out,
        shard_up,
        shard_down,
        summed[0],
        summed[1],
        summed[2],
        summed[3],
        summed[4],
        summed[5],
        summed[6],
        summed[7],
    )


def solution(mesh):
    return jax.shard_map(
        shards,
        mesh=mesh,
        in_specs=(
            P(("dp", "tensor"), None, None),
            P(("dp", "tensor")),
            P("dp", None),
            P("dp"),
            P(None, "dp", "tensor"),
            P("dp", "tensor"),
            P("dp", "tensor"),
            P("dp", "tensor"),
            P(),
            P(),
            P(),
            P(),
            P(),
            P(),
            P(),
            P(),
            P(("dp", "tensor"), None, None),
        ),
        out_specs=(
            P(("dp", "tensor"), None, None),
            P(("dp", "tensor"), None, None),
            P(None, "dp", "tensor"),
            P("dp", "tensor"),
            P("dp", "tensor"),
            P("dp", "tensor"),
            P(),
            P(),
            P(),
            P(),
            P(),
            P(),
            P(),
            P(),
        ),
        check_vma=False,
    )
```

profile of v0, /device:TPU:0, one launch (start us, length us, event | category | flops | bytes accessed | tf_op | source)
XLA Modules:
  0.0 1040.7 jit_solution(14734776910179383602)
XLA Ops:
  11.3 1.7 multiply_reduce_fusion.2
  13.0 2.7 add_convert_fusion.2
  15.9 10.7 %all_gather.26 = bf16[512,128]{1,0:T(8,128)(2,1)S(1)} all-gather(bf16[64,128]{1,0:T(8,128)(2,1)S(1)} %convert_element_type.133), channel_id=1, replica_groups=mesh['dp'=8,'tensor'=4] {'dp'}, dimensions={0}, use_global_device_ids=true | all-gather | bytes 147456 | tf_op jit(solution)/shard_map/all_gather | solution.py:143
  26.6 9.7 all_gather.25
  36.3 63.1 %all-gather.5.cloned.1.call-done = bf16[4,1024,512]{2,1,0:T(8,128)(2,1)} async-done(((bf16[1,1024,512]{2,1,0:T(8,128)(2,1)}), bf16[4,1024,512]{2,1,0:T(8,128)(2,1)}) %all-gather.5.cloned.1.call-update) | async-done | bytes 4194320 | tf_op jit(solution)/shard_map/all_gather | solution.py:155
  99.4 4.5 convert_bitcast_fusion
  109.8 42.4 %while.22 = (s32[]{:T(128)}, bf16[4,1024,128]{1,2,0:T(8,128)(2,1)S(1)}, f32[4,2,1024,1]{2,1,3,0:T(2,128)S(1)}, bf16[4,1024,128]{1,2,0:T(8,128)(2,1)S(1)}, s32[4,...) while((s32[]{:T(128)}, ...), condition=%wide.region_5.6_spmd, body=%wide.region_2.5_spmd.sunk | while | flops 566361088 | bytes 32585864 | solution.py:159
  113.6 1.9 fusion.134
  115.5 2.0 fusion.135
  117.5 2.8 fusion.136
  124.2 1.9 fusion.134
  126.1 2.0 fusion.135
  128.1 2.8 fusion.136
  134.8 1.9 fusion.134
  136.7 2.0 fusion.135
  138.7 2.8 fusion.136
  145.4 1.9 fusion.134
  147.3 2.0 fusion.135
  149.3 2.8 fusion.136
  152.2 4.5 fusion.69
  156.9 143.1 %reduce-scatter.5.cloned.1.call-done = f32[1,1024,512]{2,1,0:T(8,128)} async-done(((f32[4,1024,512]{2,1,0:T(8,128)}), f32[1,1024,512]{2,1,0:T(8,128)}) %reduce-scatter.5.cloned.1.call-update) | async-done | bytes 2097168 | tf_op jit(solution)/shard_map/reduce_scatter | solution.py:163
  299.9 1.9 fusion.79
  305.2 10.2 all_gather.29
  315.4 9.8 all_gather.28
  325.2 60.2 %all-gather.7.cloned.1.call-done = bf16[4,1024,512]{2,1,0:T(8,128)(2,1)} async-done(((bf16[1,1024,512]{2,1,0:T(8,128)(2,1)}), bf16[4,1024,512]{2,1,0:T(8,128)(2,1)}) %all-gather.7.cloned.1.call-update) | async-done | bytes 4194320 | tf_op jit(solution)/shard_map/all_gather | solution.py:171
  385.5 8.0 fusion.64
  393.4 72.8 %all-gather.9.cloned.1.call-done = bf16[4,1024,512]{2,1,0:T(8,128)(2,1)} async-done(((bf16[1,1024,512]{2,1,0:T(8,128)(2,1)}), bf16[4,1024,512]{2,1,0:T(8,128)(2,1)}) %all-gather.9.cloned.1.call-update) | async-done | bytes 4194320 | tf_op jit(solution)/shard_map/all_gather | solution.py:188
  466.2 10.3 convert_reduce_fusion
  476.5 2.0 copy-done.47
  478.5 4.5 convolution_convert_fusion
  483.1 8.8 convolution_convert_fusion.1
  491.9 66.5 %reduce-scatter.9.cloned.1.call-done = bf16[1,1024,512]{2,1,0:T(8,128)(2,1)} async-done(((bf16[4,1024,512]{2,1,0:T(8,128)(2,1)}), bf16[1,1024,512]{2,1,0:T(8,128)(2,1)}) %reduce-scatter.9.cloned.1.call-update) | async-done | bytes 1048592 | tf_op jit(solution)/shard_map/reduce_scatter | solution.py:200
  558.5 2.7 fusion.40
  561.2 76.8 %reduce-scatter.7.cloned.1.call-done = bf16[1,1024,512]{2,1,0:T(8,128)(2,1)} async-done(((bf16[4,1024,512]{2,1,0:T(8,128)(2,1)}), bf16[1,1024,512]{2,1,0:T(8,128)(2,1)}) %reduce-scatter.7.cloned.1.call-update) | async-done | bytes 1048592 | tf_op jit(solution)/shard_map/reduce_scatter | solution.py:178
  638.0 3.2 fusion.78
  644.2 81.2 %all-gather.11.cloned.1.call-done = bf16[4,1024,512]{2,1,0:T(8,128)(2,1)} async-done(((bf16[1,1024,512]{2,1,0:T(8,128)(2,1)}), bf16[4,1024,512]{2,1,0:T(8,128)(2,1)}) %all-gather.11.cloned.1.call-update) | async-done | bytes 4194320 | tf_op jit(solution)/shard_map/all_gather | solution.py:212
  725.3 3.4 convolution_convert_fusion.2
  728.8 72.6 %while.23 = (s32[]{:T(128)}, bf16[4,3,1024,128]{2,3,1,0:T(8,128)(2,1)}, bf16[4,1024,128]{1,2,0:T(8,128)(2,1)}, s32[4,1024]{1,0:T(4,128)S(1)}, s32[4]{0:T(128)S(1...) while((s32[]{:T(128)}, ...), condition=%wide.region_15.16_spmd, body=%wide.region_13.15_spmd.sunk | while | flops 1380842496 | bytes 73996440 | solution.py:217
  735.1 2.5 fusion.149
  737.6 3.4 multiply_reduce_fusion.4
  741.1 2.7 multiply_convert_fusion.5
  753.3 2.5 fusion.149
  755.8 3.4 multiply_reduce_fusion.4
  759.2 2.7 multiply_convert_fusion.5
  771.4 2.5 fusion.149
  773.9 3.4 multiply_reduce_fusion.4
  777.4 2.7 multiply_convert_fusion.5
  789.6 2.5 fusion.149
  792.1 3.4 multiply_reduce_fusion.4
  795.5 2.7 multiply_convert_fusion.5
  801.4 6.3 bitcast_convert_fusion
  809.3 6.5 fusion.47
  815.9 7.1 fusion.55
  825.3 5.1 fusion.57
  831.4 3.8 all-to-all-start
  835.2 47.9 %reduce-scatter.11.cloned.1.call-done = bf16[1,1024,512]{2,1,0:T(8,128)(2,1)} async-done(((bf16[4,1024,512]{2,1,0:T(8,128)(2,1)}), bf16[1,1024,512]{2,1,0:T(8,128)(2,1)}) %reduce-scatter.11.cloned.1.call-update) | async-done | bytes 1048592 | tf_op jit(solution)/shard_map/reduce_scatter | solution.py:225
  883.2 2.7 convert_reduce_fusion.1
  885.9 3.1 fusion.41
  889.0 4.2 all-to-all-start.1
  893.3 4.4 fusion.77
  900.1 10.1 all-to-all-done.1
  913.0 41.1 %all-reduce = (f32[512]{0:T(512)}, f32[512]{0:T(512)}, f32[512]{0:T(512)}, f32[512]{0:T(512)}, f32[512]{0:T(512)}, /*index=5*/f32[2048]{0:T(1024)}, f32[512]{0:T(512)}) all-reduce(f32[512]{0:T(512)} %copy-done.32, f32[512]{0:T(512)S(1)} %copy-done.38, f32[512]{0:T(512)S(1)} %copy-done.37, ...), channel_id=1, replica_groups=mesh['dp'=8,'tensor'=4] {'dp','tensor'}, use_global_device_ids=true, to_apply=%region_23.24 | all-reduce | flops 5120 | bytes 40960 | tf_op jit(solution)/shard_map/psum | solution.py:255
  954.1 77.5 %all-reduce.3.cloned.1.call-done = f32[512,512]{1,0:T(8,128)} async-done(((f32[512,512]{1,0:T(8,128)}), f32[512,512]{1,0:T(8,128)}) %all-reduce.3.cloned.1.call-update) | async-done | bytes 1048592 | tf_op jit(solution)/shard_map/psum | solution.py:255
  1031.6 2.3 copy.119
  (238 shorter events, 78.8 us)
Async XLA Ops:
  7.2 1.2 copy-start
  7.2 8.6 copy-start.27
  7.2 8.6 copy-start.21
  7.2 92.1 %all-gather.5.cloned.1.call-start = ((), (), s32[]{:S(2)}) async-start(), calls=%async_computation.6 | async-start | bytes 5242880 | tf_op jit(solution)/shard_map/all_gather | solution.py:155
  8.1 1.0 copy-start.33
  8.1 3.2 copy-start.35
  9.7 290.2 %copy-start.18 = (f32[512]{0:T(512)}, f32[512]{0:T(512)S(1)}, u32[]{:S(2)}) copy-start(f32[512]{0:T(512)S(1)} %add.138) | copy-start | bytes 6148
  11.3 4.6 copy-start.14
  13.0 2.9 copy-start.25
  13.0 2.8 copy-start.22
  15.7 284.2 %reduce-scatter.5.cloned.1.call-start = ((), (), s32[]{:S(2)}) async-start(), calls=%async_computation.7 | async-start | bytes 10485760 | tf_op jit(solution)/shard_map/reduce_scatter | solution.py:163
  36.3 67.6 %copy-start.12 = (bf16[3,512,128]{2,1,0:T(8,128)(2,1)}, bf16[3,512,128]{2,1,0:T(8,128)(2,1)S(1)}, u32[]{:S(2)}) copy-start(bf16[3,512,128]{2,1,0:T(8,128)(2,1)S(1)} %all_gather.25) | copy-start | bytes 1179652
  105.4 4.3 copy-start.20
  105.4 4.3 copy-start.46
  152.2 4.6 copy-start.6
  152.2 4.5 copy-start.7
  152.2 4.5 copy-start.10
  156.8 143.2 %copy-start.2 = (bf16[1,1024,512]{2,1,0:T(8,128)(2,1)S(1)}, bf16[1,1024,512]{2,1,0:T(8,128)(2,1)}, u32[]{:S(2)}) copy-start(bf16[1,1024,512]{2,1,0:T(8,128)(2,1)} %param.21) | copy-start | bytes 3145732
  156.8 145.5 %copy-start.31 = (f32[512]{0:T(512)S(1)}, f32[512]{0:T(512)}, u32[]{:S(2)}) copy-start(f32[512]{0:T(512)} %param.33) | copy-start | bytes 6148
  156.8 145.5 %copy-start.43 = (f32[512]{0:T(512)S(1)}, f32[512]{0:T(512)}, u32[]{:S(2)}) copy-start(f32[512]{0:T(512)} %param.34) | copy-start | bytes 6148
  156.8 228.6 %all-gather.7.cloned.1.call-start = ((), (), s32[]{:S(2)}) async-start(), calls=%async_computation.8 | async-start | bytes 5242880 | tf_op jit(solution)/shard_map/all_gather | solution.py:171
  301.9 2.5 copy-start.16
  301.9 2.5 copy-start.17
  303.7 162.5 %all-gather.9.cloned.1.call-start = ((), (), s32[]{:S(2)}) async-start(), calls=%async_computation.10 | async-start | bytes 5242880 | tf_op jit(solution)/shard_map/all_gather | solution.py:188
  304.3 254.1 %reduce-scatter.9.cloned.1.call-start = ((), (), s32[]{:S(2)}) async-start(), calls=%async_computation.11 | async-start | bytes 5242880 | tf_op jit(solution)/shard_map/reduce_scatter | solution.py:200
  476.5 2.0 copy-start.47
  483.0 155.0 %reduce-scatter.7.cloned.1.call-start = ((), (), s32[]{:S(2)}) async-start(), calls=%async_computation.9 | async-start | bytes 5242880 | tf_op jit(solution)/shard_map/reduce_scatter | solution.py:178
  491.8 146.2 %copy-start.44 = (f32[512]{0:T(512)S(1)}, f32[512]{0:T(512)}, u32[]{:S(2)}) copy-start(f32[512]{0:T(512)} %param.36) | copy-start | bytes 6148
  491.9 233.5 %all-gather.11.cloned.1.call-start = ((), (), s32[]{:S(2)}) async-start(), calls=%async_computation.12 | async-start | bytes 5242880 | tf_op jit(solution)/shard_map/all_gather | solution.py:212
  561.2 81.3 %copy-start.8 = (bf16[1,1024,512]{2,1,0:T(8,128)(2,1)S(1)}, bf16[1,1024,512]{2,1,0:T(8,128)(2,1)}, u32[]{:S(2)}) copy-start(bf16[1,1024,512]{2,1,0:T(8,128)(2,1)} %param.37) | copy-start | bytes 3145732
  641.2 1.3 copy-start.5
  641.2 87.6 %copy-start.24 = (f32[1024]{0:T(1024)}, f32[1024]{0:T(1024)S(1)}, u32[]{:S(2)}) copy-start(f32[1024]{0:T(1024)S(1)} %negate_multiply_fusion.1) | copy-start | bytes 12292
  643.9 239.2 %reduce-scatter.11.cloned.1.call-start = ((), (), s32[]{:S(2)}) async-start(), calls=%async_computation.13 | async-start | bytes 5242880 | tf_op jit(solution)/shard_map/reduce_scatter | solution.py:225
  728.8 72.6 %copy-start.13 = (bf16[3,512,128]{2,1,0:T(8,128)(2,1)S(1)}, bf16[3,512,128]{2,1,0:T(8,128)(2,1)}, u32[]{:S(2)}) copy-start(bf16[3,512,128]{2,1,0:T(8,128)(2,1)} %copy-done.12) | copy-start | bytes 1179652
  801.4 6.3 copy-start.34
  801.4 6.3 copy-start.36
  808.7 0.6 copy-start.28
  809.3 6.5 copy-start.45
  815.8 7.2 copy-start.4
  815.8 7.2 copy-start.11
  825.3 57.9 %copy-start.3 = (bf16[1,1024,512]{2,1,0:T(8,128)(2,1)S(1)}, bf16[1,1024,512]{2,1,0:T(8,128)(2,1)}, u32[]{:S(2)}) copy-start(bf16[1,1024,512]{2,1,0:T(8,128)(2,1)} %param.21) | copy-start | bytes 3145732
  825.3 57.9 %copy-start.15 = (f32[1024]{0:T(1024)S(1)}, f32[1024]{0:T(1024)}, u32[]{:S(2)}) copy-start(f32[1024]{0:T(1024)} %copy-done.14) | copy-start | bytes 12292
  825.3 57.9 %copy-start.19 = (f32[512]{0:T(512)S(1)}, f32[512]{0:T(512)}, u32[]{:S(2)}) copy-start(f32[512]{0:T(512)} %copy-done.18) | copy-start | bytes 6148
  825.3 57.9 %copy-start.30 = (f32[512]{0:T(512)S(1)}, f32[512]{0:T(512)}, u32[]{:S(2)}) copy-start(f32[512]{0:T(512)} %param.31) | copy-start | bytes 6148
  830.4 55.4 %copy-start.26 = (f32[1024]{0:T(1024)S(1)}, f32[1024]{0:T(1024)}, u32[]{:S(2)}) copy-start(f32[1024]{0:T(1024)} %copy-done.25) | copy-start | bytes 12292
  830.4 55.4 %copy-start.23 = (f32[1024]{0:T(1024)S(1)}, f32[1024]{0:T(1024)}, u32[]{:S(2)}) copy-start(f32[1024]{0:T(1024)} %copy-done.22) | copy-start | bytes 12292
  830.7 62.7 %copy-start.9 = (bf16[1,1024,512]{2,1,0:T(8,128)(2,1)S(1)}, bf16[1,1024,512]{2,1,0:T(8,128)(2,1)}, u32[]{:S(2)}) copy-start(bf16[1,1024,512]{2,1,0:T(8,128)(2,1)} %param.37) | copy-start | bytes 3145732
  831.4 57.5 %all-to-all-start = ((bf16[8,3,64,128]{3,2,1,0:T(8,128)(2,1)}), bf16[8,3,64,128]{3,2,1,0:T(8,128)(2,1)S(1)}, u32[]{:S(2)}, u32[]{:S(2)}) async-start(bf16[8,3,64,128]{3,2,1,0:T(8,128)(2,1)} %copy.79), calls=%async_computation.4 | async-start | bytes 786432 | tf_op jit(solution)/shard_map/all_to_all | solution.py:24
  889.0 21.2 %all-to-all-start.1 = ((bf16[8,64,1152]{2,1,0:T(8,128)(2,1)}), bf16[8,64,1152]{2,1,0:T(8,128)(2,1)}, u32[]{:S(2)}, u32[]{:S(2)}) async-start(bf16[8,64,1152]{2,1,0:T(8,128)(2,1)} %bitcast.206), calls=%async_computation.5 | async-start | bytes 2359296 | tf_op jit(solution)/shard_map/all_to_all | solution.py:24
  893.2 138.4 %all-reduce.3.cloned.1.call-start = ((), (), s32[]{:S(2)}) async-start(), calls=%async_computation.14 | async-start | bytes 2097152 | tf_op jit(solution)/shard_map/psum | solution.py:255
  893.3 5.0 copy-start.39
  893.3 140.6 %copy-start.1 = (f32[512,512]{1,0:T(8,128)S(1)}, f32[512,512]{1,0:T(8,128)}, u32[]{:S(2)}) copy-start(f32[512,512]{1,0:T(8,128)} %param.29) | copy-start | bytes 3145732
  897.7 0.6 copy-start.32
  897.7 15.3 %copy-start.29 = (f32[2048]{0:T(1024)S(1)}, f32[2048]{0:T(1024)}, u32[]{:S(2)}) copy-start(f32[2048]{0:T(1024)} %copy-done.28) | copy-start | bytes 24580
  897.7 15.3 %copy-start.37 = (f32[512]{0:T(512)S(1)}, f32[512]{0:T(512)}, u32[]{:S(2)}) copy-start(f32[512]{0:T(512)} %get-tuple-element.163) | copy-start | bytes 6148
  897.7 15.3 %copy-start.38 = (f32[512]{0:T(512)S(1)}, f32[512]{0:T(512)}, u32[]{:S(2)}) copy-start(f32[512]{0:T(512)} %get-tuple-element.160) | copy-start | bytes 6148
  897.7 15.3 %copy-start.40 = (f32[512]{0:T(512)S(1)}, f32[512]{0:T(512)}, u32[]{:S(2)}) copy-start(f32[512]{0:T(512)} %get-tuple-element.158) | copy-start | bytes 6148
  897.7 15.3 %copy-start.41 = (f32[512]{0:T(512)S(1)}, f32[512]{0:T(512)}, u32[]{:S(2)}) copy-start(f32[512]{0:T(512)} %get-tuple-element.162) | copy-start | bytes 6148
  897.7 15.3 %copy-start.42 = (f32[512]{0:T(512)S(1)}, f32[512]{0:T(512)}, u32[]{:S(2)}) copy-start(f32[512]{0:T(512)} %get-tuple-element.224) | copy-start | bytes 6148
Sparse Core Ops, SparseCore 0:
  15.9 83.4 all-gather.4
  156.9 142.9 reduce-scatter.4
  303.9 81.5 all-gather.6
  386.9 79.2 all-gather.8
  483.1 75.2 reduce-scatter.8
  560.7 77.2 reduce-scatter.6
  644.0 81.2 all-gather.10
  807.8 75.2 reduce-scatter.10
  900.7 130.9 all-reduce.2
where the time goes:
time: 1040 us
  waiting for transfers between devices  700 us (67%)
  matrix products  127 us (12%)
  blocking collectives  81.5 us (8%)
  other arithmetic  71.6 us (7%)
  local copies, waits for them, and re-layouts  35.8 us (3%)
  between operations  15.5 us (1%)
    reduce_scatter x1, waiting for transfers between devices, shards(): lax.psum_scatter(jnp.einsum('nse,de->nsd', part_rows, out_copy, preferred...  143 us
    all_gather x1, waiting for transfers between devices, shards(): grad_attn_all = lax.all_gather(grad_attn, 'tensor', axis=0, tiled=True)  81.2 us
    psum x1, waiting for transfers between devices, shards(): lax.psum((grad_time_w, grad_time_bias, grad_gain_one, grad_bias_one, grad...  77.5 us
    reduce_scatter x1, waiting for transfers between devices, shards(): lax.psum_scatter(jnp.einsum('nsf,df->nsd', part_rows, down_copy, preferre...  76.8 us
    all_gather x1, waiting for transfers between devices, shards(): grad_out_all = lax.all_gather(cotangent, 'tensor', axis=0, tiled=True)  72.8 us
    reduce_scatter x1, waiting for transfers between devices, shards(): lax.psum_scatter(jnp.einsum('nsf,df->nsd', part_rows, up_copy, preferred_...  66.5 us
    all_gather x1, waiting for transfers between devices, shards(): normed_all = lax.all_gather(normed_one, 'tensor', axis=0, tiled=True)  63.1 us
    all_gather x1, waiting for transfers between devices, shards(): second_all = lax.all_gather(normed_two, 'tensor', axis=0, tiled=True)  60.2 us
  transfers between devices with their start and end apart: 11, of which 10 were waited for; matrix products, arithmetic and copies ran while one was open for 6% of the time, Pallas kernels for 0%

commit v1 on v0

--- a/solution.py
+++ b/solution.py
@@ -137,149 +137,96 @@
     b_down,
     cotangent,
 ):
-    tensor_place = lax.axis_index("tensor")
+    def whole(w, dim):
+        w = lax.all_gather(w.astype(jnp.bfloat16), "tensor", axis=dim + 1, tiled=True)
+        return lax.all_gather(w, "dp", axis=dim, tiled=True)
+
+    def part(g, dim):
+        g = lax.psum_scatter(g.astype(jnp.bfloat16), "dp", scatter_dimension=dim, tiled=True)
+        return lax.psum_scatter(g, "tensor", scatter_dimension=dim + 1, tiled=True).astype(jnp.float32)
+
     qkv_copy, out_copy, up_copy, down_copy = (
-        lax.all_gather(w_qkv.astype(jnp.bfloat16), "dp", axis=1, tiled=True),
-        lax.all_gather(w_out_t.astype(jnp.bfloat16), "dp", axis=0, tiled=True),
-        lax.all_gather(w_up.astype(jnp.bfloat16), "dp", axis=0, tiled=True),
-        lax.all_gather(w_down_t.astype(jnp.bfloat16), "dp", axis=0, tiled=True),
-    )
-    bias_up_cols = lax.dynamic_slice_in_dim(
-        b_up, tensor_place * up_copy.shape[1], up_copy.shape[1], 0
-    )
-    ff_cols = up_copy.shape[1]
+        whole(w_qkv, 1), whole(w_out_t, 0), whole(w_up, 0), whole(w_down_t, 0),
+    )
+    row = lax.axis_index("tensor")
+    rows = tokens.shape[0]
+    own_ids = lax.dynamic_slice_in_dim(segment_ids, row * rows, rows, 0)
+    own_len = lax.dynamic_slice_in_dim(span_lengths, row * rows, rows, 0)
     time_emb = time_features(timestep, tokens.shape[2])
     time_proj = jnp.dot(time_emb, w_time, precision=highest) + b_time
     start = tokens.astype(jnp.float32) + time_proj[:, None, :]
     normed_one = norm_layer(start, ln1_gain, ln1_bias).astype(jnp.bfloat16)
-    normed_all = lax.all_gather(normed_one, "tensor", axis=0, tiled=True)
     qkv_act = jnp.einsum(
-        "nsd,cde->cnse", normed_all, qkv_copy, preferred_element_type=jnp.float32
+        "nsd,cde->cnse", normed_one, qkv_copy, preferred_element_type=jnp.float32
     ).astype(jnp.bfloat16)
     mixed, log_total = lax.map(
-        attend_forward, (qkv_act[0], qkv_act[1], qkv_act[2], segment_ids, span_lengths)
-    )
-    part_rows = mixed
-    attn_out = lax.psum_scatter(
-        jnp.einsum("nse,de->nsd", part_rows, out_copy, preferred_element_type=jnp.float32),
-        "tensor",
-        scatter_dimension=0,
-        tiled=True,
-    )
+        attend_forward, (qkv_act[0], qkv_act[1], qkv_act[2], own_ids, own_len)
+    )
+    attn_out = jnp.einsum("nse,de->nsd", mixed, out_copy, preferred_element_type=jnp.float32)
     middle = start + attn_out
     normed_two = norm_layer(middle, ln2_gain, ln2_bias).astype(jnp.bfloat16)
-    second_all = lax.all_gather(normed_two, "tensor", axis=0, tiled=True)
     upper = (
-        jnp.einsum("nsd,df->nsf", second_all, up_copy, preferred_element_type=jnp.float32)
-        + bias_up_cols
+        jnp.einsum("nsd,df->nsf", normed_two, up_copy, preferred_element_type=jnp.float32)
+        + b_up
     )
     activated = gelu_tanh(upper).astype(jnp.bfloat16)
-    part_rows = activated
-    ffn_out = lax.psum_scatter(
-        jnp.einsum("nsf,df->nsd", part_rows, down_copy, preferred_element_type=jnp.float32).astype(
-            jnp.bfloat16
-        ),
-        "tensor",
-        scatter_dimension=0,
-        tiled=True,
-    ).astype(jnp.float32)
+    ffn_out = jnp.einsum("nsf,df->nsd", activated, down_copy, preferred_element_type=jnp.float32)
     layer_out = (middle + ffn_out + b_down).astype(jnp.bfloat16)
     grad_b_down = jnp.sum(cotangent.astype(jnp.float32), axis=(0, 1))
-    grad_out_all = lax.all_gather(cotangent, "tensor", axis=0, tiled=True)
-    grad_down = jnp.einsum(
-        "nsd,nsf->df", grad_out_all, activated, preferred_element_type=jnp.float32
-    )
-    grad_act = jnp.einsum(
-        "nsd,df->nsf", grad_out_all, down_copy, preferred_element_type=jnp.float32
-    )
+    grad_down = jnp.einsum("nsd,nsf->df", cotangent, activated, preferred_element_type=jnp.float32)
+    grad_act = jnp.einsum("nsd,df->nsf", cotangent, down_copy, preferred_element_type=jnp.float32)
     gelu_value, gelu_pull = jax.vjp(gelu_tanh, upper)
     grad_upper = gelu_pull(grad_act)[0].astype(jnp.bfloat16)
-    grad_bias_cols = jnp.sum(grad_upper.astype(jnp.float32), axis=(0, 1))
-    grad_up = jnp.einsum("nsd,nsf->df", second_all, grad_upper, preferred_element_type=jnp.float32)
-    part_rows = grad_upper
-    grad_normed_two = lax.psum_scatter(
-        jnp.einsum("nsf,df->nsd", part_rows, up_copy, preferred_element_type=jnp.float32).astype(
-            jnp.bfloat16
-        ),
-        "tensor",
-        scatter_dimension=0,
-        tiled=True,
-    ).astype(jnp.float32)
+    grad_bias_up = jnp.sum(grad_upper.astype(jnp.float32), axis=(0, 1))
+    grad_up = jnp.einsum("nsd,nsf->df", normed_two, grad_upper, preferred_element_type=jnp.float32)
+    grad_normed_two = jnp.einsum("nsf,df->nsd", grad_upper, up_copy, preferred_element_type=jnp.float32)
     norm_two_value, norm_two_pull = jax.vjp(norm_layer, middle, ln2_gain, ln2_bias)
     grad_middle_norm, grad_gain_two, grad_bias_two = norm_two_pull(grad_normed_two)
     grad_middle = cotangent.astype(jnp.float32) + grad_middle_norm
     grad_attn = grad_middle.astype(jnp.bfloat16)
-    grad_attn_all = lax.all_gather(grad_attn, "tensor", axis=0, tiled=True)
-    grad_out_w = jnp.einsum("nsd,nse->de", grad_attn_all, mixed, preferred_element_type=jnp.float32)
+    grad_out_w = jnp.einsum("nsd,nse->de", grad_attn, mixed, preferred_element_type=jnp.float32)
     grad_mixed = jnp.einsum(
-        "nsd,de->nse", grad_attn_all, out_copy, preferred_element_type=jnp.float32
+        "nsd,de->nse", grad_attn, out_copy, preferred_element_type=jnp.float32
     ).astype(jnp.bfloat16)
     grad_qkv_act = lax.map(
         attend_backward,
-        (qkv_act[0], qkv_act[1], qkv_act[2], grad_mixed, log_total, segment_ids, span_lengths),
+        (qkv_act[0], qkv_act[1], qkv_act[2], grad_mixed, log_total, own_ids, own_len),
     )
     grad_qkv_w = jnp.einsum(
-        "nsd,ncse->cde", normed_all, grad_qkv_act, preferred_element_type=jnp.float32
-    )
-    part_rows = grad_qkv_act
-    grad_normed_one = lax.psum_scatter(
-        jnp.einsum("ncse,cde->nsd", part_rows, qkv_copy, preferred_element_type=jnp.float32).astype(
-            jnp.bfloat16
-        ),
-        "tensor",
-        scatter_dimension=0,
-        tiled=True,
-    ).astype(jnp.float32)
+        "nsd,ncse->cde", normed_one, grad_qkv_act, preferred_element_type=jnp.float32
+    )
+    grad_normed_one = jnp.einsum(
+        "ncse,cde->nsd", grad_qkv_act, qkv_copy, preferred_element_type=jnp.float32
+    )
     norm_one_value, norm_one_pull = jax.vjp(norm_layer, start, ln1_gain, ln1_bias)
     grad_start_norm, grad_gain_one, grad_bias_one = norm_one_pull(grad_normed_one)
     grad_tokens = grad_middle + grad_start_norm
     grad_time_rows = jnp.sum(grad_tokens, axis=1)
-    grad_time_w = jnp.dot(time_emb.T, grad_time_rows, precision=highest)
-    grad_time_bias = jnp.sum(grad_time_rows, axis=0)
-    grad_bias_up = lax.dynamic_update_slice_in_dim(
-        jnp.zeros((FF,), jnp.float32), grad_bias_cols, tensor_place * ff_cols, 0
-    )
-    shard_qkv, shard_out, shard_up, shard_down = (
-        sent_and_summed(grad_qkv_w.astype(jnp.bfloat16), "dp", 1),
-        *side_by_side(
-            (
-                grad_out_w.astype(jnp.bfloat16),
-                grad_up.astype(jnp.bfloat16),
-                grad_down.astype(jnp.bfloat16),
-            ),
-            "dp",
-            0,
-            1,
-        ),
-    )
-    summed = lax.psum(
-        (
-            grad_time_w,
-            grad_time_bias,
-            grad_gain_one,
-            grad_bias_one,
-            grad_gain_two,
-            grad_bias_two,
-            grad_bias_up,
-            grad_b_down,
-        ),
-        ("dp", "tensor"),
-    )
+    lines = jnp.concatenate([time_emb, grad_time_rows], axis=1)
+    lines = lax.all_gather(lines, ("dp", "tensor"), axis=0, tiled=True)
+    all_emb, all_grad = lines[:, : time_emb.shape[1]], lines[:, time_emb.shape[1] :]
+    grad_time_w = jnp.dot(all_emb.T, all_grad, precision=highest)
+    grad_time_bias = jnp.sum(all_grad, axis=0)
+    small = jnp.concatenate(
+        [grad_gain_one, grad_bias_one, grad_gain_two, grad_bias_two, grad_b_down, grad_bias_up]
+    )
+    small = lax.psum(small, ("dp", "tensor"))
+    cuts = jnp.split(small, [tokens.shape[2] * k for k in range(1, 6)])
     return (
         layer_out,
         grad_tokens,
-        shard_qkv,
-        shard_out,
-        shard_up,
-        shard_down,
-        summed[0],
-        summed[1],
-        summed[2],
-        summed[3],
-        summed[4],
-        summed[5],
-        summed[6],
-        summed[7],
+        part(grad_qkv_w, 1),
+        part(grad_out_w, 0),
+        part(grad_up, 0),
+        part(grad_down, 0),
+        grad_time_w,
+        grad_time_bias,
+        cuts[0],
+        cuts[1],
+        cuts[2],
+        cuts[3],
+        cuts[5],
+        cuts[4],
     )
 
 

time: 1040 us -> 528 us (0.51); the launches traced: 1040 us -> 518 us
  waiting for transfers between devices: 700 us -> 38.4 us
  blocking collectives: 81.5 us -> 173 us
  local copies, waits for them, and re-layouts: 35.8 us -> 77.5 us
  matrix products: 127 us -> 150 us
    reduce_scatter x4, waiting for transfers between devices: 334 us -> 13.7 us  [the longest x2 13.7 us: part(): lax.psum_scatter(g, 'tensor', scatter_dimension=dim + 1, tiled=True)]
    all_gather x4 -> x3, waiting for transfers between devices: 277 us -> 0.02 us  [whole(): return lax.all_gather(w, 'dp', axis=dim, tiled=True)]
    all_gather x4 -> x6, blocking collectives: 40.4 us -> 136 us  [the longest x1 67.5 us: shards(): lines = lax.all_gather(lines, ('dp', 'tensor'), axis=0, tiled=True)]
    psum x1 -> x0, waiting for transfers between devices: 77.5 us -> none  [shards(): lax.psum((grad_time_w, grad_time_bias, grad_gain_one, grad_bias_one, grad...]
    unnamed x97 -> x134, local copies, waits for them, and re-layouts: 7.23 us -> 59.4 us
    unnamed x9 -> x15, waiting for transfers between devices: 0.65 us -> 24.6 us
    convert_element_type x4 -> x1, other arithmetic: 10.8 us -> 28.7 us  [attend_backward(): grad_scores = (attn_probs * (grad_probs - row_delta)).astype(jnp.bfloat16)]
    dynamic_slice x41 -> x2, local copies, waits for them, and re-layouts: 18.5 us -> 1.32 us  [the longest x1 0.73 us: shards(): own_ids = lax.dynamic_slice_in_dim(segment_ids, row * rows, rows, 0)]
  transfers between devices with their start and end apart: 11 -> 11, of which waited for: 10 -> 2; matrix products, arithmetic and copies ran while one was open for 6% -> 42% of each run, Pallas kernels for 0% -> 0%
where the time goes in v1:
time: 528 us; the launch traced here: 518 us
  blocking collectives  173 us (33%)
  matrix products  150 us (28%)
  local copies, waits for them, and re-layouts  77.5 us (15%)
  other arithmetic  61.4 us (12%)
  waiting for transfers between devices  38.4 us (7%)
  between operations  16.4 us (3%)
    all_gather x1, blocking collectives, shards(): lines = lax.all_gather(lines, ('dp', 'tensor'), axis=0, tiled=True)  67.5 us
    unnamed x134, local copies, waits for them, and re-layouts  59.4 us
    all_gather x4, blocking collectives, whole(): lax.all_gather(w.astype(jnp.bfloat16), 'tensor', axis=dim + 1, tiled=True)  56.8 us
    psum x1, blocking collectives, shards(): small = lax.psum(small, ('dp', 'tensor'))  37.5 us
    convert_element_type x1, other arithmetic, attend_backward(): grad_scores = (attn_probs * (grad_probs - row_delta)).astype(jnp.bfloat16)  28.7 us
    unnamed x15, waiting for transfers between devices  24.6 us
    dot_general x1, matrix products, attend_backward(): jnp.einsum('qhe,khe->hqk', grad_heads, value_heads, preferred_element_typ...  22 us
    dot_general x1, matrix products, attend_backward(): jnp.einsum('hqk,qhe->khe', probs_low, grad_heads, preferred_element_type=...  14.4 us
  transfers between devices with their start and end apart: 11, of which 2 were waited for; matrix products, arithmetic and copies ran while one was open for 42% of the time, Pallas kernels for 0%

profile of v1, /device:TPU:0, one launch (start us, length us, event | category | flops | bytes accessed | tf_op | source)
XLA Modules:
  0.0 517.9 jit_solution(3765666602704823875)
XLA Ops:
  7.3 1.0 convert_element_type.127
  8.3 14.8 %all_gather.27 = bf16[3,64,512]{2,1,0:T(8,128)(2,1)} all-gather(bf16[3,64,128]{2,1,0:T(8,128)(2,1)S(1)} %convert_element_type.127), channel_id=1, replica_groups=mesh['dp'=8,'tensor'=4] {'tensor'}, dimensions={2}, use_global_device_ids=true | all-gather | bytes 245760 | tf_op jit(solution)/shard_map/all_gather | solution.py:141
  23.2 0.9 convert_element_type.138
  24.1 15.1 %all_gather.31 = bf16[64,2048]{1,0:T(8,128)(2,1)} all-gather(bf16[64,512]{1,0:T(8,128)(2,1)S(1)} %convert_element_type.138), channel_id=1, replica_groups=mesh['dp'=8,'tensor'=4] {'tensor'}, dimensions={1}, use_global_device_ids=true | all-gather | bytes 327680 | tf_op jit(solution)/shard_map/all_gather | solution.py:141
  39.3 0.9 convert_element_type.140
  40.2 14.9 %all_gather.33 = bf16[64,2048]{1,0:T(8,128)(2,1)} all-gather(bf16[64,512]{1,0:T(8,128)(2,1)S(1)} %convert_element_type.140), channel_id=1, replica_groups=mesh['dp'=8,'tensor'=4] {'tensor'}, dimensions={1}, use_global_device_ids=true | all-gather | bytes 327680 | tf_op jit(solution)/shard_map/all_gather | solution.py:141
  57.2 0.7 constant_dynamic-slice_fusion.1
  58.0 12.0 %all_gather.29 = bf16[64,512]{1,0:T(8,128)(2,1)S(1)} all-gather(bf16[64,128]{1,0:T(8,128)(2,1)S(1)} %convert_element_type.136), channel_id=1, replica_groups=mesh['dp'=8,'tensor'=4] {'tensor'}, dimensions={1}, use_global_device_ids=true | all-gather | bytes 81920 | tf_op jit(solution)/shard_map/all_gather | solution.py:141
  69.9 11.6 %all_gather.30 = bf16[512,512]{1,0:T(8,128)(2,1)} all-gather(bf16[64,512]{1,0:T(8,128)(2,1)S(1)} %all_gather.29), channel_id=1, replica_groups=mesh['dp'=8,'tensor'=4] {'dp'}, dimensions={0}, use_global_device_ids=true | all-gather | bytes 589824 | tf_op jit(solution)/shard_map/all_gather | solution.py:142
  84.5 2.3 fusion.14
  86.8 3.5 convert_bitcast_fusion
  90.7 1.0 copy-done.15
  91.7 14.0 %fusion.59 = (f32[8,1024]{1,0:T(8,128)S(1)}, f32[8,1024,1024]{1,2,0:T(8,128)}) fusion(bf16[1024,8,64]{0,2,1:T(8,128)(2,1)S(1)} %bitcast.135, bf16[1024,8,64]{0,2,1:T(8,128)(2,1)S(1)} %bitcast.133, pred[1024,1024]{0,1:T(8,128)(4,1)S(1)} %copy-done.15), kind=kOutput, calls=%fused_computation.112 | convolution fusion | flops 1098899456 | bytes 36732928 | tf_op jit(solution)/shard_map/while/body/eval_jaxpr/qhe,khe->hqk/dot_general | solution.py:67
  105.7 13.1 %fusion = f32[8,1024]{1,0:T(8,128)S(1)} fusion(f32[8,1024,1024]{1,2,0:T(8,128)} %get-tuple-element.125, f32[8,1024]{1,0:T(8,128)S(1)} %get-tuple-element.124), kind=kLoop, calls=%fused_computation.6 | loop fusion | flops 16769024 | bytes 33619968 | tf_op jit(solution)/shard_map/while/body/eval_jaxpr/reduce_sum | solution.py:80
  118.8 14.0 %fusion.29 = bf16[8,64,1024]{2,1,0:T(8,128)(2,1)S(1)} fusion(bf16[1024,8,64]{0,2,1:T(8,128)(2,1)S(1)} %bitcast.140, f32[8,1024,1024]{1,2,0:T(8,128)} %get-tuple-element.125, f32[8,1024]{1,0:T(8,128)S(1)} %fusion, f32[8,1024]{1,0:T(8,128)S(1)} %get-tuple-element.124), kind=kOutput, calls=%fused_computation.62 | convolution fusion | flops 1099431936 | bytes 35717120 | tf_op jit(solution)/shard_map/while/body/eval_jaxpr/hqk,khe->qhe/dot_general | solution.py:82
  132.9 0.8 fusion.60
  133.9 1.3 copy-done.5
  135.6 11.5 %multiply_convert_fusion.1 = (bf16[1024,2048]{1,0:T(8,128)(2,1)}, f32[1024,2048]{1,0:T(8,128)}) fusion(f32[2048]{0:T(1024)S(1)} %copy-done.46, bf16[512,2048]{1,0:T(8,128)(2,1)} %all-gather.7.cloned.1.call-done, f32[1,1024,512]{1,2,0:T(8,128)} %copy-done.5, f32[512]{0:T(512)S(1)} %copy-done.49, f32[512]{0:T(512)S(1)} %copy-done.43, f32[1024]{0:T(1024)S(1)} %fusion.40, ...), kind=kOutput, calls=%fused_computation.21 | convolution fusion | flops 2171076608 | bytes 16797696 | tf_op jit(solution)/shard_map/nsd,df->nsf/dot_general | solution.py:169
  147.1 10.2 %convert_reduce_fusion = (f32[2048]{0:T(1024)S(1)}, bf16[1024,2048]{1,0:T(8,128)(2,1)S(1)}) fusion(f32[1024,2048]{1,0:T(8,128)} %get-tuple-element.129, f32[2048]{0:T(1024)S(1)} %copy-done.46, bf16[512,2048]{1,0:T(8,128)(2,1)} %all-gather.9.cloned.1.call-done, bf16[1,1024,512]{2,1,0:T(8,128)(2,1)S(1)} %copy-done.24), kind=kOutput, calls=%fused_computation.20 | convolution fusion | flops 2195716096 | bytes 15745024 | tf_op jit(solution)/shard_map/nsd,df->nsf/dot_general | solution.py:177
  157.3 3.7 fusion.62
  161.0 3.0 copy.79
  164.0 3.0 fusion.16
  168.5 0.9 copy-done.3
  169.4 0.7 copy-done.53
  170.0 1.6 convolution_convert_fusion.4
  171.6 2.0 convolution_convert_fusion.3
  173.6 14.4 %fusion.25 = bf16[8,64,1024]{2,1,0:T(8,128)(2,1)} fusion(bf16[1024,8,64]{0,2,1:T(8,128)(2,1)S(1)} %bitcast.138, f32[8,1024,1024]{1,2,0:T(8,128)} %get-tuple-element.125, f32[8,1024]{1,0:T(8,128)S(1)} %log_add_fusion), kind=kOutput, calls=%fused_computation.59 | convolution fusion | flops 1091043328 | bytes 35684352 | tf_op jit(solution)/shard_map/while/body/eval_jaxpr/hqk,qhe->khe/dot_general | solution.py:94
  188.0 22.0 %multiply_reduce_fusion = (f32[8,1024]{1,0:T(8,128)S(1)}, f32[8,1024,1024]{1,2,0:T(8,128)}) fusion(f32[8,1024,1024]{1,2,0:T(8,128)} %get-tuple-element.125, f32[8,1024]{1,0:T(8,128)S(1)} %log_add_fusion, bf16[1024,8,64]{0,2,1:T(8,128)(2,1)S(1)} %bitcast.139, bf16[1024,8,64]{0,2,1:T(8,128)(2,1)S(1)} %bitcast.141), kind=kOutput, calls=%fused_computation.1 | convolution fusion | flops 1098899456 | bytes 69271552 | tf_op jit(solution)/shard_map/while/body/eval_jaxpr/qhe,khe->hqk/dot_general | solution.py:97
  210.1 28.7 %multiply_convert_fusion = bf16[8,1024,1024]{1,2,0:T(8,128)(2,1)} fusion(f32[8,1024,1024]{1,2,0:T(8,128)} %get-tuple-element.131, f32[8,1024,1024]{1,2,0:T(8,128)} %get-tuple-element.125, f32[8,1024]{1,0:T(8,128)S(1)} %get-tuple-element.130, f32[8,1024]{1,0:T(8,128)S(1)} %log_add_fusion), kind=kLoop, calls=%fused_computation | loop fusion | flops 33554432 | bytes 83951616 | tf_op jit(solution)/shard_map/while/body/eval_jaxpr/convert_element_type | solution.py:101
  238.9 12.1 %multiply_convert_fusion.2 = bf16[8,64,1024]{2,1,0:T(8,128)(2,1)} fusion(bf16[1024,8,64]{0,2,1:T(8,128)(2,1)S(1)} %bitcast.136, bf16[8,1024,1024]{1,2,0:T(8,128)(2,1)} %multiply_convert_fusion), kind=kOutput, calls=%fused_computation.47 | convolution fusion | flops 1074790400 | bytes 18874368 | tf_op jit(solution)/shard_map/while/body/eval_jaxpr/hqk,qhe->khe/dot_general | solution.py:108
  250.9 9.9 %multiply_convert_fusion.3 = bf16[8,64,1024]{2,1,0:T(8,128)(2,1)} fusion(bf16[1024,8,64]{0,2,1:T(8,128)(2,1)S(1)} %bitcast.134, bf16[8,1024,1024]{1,2,0:T(8,128)(2,1)} %multiply_convert_fusion), kind=kOutput, calls=%fused_computation.48 | convolution fusion | flops 1074790400 | bytes 18874368 | tf_op jit(solution)/shard_map/while/body/eval_jaxpr/hqk,khe->qhe/dot_general | solution.py:104
  260.8 1.3 copy.85
  262.1 2.4 copy.83
  264.5 1.3 copy.84
  265.9 4.8 fusion.28
  270.7 4.4 copy.89
  275.2 6.7 %convolution_convert_fusion.1 = bf16[512,2048]{1,0:T(8,128)(2,1)} fusion(bf16[1024,2048]{1,0:T(8,128)(2,1)} %copy-done.55, f32[1,1024,512]{1,2,0:T(8,128)} %copy-done.5, f32[512]{0:T(512)S(1)} %copy-done.49, f32[512]{0:T(512)S(1)} %copy-done.43, f32[1024]{0:T(1024)S(1)} %fusion.40, f32[1024]{0:T(1024)S(1)} %broadcast_multiply_fusion), kind=kOutput, calls=%fused_computation.30 | convolution fusion | flops 2151153664 | bytes 8400896 | tf_op jit(solution)/shard_map/nsd,nsf->df/dot_general | solution.py:181
  282.1 0.9 copy-done.25
  283.1 6.0 %fusion.15 = bf16[512,2048]{0,1:T(8,128)(2,1)} fusion(bf16[1024,2048]{1,0:T(8,128)(2,1)} %get-tuple-element.128, bf16[1,1024,512]{2,1,0:T(8,128)(2,1)S(1)} %copy-done.25), kind=kOutput, calls=%fused_computation.31 | convolution fusion | flops 2148532224 | bytes 7340032 | tf_op jit(solution)/shard_map/nsd,nsf->df/dot_general | solution.py:176
  289.1 4.0 copy.110
  295.0 4.9 fusion.61
  299.9 2.9 copy.86
  302.8 2.3 fusion.18
  305.1 1.0 fusion.17
  306.9 2.6 fusion.55
  309.6 1.6 copy.108
  311.3 24.4 %all-reduce.3.cloned.1.call-done = bf16[3,512,512]{2,0,1:T(4,128)(2,1)} async-done(((bf16[3,512,512]{2,0,1:T(4,128)(2,1)}), bf16[3,512,512]{2,0,1:T(4,128)(2,1)}) %all-reduce.3.cloned.1.call-update) | async-done | bytes 1572880
  335.7 1.0 constant_dynamic-slice_fusion
  336.7 14.0 %copy.106 = bf16[3,64,512]{0,1,2:T(8,128)(2,1)} copy(bf16[3,64,512]{2,0,1:T(4,128)(2,1)S(1)} %constant_dynamic-slice_fusion) | data formatting | bytes 393216
  350.7 13.9 %reshape.435 = bf16[512,192]{1,0:T(8,128)(2,1)} reshape(bf16[512,64,3]{2,1,0:T(8,128)(2,1)} %bitcast.132) | data formatting | bytes 393216
  364.6 67.5 %all-gather = f32[32,1,1024]{2,1,0:T(1,128)S(1)} all-gather(f32[1,1,1024]{2,1,0:T(1,128)S(1)} %maximum_bitcast_fusion), channel_id=1, replica_groups=mesh['dp'=8,'tensor'=4] {'dp','tensor'}, dimensions={0}, use_global_device_ids=true | all-gather | bytes 135168 | tf_op jit(solution)/shard_map/all_gather | solution.py:206
  433.2 5.2 %fusion.21 = bf16[1,1024,512]{1,2,0:T(8,128)(2,1)S(1)} fusion(f32[1,1024,512]{1,2,0:T(8,128)S(1)} %copy-done.7, bf16[1024,2048]{1,0:T(8,128)(2,1)} %get-tuple-element.128, bf16[512,2048]{1,0:T(8,128)(2,1)} %all-gather.9.cloned.1.call-done, f32[512]{0:T(512)S(1)} %copy-done.50), kind=kOutput, calls=%fused_computation.44 | convolution fusion | flops 2149056512 | bytes 9439232 | tf_op jit(solution)/shard_map/nsf,df->nsd/dot_general | solution.py:173
  438.5 2.1 copy.111
  440.6 1.3 copy.92
  441.9 37.5 %psum.7 = f32[4608]{0:T(1024)S(1)} all-reduce(f32[4608]{0:T(1024)S(1)} %constant_dynamic-update-slice_fusion), channel_id=1, replica_groups=mesh['dp'=8,'tensor'=4] {'dp','tensor'}, use_global_device_ids=true, to_apply=%region_27.28 | all-reduce | flops 4608 | bytes 36864 | tf_op jit(solution)/shard_map/psum | solution.py:213
  480.0 1.8 copy.93
  482.4 2.0 fusion.36
  484.4 0.8 copy.109
  485.9 5.3 %reshape.436 = bf16[128,64,3]{2,1,0:T(8,128)(2,1)S(1)} reshape(bf16[128,192]{1,0:T(8,128)(2,1)} %reduce-scatter.22.cloned.1.call-done) | data formatting | bytes 98304
  491.2 2.2 copy.107
  493.4 0.7 copy.94
  494.1 1.5 convert_element_type.154
  495.6 13.7 %reduce-scatter.20.cloned.1.call-done = bf16[64,512]{0,1:T(8,128)(2,1)} async-done(((bf16[64,2048]{0,1:T(8,128)(2,1)}), bf16[64,512]{0,1:T(8,128)(2,1)}) %reduce-scatter.20.cloned.1.call-update) | async-done | bytes 65552 | tf_op jit(solution)/shard_map/reduce_scatter | solution.py:146
  509.3 1.6 copy.95
  (175 shorter events, 12.1 us)
Async XLA Ops:
  7.2 74.9 %copy-start = (f32[512,512]{1,0:T(8,128)S(1)}, f32[512,512]{1,0:T(8,128)}, u32[]{:S(2)}) copy-start(f32[512,512]{1,0:T(8,128)} %param.25) | copy-start | bytes 3145732
  7.2 48.7 %copy-start.51 = (s32[4]{0:T(128)S(1)}, s32[4]{0:T(128)}, u32[]{:S(2)}) copy-start(s32[4]{0:T(128)} %param.20) | copy-start | bytes 52
  7.2 50.7 %copy-start.36 = (f32[64,128]{1,0:T(8,128)S(1)}, f32[64,128]{1,0:T(8,128)}, u32[]{:S(2)}) copy-start(f32[64,128]{1,0:T(8,128)} %param.22) | copy-start | bytes 98308
  7.2 74.4 %copy-start.22 = (bf16[1,1024,512]{2,1,0:T(8,128)(2,1)S(1)}, bf16[1,1024,512]{2,1,0:T(8,128)(2,1)}, u32[]{:S(2)}) copy-start(bf16[1,1024,512]{2,1,0:T(8,128)(2,1)} %param.17) | copy-start | bytes 3145732
  7.2 79.6 %all-gather.5.cloned.1.call-start = ((), (), s32[]{:S(2)}) async-start(), calls=%async_computation.7 | async-start | bytes 1769472 | tf_op jit(solution)/shard_map/all_gather | solution.py:142
  23.1 112.4 %all-gather.7.cloned.1.call-start = ((), (), s32[]{:S(2)}) async-start(), calls=%async_computation.8 | async-start | bytes 2359296 | tf_op jit(solution)/shard_map/all_gather | solution.py:142
  39.2 107.9 %all-gather.9.cloned.1.call-start = ((), (), s32[]{:S(2)}) async-start(), calls=%async_computation.9 | async-start | bytes 2359296 | tf_op jit(solution)/shard_map/all_gather | solution.py:142
  55.1 27.6 %copy-start.44 = (f32[512]{0:T(512)S(1)}, f32[512]{0:T(512)}, u32[]{:S(2)}) copy-start(f32[512]{0:T(512)} %param.26) | copy-start | bytes 6148
  55.2 254.4 %reduce-scatter.14.cloned.1.call-start = ((), (), s32[]{:S(2)}) async-start(), calls=%async_computation.10 | async-start | bytes 589824 | tf_op jit(solution)/shard_map/reduce_scatter | solution.py:145
  57.2 25.6 %copy-start.41 = (f32[1,256]{1,0:T(1,128)}, f32[1,256]{1,0:T(1,128)S(1)}, u32[]{:S(2)}) copy-start(f32[1,256]{1,0:T(1,128)S(1)} %get-tuple-element.139) | copy-start | bytes 3076
  57.2 25.6 %copy-start.39 = (f32[1,256]{1,0:T(1,128)}, f32[1,256]{1,0:T(1,128)S(1)}, u32[]{:S(2)}) copy-start(f32[1,256]{1,0:T(1,128)S(1)} %get-tuple-element.138) | copy-start | bytes 3076
  82.7 1.2 copy-start.23
  83.1 3.7 copy-start.30
  83.1 3.7 copy-start.37
  83.1 3.7 copy-start.47
  83.5 6.8 %copy-start.34 = (f32[1024]{0:T(1024)}, f32[1024]{0:T(1024)S(1)}, u32[]{:S(2)}) copy-start(f32[1024]{0:T(1024)S(1)} %multiply_reduce_fusion.2) | copy-start | bytes 12292
  84.0 6.3 %copy-start.32 = (f32[1024]{0:T(1024)}, f32[1024]{0:T(1024)S(1)}, u32[]{:S(2)}) copy-start(f32[1024]{0:T(1024)S(1)} %fusion.39) | copy-start | bytes 12292
  84.5 83.5 %copy-start.13 = (bf16[1,1024,512]{1,2,0:T(8,128)(2,1)}, bf16[1,1024,512]{1,2,0:T(8,128)(2,1)S(1)}, u32[]{:S(2)}) copy-start(bf16[1,1024,512]{1,2,0:T(8,128)(2,1)S(1)} %copy.78) | copy-start | bytes 3145732
  90.3 1.4 copy-start.15
  90.6 15.0 %copy-start.9 = (bf16[1,1,1024,512]{2,3,0,1:T(8,128)(2,1)}, bf16[1,1,1024,512]{2,3,0,1:T(8,128)(2,1)S(1)}, u32[]{:S(2)}) copy-start(bf16[1,1,1024,512]{2,3,0,1:T(8,128)(2,1)S(1)} %get-tuple-element.115) | copy-start | bytes 3145732
  90.7 15.0 %copy-start.11 = (bf16[1,1,1024,512]{2,3,0,1:T(8,128)(2,1)}, bf16[1,1,1024,512]{2,3,0,1:T(8,128)(2,1)S(1)}, u32[]{:S(2)}) copy-start(bf16[1,1,1024,512]{2,3,0,1:T(8,128)(2,1)S(1)} %get-tuple-element.116) | copy-start | bytes 3145732
  90.7 28.1 %copy-start.17 = (bf16[1,1,1024,512]{2,3,0,1:T(8,128)(2,1)}, bf16[1,1,1024,512]{2,3,0,1:T(8,128)(2,1)S(1)}, u32[]{:S(2)}) copy-start(bf16[1,1,1024,512]{2,3,0,1:T(8,128)(2,1)S(1)} %get-tuple-element.117) | copy-start | bytes 3145732
  118.8 14.1 %copy-start.28 = (bf16[512,512]{1,0:T(8,128)(2,1)S(1)}, bf16[512,512]{1,0:T(8,128)(2,1)}, u32[]{:S(2)}) copy-start(bf16[512,512]{1,0:T(8,128)(2,1)} %all_gather.30) | copy-start | bytes 1572868
  133.8 1.3 copy-start.5
  133.8 1.7 copy-start.43
  133.8 1.7 copy-start.46
  133.8 1.7 copy-start.49
  135.5 11.6 %copy-start.24 = (bf16[1,1024,512]{2,1,0:T(8,128)(2,1)S(1)}, bf16[1,1024,512]{2,1,0:T(8,128)(2,1)}, u32[]{:S(2)}) copy-start(bf16[1,1024,512]{2,1,0:T(8,128)(2,1)} %param.33) | copy-start | bytes 3145732
  147.1 10.3 %copy-start.45 = (bf16[512,2048]{1,0:T(8,128)(2,1)S(1)}, bf16[512,2048]{1,0:T(8,128)(2,1)}, u32[]{:S(2)}) copy-start(bf16[512,2048]{1,0:T(8,128)(2,1)} %all-gather.7.cloned.1.call-done) | copy-start | bytes 6291460
  157.3 3.7 copy-start.55
  164.0 3.0 copy-start.6
  164.0 3.5 copy-start.8
  168.0 1.4 copy-start.3
  168.1 2.0 copy-start.53
  170.0 1.6 copy-start.21
  170.0 1.6 copy-start.29
  173.6 14.4 %copy-start.18 = (bf16[1,1,1024,512]{2,3,0,1:T(8,128)(2,1)S(1)}, bf16[1,1,1024,512]{2,3,0,1:T(8,128)(2,1)}, u32[]{:S(2)}) copy-start(bf16[1,1,1024,512]{2,3,0,1:T(8,128)(2,1)} %copy-done.17) | copy-start | bytes 3145732
  210.1 125.6 %all-reduce.3.cloned.1.call-start = ((), (), s32[]{:S(2)}) async-start(), calls=%async_computation.17 | async-start | bytes 4194304
  210.1 28.7 %copy-start.12 = (bf16[1,1,1024,512]{2,3,0,1:T(8,128)(2,1)S(1)}, bf16[1,1,1024,512]{2,3,0,1:T(8,128)(2,1)}, u32[]{:S(2)}) copy-start(bf16[1,1,1024,512]{2,3,0,1:T(8,128)(2,1)} %copy-done.11) | copy-start | bytes 3145732
  238.9 12.1 %copy-start.10 = (bf16[1,1,1024,512]{2,3,0,1:T(8,128)(2,1)S(1)}, bf16[1,1,1024,512]{2,3,0,1:T(8,128)(2,1)}, u32[]{:S(2)}) copy-start(bf16[1,1,1024,512]{2,3,0,1:T(8,128)(2,1)} %copy-done.9) | copy-start | bytes 3145732
  250.9 9.9 %copy-start.19 = (bf16[8,64,1024]{2,1,0:T(8,128)(2,1)S(1)}, bf16[8,64,1024]{2,1,0:T(8,128)(2,1)}, u32[]{:S(2)}) copy-start(bf16[8,64,1024]{2,1,0:T(8,128)(2,1)} %fusion.25) | copy-start | bytes 3145732
  260.8 3.7 copy-start.20
  262.1 3.7 copy-start.26
  262.1 3.7 copy-start.31
  262.1 3.7 copy-start.33
  262.1 3.7 copy-start.38
  262.1 3.7 copy-start.48
  275.1 157.7 %reduce-scatter.16.cloned.1.call-start = ((), (), s32[]{:S(2)}) async-start(), calls=%async_computation.11 | async-start | bytes 2359296 | tf_op jit(solution)/shard_map/reduce_scatter | solution.py:145
  281.9 156.6 %reduce-scatter.26.cloned.1.call-start = ((), (), s32[]{:S(2)}) async-start(), calls=%async_computation.16 | async-start | bytes 2359296
  293.1 1.9 copy-start.27
  293.1 191.3 %reduce-scatter.24.cloned.1.call-start = ((), (), s32[]{:S(2)}) async-start(), calls=%async_computation.15 | async-start | bytes 163840
  302.8 2.3 copy-start.35
  302.8 2.3 copy-start.2
  305.1 1.6 copy-start.4
  305.1 1.8 copy-start.14
  306.9 2.6 copy-start.40
  306.9 2.6 copy-start.42
  311.2 174.7 %reduce-scatter.22.cloned.1.call-start = ((), (), s32[]{:S(2)}) async-start(), calls=%async_computation.14 | async-start | bytes 327680
  350.7 82.5 %copy-start.7 = (f32[1,1024,512]{1,2,0:T(8,128)S(1)}, f32[1,1024,512]{1,2,0:T(8,128)}, u32[]{:S(2)}) copy-start(f32[1,1024,512]{1,2,0:T(8,128)} %copy-done.5) | copy-start | bytes 6291460
  350.7 82.5 %copy-start.50 = (f32[512]{0:T(512)S(1)}, f32[512]{0:T(512)}, u32[]{:S(2)}) copy-start(f32[512]{0:T(512)} %param.32) | copy-start | bytes 6148
  364.6 129.5 %reduce-scatter.18.cloned.1.call-start = ((), (), s32[]{:S(2)}) async-start(), calls=%async_computation.12 | async-start | bytes 327680 | tf_op jit(solution)/shard_map/reduce_scatter | solution.py:146
  432.9 76.4 %reduce-scatter.20.cloned.1.call-start = ((), (), s32[]{:S(2)}) async-start(), calls=%async_computation.13 | async-start | bytes 655360 | tf_op jit(solution)/shard_map/reduce_scatter | solution.py:146
  438.4 41.6 %copy-start.16 = (f32[1,1024,512]{1,2,0:T(8,128)S(1)}, f32[1,1024,512]{1,2,0:T(8,128)}, u32[]{:S(2)}) copy-start(f32[1,1024,512]{1,2,0:T(8,128)} %get-tuple-element.112) | copy-start | bytes 6291460
  485.2 25.7 %copy-start.1 = (f32[512,512]{1,0:T(8,128)S(1)}, f32[512,512]{1,0:T(8,128)}, u32[]{:S(2)}) copy-start(f32[512,512]{1,0:T(8,128)} %param.25) | copy-start | bytes 3145732
  (3 other events, 2.9 us)
Sparse Core Ops, SparseCore 0:
  23.3 25.8 all-gather.4
  51.1 28.5 all-gather.6
  81.6 29.2 all-gather.8
  210.2 32.9 reduce-scatter.13
  275.3 60.3 all-reduce.2
  339.2 40.4 reduce-scatter.15
  382.9 41.2 reduce-scatter.25
  427.1 19.2 reduce-scatter.23
  448.6 18.0 reduce-scatter.21
  468.9 18.1 reduce-scatter.17
  489.4 19.8 reduce-scatter.19

commit v2 on v1

v2 whole, which is shorter than its diff:
```python
import functools
import math

import jax
import jax.numpy as jnp
from jax import lax
from jax.experimental import pallas as pl
from jax.experimental.pallas import tpu as pltpu
from jax.sharding import PartitionSpec as P_

f32, bf16 = jnp.float32, jnp.bfloat16
HS = 64
TR = 256
BIG = 1e30
EPS = 1e-5
LOG2E = math.log2(math.e)
LN2 = math.log(2.0)
SCALE = 1.0 / math.sqrt(HS)


def nt_dot(a, b):
    return lax.dot_general(a, b, (((1,), (1,)), ((), ())), preferred_element_type=f32)


def tn_dot(a, b):
    return lax.dot_general(a, b, (((0,), (0,)), ((), ())), preferred_element_type=f32)


def nn_dot(a, b):
    return jnp.dot(a, b, preferred_element_type=f32)


def lane(shape):
    return lax.broadcasted_iota(jnp.int32, shape, len(shape) - 1)


def rows_of(i, n=TR):
    return pl.ds(pl.multiple_of(i * n, n), n)


def normed(x):
    mean = jnp.mean(x, axis=-1, keepdims=True)
    c = x - mean
    var = jnp.mean(c * c, axis=-1, keepdims=True)
    r = lax.rsqrt(var + EPS)
    return c * r, r


def norm_back(xhat, r, gain, gy):
    gh = gy * gain
    a = jnp.mean(gh, axis=-1, keepdims=True)
    b = jnp.mean(gh * xhat, axis=-1, keepdims=True)
    return r * (gh - a - xhat * b)


def colsum(x):
    return jnp.sum(x, axis=0, keepdims=True)


def halves(prod):
    low = lane(prod.shape) < HS
    s0 = jnp.sum(jnp.where(low, prod, 0.0), axis=-1, keepdims=True)
    s1 = jnp.sum(jnp.where(low, 0.0, prod), axis=-1, keepdims=True)
    return s0, s1


def split3(x):
    hi = x.astype(bf16)
    rest = x - hi.astype(f32)
    mid = rest.astype(bf16)
    lo = (rest - mid.astype(f32)).astype(bf16)
    return hi, mid, lo


def window(i, seq, most):
    lo = max(0, (i * TR - most + 1) // 128 * 128)
    hi = min(seq, -(-(i * TR + TR - 1 + most) // 128) * 128)
    return lo, hi


def attend_fwd(seq, most, length, qkv, qaug, kaug, mixed, lse, qq, kk, vv, hp):
    n = seq // TR
    def prep(i, _):
        r = rows_of(i)
        low = lane((TR, 128)) < HS
        q, k, v = (qkv[hp, r, 128 * c:128 * c + 128] for c in range(3))
        qa, ka = qaug[r, :], kaug[r, :]
        one = jnp.ones_like(v)
        qq[0, r, :] = jnp.where(low, q, qa)
        qq[1, r, :] = jnp.where(low, qa, q)
        kk[0, r, :] = jnp.where(low, k, ka)
        kk[1, r, :] = jnp.where(low, ka, k)
        vv[0, r, :] = jnp.where(low, v, one)
        vv[1, r, :] = jnp.where(low, one, v)
        return 0
    lax.fori_loop(0, n, prep, 0)
    for i in range(n):
        lo, hi = window(i, seq, most)
        r = slice(i * TR, i * TR + TR)
        low = lane((TR, 128)) < HS
        q, k, v = (qkv[hp, r, 128 * c:128 * c + 128].astype(f32) for c in range(3))
        own = halves(q * k)
        pad = (lax.broadcasted_iota(jnp.int32, (TR, 1), 0) + i * TR) >= length
        tops, outs = [], []
        for h in range(2):
            s = nt_dot(qq[h, r, :], kk[h, lo:hi, :])
            m = jnp.max(s, axis=-1, keepdims=True)
            m = jnp.where(pad, jnp.maximum(m, own[h]), m)
            p = jnp.exp2(s - m).astype(bf16)
            outs.append(nn_dot(p, vv[h, lo:hi, :]))
            tops.append(m)
        padf = pad.astype(f32)
        e0 = jnp.exp2(jnp.minimum(own[0] - tops[0], 0.0)).astype(bf16).astype(f32) * padf
        e1 = jnp.exp2(jnp.minimum(own[1] - tops[1], 0.0)).astype(bf16).astype(f32) * padf
        num = jnp.where(low, outs[0], outs[1]) + jnp.where(low, e0, e1) * v
        den_x = jnp.where(low, outs[1], outs[0]) + jnp.where(low, e1, e0)
        den = pltpu.roll(den_x, HS, 1)
        mixed[hp, r, :] = (num / den).astype(bf16)
        lse[hp, r, :] = jnp.where(low, tops[1], tops[0]) + jnp.log2(den_x)


def attend_bwd(seq, most, length, qkv, qaug, kaug, mixed, lse, gm, qq, kk, vv, oo, dq, dkv, dqkv, hp):
    n = seq // TR
    def prep(i, _):
        r = rows_of(i)
        low = lane((TR, 128)) < HS
        spot = lane((TR, 128)) % HS
        q, k, v = (qkv[hp, r, 128 * c:128 * c + 128] for c in range(3))
        g = gm[hp, r, :]
        d0, d1 = halves(g.astype(f32) * mixed[hp, r, :].astype(f32))
        dx = jnp.where(low, d1, d0)
        def put(base, x):
            hi, mid, lo = split3(x)
            z = jnp.where(spot == 8, hi, base)
            z = jnp.where(spot == 9, mid, z)
            return jnp.where(spot == 10, lo, z)
        zero = jnp.zeros((TR, 128), bf16)
        qa = put(qaug[r, :], lse[hp, r, :])
        oa = put(zero, dx)
        ka = kaug[r, :]
        va = jnp.where((spot >= 8) & (spot < 11), -jnp.ones_like(zero), zero)
        for ref, x, a in ((qq, q, qa), (kk, k, ka), (vv, v, va), (oo, g, oa)):
            ref[0, r, :] = jnp.where(low, x, a)
            ref[1, r, :] = jnp.where(low, a, x)
        return 0
    lax.fori_loop(0, n, prep, 0)
    for h in range(2):
        dq[h] = jnp.zeros(dq.shape[1:], f32)
    for i in range(n):
        lo, hi = window(i, seq, most)
        r = slice(i * TR, i * TR + TR)
        for h in range(2):
            st = nt_dot(kk[h, r, :], qq[h, lo:hi, :])
            pt = jnp.exp2(st)
            dpt = nt_dot(vv[h, r, :], oo[h, lo:hi, :])
            dst = (pt * dpt).astype(bf16)
            dkv[h, 0, r, :] = nn_dot(dst, qq[h, lo:hi, :])
            dkv[h, 1, r, :] = nn_dot(pt.astype(bf16), oo[h, lo:hi, :])
            dq[h, lo:hi, :] += tn_dot(dst, kk[h, r, :])
    def post(i, _):
        r = rows_of(i)
        low = lane((TR, 128)) < HS
        q, k, v = (qkv[hp, r, 128 * c:128 * c + 128].astype(f32) for c in range(3))
        g = gm[hp, r, :].astype(f32)
        pad = (lax.broadcasted_iota(jnp.int32, (TR, 1), 0) + i * TR) >= length
        padf = pad.astype(f32)
        s0, s1 = halves(q * k)
        p0, p1 = halves(g * v)
        d0, d1 = halves(g * mixed[hp, r, :].astype(f32))
        ls = pltpu.roll(lse[hp, r, :], HS, 1)
        pf = jnp.exp2(jnp.minimum(jnp.where(low, s0, s1) - ls, 1.0)) * padf
        ds = (pf * (jnp.where(low, p0, p1) - jnp.where(low, d0, d1))).astype(bf16).astype(f32)
        pf = pf.astype(bf16).astype(f32)
        gq = jnp.where(low, dq[0, r, :], dq[1, r, :]) + ds * k
        gk = jnp.where(low, dkv[0, 0, r, :], dkv[1, 0, r, :]) + ds * q
        gv = jnp.where(low, dkv[0, 1, r, :], dkv[1, 1, r, :]) + pf * g
        dqkv[r, 0:128] = (gq * SCALE).astype(bf16)
        dqkv[r, 128:256] = (gk * LN2).astype(bf16)
        dqkv[r, 256:384] = gv.astype(bf16)
        return 0
    lax.fori_loop(0, n, post, 0)


def gelu_parts(u):
    c0, c1 = 0.7978845608028654, 0.044715
    u2 = u * u
    th = jnp.tanh(u * (c0 + (c0 * c1) * u2))
    half = 0.5 + 0.5 * th
    act = u * half
    grad = half + (0.5 * u) * (1.0 - th * th) * (c0 + (3.0 * c0 * c1) * u2)
    return act, grad


def transpose_into(dst, src, seq):
    def step(i, _):
        r = rows_of(i)
        dst[:, r] = src[r, :].T
        return 0
    for i in range(seq // TR):
        r = slice(i * TR, i * TR + TR)
        dst[:, r] = src[r, :].T


def kernel(T, most, len_ref, ts_ref, tok, cot, seg, wq, wo, wu, wd, wt, btime, g1, b1, g2, b2, bdown, bup,
           out, gtok, dwq, dwo, dwu, dwd, vec,
           tp, n1, qkv, qaug, kaug, mixed, lse, qq, kk, vv, oo, dq, dkv, dqkv, mid, n2, ffn, gn, act, gu, gm, xT, xT2):
    seq, D = tok.shape
    P = wq.shape[0]
    n = seq // TR
    length = len_ref[T()]
    t = ts_ref[0].astype(f32)
    half = D // 2
    ang = t * jnp.exp(-math.log(10000.0) * lax.broadcasted_iota(jnp.int32, (8, half), 1).astype(f32) / half)
    emb = jnp.concatenate([jnp.sin(ang), jnp.cos(ang)], axis=1)
    vec[0:1, :] = emb[0:1, :]
    proj = jnp.dot(emb, wt[...], precision=lax.Precision.HIGHEST, preferred_element_type=f32)[0:1, :] + btime[...]
    tp[...] = proj
    def ln1(i, _):
        r = rows_of(i)
        xh, _r = normed(tok[r, :].astype(f32) + tp[...])
        n1[r, :] = (xh * g1[...] + b1[...]).astype(bf16)
        return 0
    lax.fori_loop(0, n, ln1, 0)
    srow = seg[pl.ds(T(), 1), :].astype(f32)
    for b in range(seq // 128):
        col = jnp.broadcast_to(srow[:, 128 * b:128 * b + 128], (128, 128)).T
        spot = lane((128, 128)) % HS
        pos = lax.broadcasted_iota(jnp.int32, (128, 128), 0) + 128 * b
        same = col == spot.astype(f32)
        r = slice(128 * b, 128 * b + 128)
        qaug[r, :] = jnp.where(same & (spot < 8), 1.0, 0.0).astype(bf16)
        ka = jnp.where(same & (pos < length), 0.0, -BIG)
        kaug[r, :] = jnp.where(spot < 8, ka, jnp.where(spot < 11, -1.0, 0.0)).astype(bf16)
    def pair_fwd(hp, _):
        def proj(i, _):
            r = rows_of(i)
            x = nn_dot(n1[r, :], wq[hp])
            s = jnp.where(lane((1, 384)) < 128, SCALE * LOG2E, 1.0)
            qkv[hp, r, :] = (x * s).astype(bf16)
            return 0
        lax.fori_loop(0, n, proj, 0)
        attend_fwd(seq, most, length, qkv, qaug, kaug, mixed, lse, qq, kk, vv, hp)
        return 0
    lax.fori_loop(0, P, pair_fwd, 0)
    def ln2(i, _):
        r = rows_of(i)
        mx = jnp.concatenate([mixed[p, r, :] for p in range(P)], axis=1)
        w = jnp.concatenate([wo[p] for p in range(P)], axis=1)
        x = tok[r, :].astype(f32) + tp[...] + nt_dot(mx, w)
        mid[r, :] = x
        xh, _r = normed(x)
        n2[r, :] = (xh * g2[...] + b2[...]).astype(bf16)
        return 0
    lax.fori_loop(0, n, ln2, 0)
    transpose_into(xT, cot, seq)
    transpose_into(xT2, n2, seq)
    for f in range(wu.shape[0]):
        F = wu.shape[2]
        def tile(i, acc):
            r = rows_of(i)
            u = nn_dot(n2[r, :], wu[f]) + bup[:, f * F:f * F + F]
            a, ga = gelu_parts(u)
            a = a.astype(bf16)
            g = (nn_dot(cot[r, :], wd[f]) * ga).astype(bf16)
            act[r, :] = a
            gu[r, :] = g
            fo = nt_dot(a, wd[f])
            go = nt_dot(g, wu[f])
            if f == 0:
                ffn[r, :] = fo
                gn[r, :] = go
            else:
                ffn[r, :] += fo
                gn[r, :] += go
            return acc + colsum(g.astype(f32))
        acc = lax.fori_loop(0, n, tile, jnp.zeros((1, F), f32))
        vec[7 + f:8 + f, :] = acc
        def wgrad(i, _):
            r = rows_of(i)
            dwd[f, r, :] = nn_dot(xT[r, :], act[...]).astype(bf16)
            dwu[f, r, :] = nn_dot(xT2[r, :], gu[...]).astype(bf16)
            return 0
        lax.fori_loop(0, D // TR, wgrad, 0)
    def ln2b(i, acc):
        r = rows_of(i)
        c = cot[r, :].astype(f32)
        x = mid[r, :]
        out[r, :] = (x + ffn[r, :] + bdown[...]).astype(bf16)
        xh, rr = normed(x)
        gy = gn[r, :]
        gmid = c + norm_back(xh, rr, g2[...], gy)
        mid[r, :] = gmid
        n2[r, :] = gmid.astype(bf16)
        return acc[0] + colsum(gy * xh), acc[1] + colsum(gy), acc[2] + colsum(c)
    z = jnp.zeros((1, D), f32)
    a = lax.fori_loop(0, n, ln2b, (z, z, z))
    vec[4:5, :], vec[5:6, :], vec[6:7, :] = a
    transpose_into(xT2, n2, seq)
    def gmix(i, _):
        r = rows_of(i)
        w = jnp.concatenate([wo[p] for p in range(P)], axis=1)
        x = nn_dot(n2[r, :], w).astype(bf16)
        for p in range(P):
            gm[p, r, :] = x[:, 128 * p:128 * p + 128]
        return 0
    lax.fori_loop(0, n, gmix, 0)
    def gwo(i, _):
        r = rows_of(i)
        m = jnp.concatenate([mixed[p] for p in range(P)], axis=1)
        x = nn_dot(xT2[r, :], m).astype(bf16)
        for p in range(P):
            dwo[p, r, :] = x[:, 128 * p:128 * p + 128]
        return 0
    lax.fori_loop(0, D // TR, gwo, 0)
    transpose_into(xT, n1, seq)
    gn[...] = jnp.zeros(gn.shape, f32)
    def pair_bwd(hp, _):
        attend_bwd(seq, most, length, qkv, qaug, kaug, mixed, lse, gm, qq, kk, vv, oo, dq, dkv, dqkv, hp)
        def wgrad(i, _):
            r = rows_of(i)
            dwq[hp, r, :] = nn_dot(xT[r, :], dqkv[...]).astype(bf16)
            return 0
        lax.fori_loop(0, D // TR, wgrad, 0)
        def back(i, _):
            r = rows_of(i)
            gn[r, :] += nt_dot(dqkv[r, :], wq[hp])
            return 0
        lax.fori_loop(0, n, back, 0)
        return 0
    lax.fori_loop(0, P, pair_bwd, 0)
    def ln1b(i, acc):
        r = rows_of(i)
        xh, rr = normed(tok[r, :].astype(f32) + tp[...])
        gy = gn[r, :]
        gt = mid[r, :] + norm_back(xh, rr, g1[...], gy)
        gtok[r, :] = gt
        return acc[0] + colsum(gt), acc[1] + colsum(gy * xh), acc[2] + colsum(gy)
    a = lax.fori_loop(0, n, ln1b, (z, z, z))
    vec[1:2, :], vec[2:3, :], vec[3:4, :] = a


def run(T, most, length, ts, tok, cot, seg, wq, wo, wu, wd, wt, btime, g1, b1, g2, b2, bdown, bup):
    seq, D = tok.shape
    P, NF, F = wq.shape[0], wu.shape[0], wu.shape[2]
    V = pltpu.VMEM
    S = jax.ShapeDtypeStruct
    scratch = [V((1, D), f32), V((seq, D), bf16), V((P, seq, 384), bf16), V((seq, 128), bf16), V((seq, 128), bf16),
        V((P, seq, 128), bf16), V((P, seq, 128), f32)] + [V((2, seq, 128), bf16)] * 4 + [V((2, seq, 128), f32),
        V((2, 2, seq, 128), f32), V((seq, 384), bf16), V((seq, D), f32), V((seq, D), bf16), V((seq, D), f32), V((seq, D), f32),
        V((seq, F), bf16), V((seq, F), bf16), V((P, seq, 128), bf16), V((D, seq), bf16), V((D, seq), bf16)]
    vm = pl.BlockSpec(memory_space=pltpu.VMEM)
    sm = pl.BlockSpec(memory_space=pltpu.SMEM)
    return pl.pallas_call(
        functools.partial(kernel, T, most),
        out_shape=(S((seq, D), bf16), S((seq, D), f32), S(wq.shape, bf16), S(wo.shape, bf16), S(wu.shape, bf16), S(wd.shape, bf16), S((16, D), f32)),
        in_specs=[sm, sm] + [vm] * 15, out_specs=[vm] * 7,
        scratch_shapes=scratch,
        compiler_params=pltpu.CompilerParams(vmem_limit_bytes=62 << 20),
    )(length, ts, tok, cot, seg, wq, wo, wu, wd, wt, btime[None], g1[None], b1[None], g2[None], b2[None], bdown[None], bup[None])


def shards(
    tokens,
    timestep,
    segment_ids,
    span_lengths,
    w_qkv,
    w_out_t,
    w_up,
    w_down_t,
    w_time,
    b_time,
    ln1_gain,
    ln1_bias,
    ln2_gain,
    ln2_bias,
    b_up,
    b_down,
    cotangent,
):
    b = lambda w: w.astype(bf16)
    rows, seq, D = tokens.shape
    HB = w_qkv.shape[2]

    def whole(w):
        return lax.all_gather(lax.all_gather(b(w), "dp", axis=0, tiled=True), "tensor", axis=0)

    def part(g):
        g = lax.psum_scatter(g, "dp", scatter_dimension=1, tiled=True)
        return lax.psum_scatter(g, "tensor", scatter_dimension=0, tiled=True)[0].astype(f32)

    wq = whole(jnp.transpose(w_qkv, (1, 0, 2)).reshape(w_qkv.shape[1], 3 * HB))
    wo, wu, wd = whole(w_out_t), whole(w_up), whole(w_down_t)
    out, gtok, dwq, dwo, dwu, dwd, vec = run(
        lambda: lax.axis_index("tensor"), seq // 2, span_lengths, timestep, tokens[0], cotangent[0], segment_ids,
        wq, wo, wu, wd, w_time, b_time, ln1_gain, ln1_bias, ln2_gain, ln2_bias, b_down, b_up)
    lines = lax.all_gather(vec[:2], ("dp", "tensor"), axis=1, tiled=False)
    gwt = jnp.dot(lines[0].T, lines[1], precision=lax.Precision.HIGHEST)
    small = lax.psum(vec[1:], ("dp", "tensor"))
    gq = part(dwq)
    return (
        out[None], gtok[None], jnp.transpose(gq.reshape(gq.shape[0], 3, HB), (1, 0, 2)), part(dwo), part(dwu), part(dwd),
        gwt, small[0], small[1], small[2], small[3], small[4], small[6:10].reshape(-1), small[5])


def solution(mesh):
    return jax.shard_map(
        shards,
        mesh=mesh,
        in_specs=(
            P_(("dp", "tensor"), None, None),
            P_(("dp", "tensor")),
            P_("dp", None),
            P_("dp"),
            P_(None, "dp", "tensor"),
            P_("dp", "tensor"),
            P_("dp", "tensor"),
            P_("dp", "tensor"),
            P_(),
            P_(),
            P_(),
            P_(),
            P_(),
            P_(),
            P_(),
            P_(),
            P_(("dp", "tensor"), None, None),
        ),
        out_specs=(
            P_(("dp", "tensor"), None, None),
            P_(("dp", "tensor"), None, None),
            P_(None, "dp", "tensor"),
            P_("dp", "tensor"),
            P_("dp", "tensor"),
            P_("dp", "tensor"),
            P_(),
            P_(),
            P_(),
            P_(),
            P_(),
            P_(),
            P_(),
            P_(),
        ),
        check_vma=False,
    )
```

time: 528 us -> 507 us (0.960); the launches traced: 518 us -> 506 us
  waiting for transfers between devices: 38.4 us -> 215 us
  matrix products: 150 us -> 2 us
  Pallas kernels: 0 us -> 100 us
  local copies, waits for them, and re-layouts: 77.5 us -> 3.08 us
  other arithmetic: 61.4 us -> 6.19 us
  blocking collectives: 173 us -> 164 us
    dot_general x20 -> x1, matrix products: 150 us -> 2 us  [shards(): gwt = jnp.dot(lines[0].T, lines[1], precision=lax.Precision.HIGHEST)]
    reduce_scatter x4 -> x8, waiting for transfers between devices: 13.7 us -> 131 us  [the longest x4 72.9 us: part(): g = lax.psum_scatter(g, 'dp', scatter_dimension=1, tiled=True)]
    pallas_call x0 -> x1, Pallas kernels: none -> 100 us  [run(): pl.pallas_call(functools.partial(kernel, T, most), out_shape=(S((seq, D),...]
    all_gather x3, waiting for transfers between devices: 0.02 us -> 82.9 us  [whole(): lax.all_gather(lax.all_gather(b(w), 'dp', axis=0, tiled=True), 'tensor',...]
    unnamed x134 -> x9, local copies, waits for them, and re-layouts: 59.4 us -> 1.27 us
    convert_element_type x7, other arithmetic: 33.7 us -> 6.19 us  [the longest x3 4.34 us: part(): lax.psum_scatter(g, 'tensor', scatter_dimension=0, tiled=True)[0]]
    reduce_sum x10 -> x0, other arithmetic: 24.2 us -> none  [the longest x1 13.1 us: attend_forward(): row_total = jnp.sum(raised, axis=-1, keepdims=True)]
    unnamed x15 -> x11, waiting for transfers between devices: 24.6 us -> 1.87 us
  transfers between devices with their start and end apart: 11 -> 11, of which waited for: 2 -> 8; matrix products, arithmetic and copies ran while one was open for 42% -> 2% of each run, Pallas kernels for 0% -> 0%
where the time goes in v2:
time: 507 us; the launch traced here: 506 us
  waiting for transfers between devices  215 us (42%)
  blocking collectives  164 us (32%)
  Pallas kernels  100 us (20%)
  between operations  14.7 us (3%)
  other arithmetic  6.19 us (1%)
    pallas_call x1, Pallas kernels, run(): pl.pallas_call(functools.partial(kernel, T, most), out_shape=(S((seq, D),...  100 us
    all_gather x3, waiting for transfers between devices, whole(): lax.all_gather(lax.all_gather(b(w), 'dp', axis=0, tiled=True), 'tensor',...  82.9 us
    reduce_scatter x4, waiting for transfers between devices, part(): g = lax.psum_scatter(g, 'dp', scatter_dimension=1, tiled=True)  72.9 us
    all_gather x1, blocking collectives, shards(): lines = lax.all_gather(vec[:2], ('dp', 'tensor'), axis=1, tiled=False)  68.3 us
    reduce_scatter x4, waiting for transfers between devices, part(): lax.psum_scatter(g, 'tensor', scatter_dimension=0, tiled=True)[0]  57.7 us
    all_gather x4, blocking collectives, whole(): lax.all_gather(b(w), 'dp', axis=0, tiled=True)  41.9 us
    psum x1, blocking collectives, shards(): small = lax.psum(vec[1:], ('dp', 'tensor'))  37.1 us
    all_gather x1, blocking collectives, whole(): lax.all_gather(lax.all_gather(b(w), 'dp', axis=0, tiled=True), 'tensor',...  17.1 us
  transfers between devices with their start and end apart: 11, of which 8 were waited for; matrix products, arithmetic and copies ran while one was open for 2% of the time, Pallas kernels for 0%

profile of v2, /device:TPU:0, one launch (start us, length us, event | category | flops | bytes accessed | tf_op | source)
XLA Modules:
  0.0 506.1 jit_solution(11984401455087438584)
XLA Ops:
  7.2 0.0 copy-start
  7.2 0.0 copy-start.2
  7.2 0.0 all-gather.9.cloned.1.call-start
  7.2 0.9 copy_bitcast_fusion
  8.2 12.1 %all_gather.42 = bf16[512,384]{1,0:T(8,128)(2,1)} all-gather(bf16[64,384]{1,0:T(8,128)(2,1)S(1)} %copy_bitcast_fusion), channel_id=1, replica_groups=mesh['dp'=8,'tensor'=4] {'dp'}, dimensions={0}, use_global_device_ids=true | all-gather | bytes 442368 | tf_op jit(solution)/shard_map/all_gather | solution.py:386
  20.2 0.0 all-gather.9.cloned.1.call-update
  20.2 0.0 all-gather.13.cloned.1.call-start
  20.3 0.9 convert_element_type.46
  21.2 10.7 %all_gather.51 = bf16[512,512]{1,0:T(8,128)(2,1)} all-gather(bf16[64,512]{1,0:T(8,128)(2,1)S(1)} %convert_element_type.46), channel_id=1, replica_groups=mesh['dp'=8,'tensor'=4] {'dp'}, dimensions={0}, use_global_device_ids=true | all-gather | bytes 589824 | tf_op jit(solution)/shard_map/all_gather | solution.py:386
  32.0 0.0 all-gather.13.cloned.1.call-update
  32.0 0.0 all-gather.11.cloned.1.call-start
  32.0 0.0 copy-done
  32.1 9.9 %all_gather.48 = bf16[512,512]{1,0:T(8,128)(2,1)} all-gather(bf16[64,512]{1,0:T(8,128)(2,1)S(1)} %convert_element_type.45), channel_id=1, replica_groups=mesh['dp'=8,'tensor'=4] {'dp'}, dimensions={0}, use_global_device_ids=true | all-gather | bytes 589824 | tf_op jit(solution)/shard_map/all_gather | solution.py:386
  42.0 0.0 all-gather.11.cloned.1.call-update
  42.0 0.0 reduce-scatter.13.cloned.1.call-start
  42.7 0.0 copy-done.2
  42.8 9.1 %all_gather.45 = bf16[512,128]{1,0:T(8,128)(2,1)S(1)} all-gather(bf16[64,128]{1,0:T(8,128)(2,1)S(1)} %convert_element_type.44), channel_id=1, replica_groups=mesh['dp'=8,'tensor'=4] {'dp'}, dimensions={0}, use_global_device_ids=true | all-gather | bytes 147456 | tf_op jit(solution)/shard_map/all_gather | solution.py:386
  51.9 17.1 %all-gather.1 = bf16[2048,128]{1,0:T(8,128)(2,1)} all-gather(bf16[512,128]{1,0:T(8,128)(2,1)S(1)} %all_gather.45), channel_id=3, replica_groups=mesh['dp'=8,'tensor'=4] {'tensor'}, dimensions={0}, use_global_device_ids=true | all-gather | bytes 655360 | tf_op jit(solution)/shard_map/all_gather | solution.py:386
  69.0 0.0 all-gather.9.cloned.1.call-done
  69.0 36.7 %all-gather.13.cloned.1.call-done = bf16[2048,512]{1,0:T(8,128)(2,1)} async-done(((bf16[512,512]{1,0:T(8,128)(2,1)}), bf16[2048,512]{1,0:T(8,128)(2,1)}) %all-gather.13.cloned.1.call-update) | async-done | bytes 2097168 | tf_op jit(solution)/shard_map/all_gather | solution.py:386
  105.6 46.3 %all-gather.11.cloned.1.call-done = bf16[2048,512]{1,0:T(8,128)(2,1)} async-done(((bf16[512,512]{1,0:T(8,128)(2,1)}), bf16[2048,512]{1,0:T(8,128)(2,1)}) %all-gather.11.cloned.1.call-update) | async-done | bytes 2097168 | tf_op jit(solution)/shard_map/all_gather | solution.py:386
  151.9 100.0 %shard_map.272 = (bf16[1024,512]{1,0:T(8,128)(2,1)}, f32[1024,512]{1,0:T(8,128)}, bf16[4,512,384]{2,1,0:T(8,128)(2,1)}, bf16[4,512,128]{2,1,0:T(8,128)(2,1)}, bf...) custom-call(s32[4]{0:T(128)} %len_ref.1, s32[1]{0:T(128)S(6)} %copy.37.ts_ref, ...), custom_call_target="tpu_custom_call" | custom-call | tf_op jit(solution)/shard_map/pallas_call | solution.py:353
  251.9 0.0 reduce-scatter.13.cloned.1.call-update
  251.9 0.0 reduce-scatter.9.cloned.1.call-start
  252.0 0.5 reduce-scatter.9.cloned.1.call-update
  252.5 0.0 reduce-scatter.21.cloned.1.call-start
  252.6 0.0 copy-start.1
  252.6 0.5 reduce-scatter.21.cloned.1.call-update
  253.1 0.0 reduce-scatter.17.cloned.1.call-start
  253.1 0.7 reduce-scatter.17.cloned.1.call-update
  253.8 0.0 reduce-scatter.15.cloned.1.call-start
  253.9 31.0 %reduce-scatter.13.cloned.1.call-done = bf16[4,64,128]{2,1,0:T(8,128)(2,1)} async-done(((bf16[4,512,128]{2,1,0:T(8,128)(2,1)}), bf16[4,64,128]{2,1,0:T(8,128)(2,1)}) %reduce-scatter.13.cloned.1.call-update) | async-done | bytes 65552 | tf_op jit(solution)/shard_map/reduce_scatter | solution.py:389
  284.9 0.0 reduce-scatter.15.cloned.1.call-update
  284.9 0.0 reduce-scatter.11.cloned.1.call-start
  285.0 41.9 %reduce-scatter.9.cloned.1.call-done = bf16[4,64,384]{2,1,0:T(8,128)(2,1)} async-done(((bf16[4,512,384]{2,1,0:T(8,128)(2,1)}), bf16[4,64,384]{2,1,0:T(8,128)(2,1)}) %reduce-scatter.9.cloned.1.call-update) | async-done | bytes 196624 | tf_op jit(solution)/shard_map/reduce_scatter | solution.py:389
  326.9 0.0 reduce-scatter.11.cloned.1.call-update
  326.9 0.0 reduce-scatter.23.cloned.1.call-start
  327.0 0.0 copy-done.1
  327.0 68.3 %all-gather.4 = f32[2,16384]{1,0:T(2,128)S(1)} all-gather(f32[2,512]{1,0:T(2,128)S(1)} %slice.33), channel_id=6, replica_groups=mesh['dp'=8,'tensor'=4] {'dp','tensor'}, dimensions={1}, use_global_device_ids=true | all-gather | bytes 135168 | tf_op jit(solution)/shard_map/all_gather | solution.py:397
  395.2 0.0 reduce-scatter.21.cloned.1.call-done
  395.2 0.0 reduce-scatter.23.cloned.1.call-update
  395.3 0.0 reduce-scatter.19.cloned.1.call-start
  395.3 0.3 slice_reduce_fusion
  395.7 37.1 %psum.7 = f32[15,512]{1,0:T(8,128)S(1)} all-reduce(f32[15,512]{1,0:T(8,128)S(1)} %slice.36), channel_id=1, replica_groups=mesh['dp'=8,'tensor'=4] {'dp','tensor'}, use_global_device_ids=true, to_apply=%region_8.0 | all-reduce | flops 7680 | bytes 61440 | tf_op jit(solution)/shard_map/psum | solution.py:399
  432.8 0.6 fusion
  433.4 2.0 fusion.1
  435.4 0.0 reduce-scatter.17.cloned.1.call-done
  435.4 0.0 reduce-scatter.19.cloned.1.call-update
  435.5 0.6 copy.35
  436.1 1.9 reduce-scatter.15.cloned.1.call-done
  437.9 1.3 bitcast_convert_fusion.2
  439.3 18.6 %reduce-scatter.11.cloned.1.call-done = bf16[1,64,384]{2,1,0:T(8,128)(2,1)} async-done(((bf16[4,64,384]{2,1,0:T(8,128)(2,1)}), bf16[1,64,384]{2,1,0:T(8,128)(2,1)}) %reduce-scatter.11.cloned.1.call-update) | async-done | bytes 49168 | tf_op jit(solution)/shard_map/reduce_scatter | solution.py:390
  457.8 0.8 reshape.47
  458.7 0.6 copy.33
  459.3 18.5 %reduce-scatter.23.cloned.1.call-done = bf16[1,64,512]{2,1,0:T(8,128)(2,1)} async-done(((bf16[4,64,512]{2,1,0:T(8,128)(2,1)}), bf16[1,64,512]{2,1,0:T(8,128)(2,1)}) %reduce-scatter.23.cloned.1.call-update) | async-done | bytes 65552 | tf_op jit(solution)/shard_map/reduce_scatter | solution.py:390
  477.9 1.5 bitcast_convert_fusion
  479.4 18.7 %reduce-scatter.19.cloned.1.call-done = bf16[1,64,512]{2,1,0:T(8,128)(2,1)} async-done(((bf16[4,64,512]{2,1,0:T(8,128)(2,1)}), bf16[1,64,512]{2,1,0:T(8,128)(2,1)}) %reduce-scatter.19.cloned.1.call-update) | async-done | bytes 65552 | tf_op jit(solution)/shard_map/reduce_scatter | solution.py:390
  498.1 1.5 bitcast_convert_fusion.1
  (7 shorter events, 0.1 us)
Async XLA Ops:
  7.2 24.9 %copy-start = (f32[64,512]{1,0:T(8,128)S(1)}, f32[64,512]{1,0:T(8,128)}, u32[]{:S(2)}) copy-start(f32[64,512]{1,0:T(8,128)} %param.23) | copy-start | bytes 393220
  7.2 35.6 %copy-start.2 = (f32[64,128]{1,0:T(8,128)S(1)}, f32[64,128]{1,0:T(8,128)}, u32[]{:S(2)}) copy-start(f32[64,128]{1,0:T(8,128)} %param.22) | copy-start | bytes 98308
  7.2 61.8 %all-gather.9.cloned.1.call-start = ((), (), s32[]{:S(2)}) async-start(), calls=%async_computation.16 | async-start | bytes 1966080 | tf_op jit(solution)/shard_map/all_gather | solution.py:386
  20.2 85.4 %all-gather.13.cloned.1.call-start = ((), (), s32[]{:S(2)}) async-start(), calls=%async_computation.18 | async-start | bytes 2621440 | tf_op jit(solution)/shard_map/all_gather | solution.py:386
  32.0 119.9 %all-gather.11.cloned.1.call-start = ((), (), s32[]{:S(2)}) async-start(), calls=%async_computation.17 | async-start | bytes 2621440 | tf_op jit(solution)/shard_map/all_gather | solution.py:386
  42.0 242.8 %reduce-scatter.13.cloned.1.call-start = ((), (), s32[]{:S(2)}) async-start(), calls=%async_computation.10 | async-start | bytes 589824 | tf_op jit(solution)/shard_map/reduce_scatter | solution.py:389
  251.9 75.0 %reduce-scatter.9.cloned.1.call-start = ((), (), s32[]{:S(2)}) async-start(), calls=%async_computation.8 | async-start | bytes 1769472 | tf_op jit(solution)/shard_map/reduce_scatter | solution.py:389
  252.5 142.7 %reduce-scatter.21.cloned.1.call-start = ((), (), s32[]{:S(2)}) async-start(), calls=%async_computation.14 | async-start | bytes 2359296 | tf_op jit(solution)/shard_map/reduce_scatter | solution.py:389
  252.6 74.4 %copy-start.1 = (f32[16,512]{1,0:T(8,128)S(1)}, f32[16,512]{1,0:T(8,128)}, u32[]{:S(2)}) copy-start(f32[16,512]{1,0:T(8,128)} %get-tuple-element.27) | copy-start | bytes 98308
  253.1 182.4 %reduce-scatter.17.cloned.1.call-start = ((), (), s32[]{:S(2)}) async-start(), calls=%async_computation.12 | async-start | bytes 2359296 | tf_op jit(solution)/shard_map/reduce_scatter | solution.py:389
  253.8 184.1 %reduce-scatter.15.cloned.1.call-start = ((), (), s32[]{:S(2)}) async-start(), calls=%async_computation.11 | async-start | bytes 81920 | tf_op jit(solution)/shard_map/reduce_scatter | solution.py:390
  284.9 172.9 %reduce-scatter.11.cloned.1.call-start = ((), (), s32[]{:S(2)}) async-start(), calls=%async_computation.9 | async-start | bytes 245760 | tf_op jit(solution)/shard_map/reduce_scatter | solution.py:390
  326.9 150.9 %reduce-scatter.23.cloned.1.call-start = ((), (), s32[]{:S(2)}) async-start(), calls=%async_computation.15 | async-start | bytes 327680 | tf_op jit(solution)/shard_map/reduce_scatter | solution.py:390
  395.3 102.8 %reduce-scatter.19.cloned.1.call-start = ((), (), s32[]{:S(2)}) async-start(), calls=%async_computation.13 | async-start | bytes 327680 | tf_op jit(solution)/shard_map/reduce_scatter | solution.py:390
Sparse Core Ops, SparseCore 0:
  20.4 37.4 all-gather.8
  59.5 46.1 all-gather.12
  107.2 44.6 all-gather.10
  252.0 32.7 reduce-scatter.12
  288.4 38.4 reduce-scatter.8
  330.4 41.2 reduce-scatter.20
  374.9 41.6 reduce-scatter.16
  418.9 18.9 reduce-scatter.14
  440.2 17.5 reduce-scatter.10
  460.0 17.7 reduce-scatter.22
  480.1 17.9 reduce-scatter.18

commit v3 on v2

--- a/solution.py
+++ b/solution.py
@@ -13,6 +13,7 @@
 TR = 256
 BIG = 1e30
 EPS = 1e-5
+DOC = 512
 LOG2E = math.log2(math.e)
 LN2 = math.log(2.0)
 SCALE = 1.0 / math.sqrt(HS)
@@ -201,27 +202,466 @@
         dst[:, r] = src[r, :].T
 
 
-def kernel(T, most, len_ref, ts_ref, tok, cot, seg, wq, wo, wu, wd, wt, btime, g1, b1, g2, b2, bdown, bup,
-           out, gtok, dwq, dwo, dwu, dwd, vec,
-           tp, n1, qkv, qaug, kaug, mixed, lse, qq, kk, vv, oo, dq, dkv, dqkv, mid, n2, ffn, gn, act, gu, gm, xT, xT2):
+MESH = pl.DeviceIdType.MESH
+
+
+class Plain:
+    def __init__(self, wq, wo, w2, dwq, dwo, dw2, vec):
+        self.wq, self.wo, self.w2 = wq, wo, w2
+        self.dwq, self.dwo, self.dw2, self.vec = dwq, dwo, dw2, vec
+
+    def getq(self, p):
+        return self.wq[p]
+
+    def geto(self):
+        return jnp.concatenate([self.wo[p] for p in range(self.wo.shape[0])], axis=1)
+
+    def getu(self, f):
+        return self.w2[f, 0]
+
+    def getd(self, f):
+        return self.w2[f, 1]
+
+    def putq(self, p, i, x):
+        self.dwq[p, rows_of(i), :] = x
+
+    def puto(self, p, i, x):
+        self.dwo[p, rows_of(i), :] = x
+
+    def put2(self, f, k, i, x):
+        self.dw2[f, k, rows_of(i), :] = x
+
+    def order(self, j):
+        return j
+
+    def order_back(self, j):
+        return j
+
+    def hook(self, *_):
+        pass
+
+    def early(self, rows):
+        for k, x in enumerate(rows):
+            self.vec[k:k + 1, :] = x
+
+    def late(self, rows):
+        for k, x in enumerate(rows):
+            self.vec[8 + k:9 + k, :] = x
+
+
+class Linked:
+    def __init__(self, ng, nt, bufs, sems):
+        self.ng, self.nt = ng, nt
+        self.__dict__.update(bufs)
+        self.sem = sems
+        d, self.t = lax.axis_index("dp"), lax.axis_index("tensor")
+        self.d, self.g, self.c = d, d // 2, d % 2
+        self.sent = []
+
+    def dev(self, kind, k):
+        if kind == "core":
+            return (2 * self.g + 1 - self.c, self.t)
+        if kind == "plane":
+            return (2 * (self.g ^ k) + self.c, self.t)
+        return (self.d, self.t ^ k)
+
+    def copy(self, name, at, kind, k, src, dst):
+        s, r = self.sem[name]
+        for i in at:
+            s, r = s.at[i], r.at[i]
+        return pltpu.make_async_remote_copy(
+            src_ref=src, dst_ref=dst, send_sem=s, recv_sem=r,
+            device_id=self.dev(kind, k), device_id_type=MESH)
+
+    def getq(self, p):
+        x = self.WQ[p]
+        return x.reshape(-1, x.shape[-1])
+
+    def geto(self):
+        return jnp.concatenate([self.WO[p].reshape(-1, 128) for p in range(self.nt)], axis=1)
+
+    def getu(self, f):
+        x = self.W2[f, 0]
+        return x.reshape(-1, x.shape[-1])
+
+    def getd(self, f):
+        x = self.W2[f, 1]
+        return x.reshape(-1, x.shape[-1])
+
+    def blocks(self, ref, i):
+        rows = ref.shape[-2]
+        m = TR // (2 * rows)
+        return pl.ds(i * m, m), (m, 2, rows, ref.shape[-1])
+
+    def putq(self, p, i, x):
+        b, shape = self.blocks(self.DQ, i)
+        self.DQ[p, b] = x.reshape(shape)
+
+    def puto(self, p, i, x):
+        b, shape = self.blocks(self.DO, i)
+        self.DO[p, b] = x.reshape(shape)
+
+    def put2(self, f, k, i, x):
+        b, shape = self.blocks(self.D2, i)
+        self.D2[f, k, b] = x.reshape(shape)
+
+    def order(self, j):
+        return self.t ^ j
+
+    def order_back(self, j):
+        return self.t ^ (self.nt - 1 - j)
+
+    def enter(self):
+        bar = pltpu.get_barrier_semaphore()
+        peers = [("core", 0)] + [("plane", k) for k in range(1, self.ng)] + [("z", k) for k in range(1, self.nt)]
+        for kind, k in peers:
+            pl.semaphore_signal(bar, inc=1, device_id=self.dev(kind, k), device_id_type=MESH)
+        pl.semaphore_wait(bar, len(peers))
+
+    def q_plane(self, k):
+        g, c, t = self.g, self.c, self.t
+        return self.copy("gq_plane", (k,), "plane", k, self.WQ.at[t, g, c], self.WQ.at[t, g, c])
+
+    def q_plane_in(self, k):
+        g, c, t = self.g, self.c, self.t
+        return self.copy("gq_plane", (k,), "plane", k, self.WQ.at[t, g, c], self.WQ.at[t, g ^ k, c])
+
+    def q_z(self, k):
+        c, t = self.c, self.t
+        return self.copy("gq_z", (k,), "z", k, self.WQ.at[t, :, c], self.WQ.at[t, :, c])
+
+    def q_z_in(self, k):
+        c, t = self.c, self.t
+        return self.copy("gq_z", (k,), "z", k, self.WQ.at[t, :, c], self.WQ.at[t ^ k, :, c])
+
+    def q_core(self, k):
+        c, t = self.c, self.t
+        return self.copy("gq_core", (k,), "core", 0, self.WQ.at[t ^ k, :, c], self.WQ.at[t ^ k, :, c])
+
+    def q_core_in(self, k):
+        c, t = self.c, self.t
+        return self.copy("gq_core", (k,), "core", 0, self.WQ.at[t ^ k, :, c], self.WQ.at[t ^ k, :, 1 - c])
+
+    def r_z(self, k, into=None):
+        g, c, t = self.g, self.c, self.t
+        u = t if into is None else into
+        return [self.copy("go_z", (k,), "z", k, self.WO.at[t, g, c], self.WO.at[u, g, c]),
+                self.copy("g2_z", (k,), "z", k, self.W2.at[t, :, g, c], self.W2.at[u, :, g, c])]
+
+    def o_plane(self, k, incoming=False):
+        g, c = self.g, self.c
+        return self.copy("go_plane", (k,), "plane", k, self.WO.at[:, g, c], self.WO.at[:, g ^ k if incoming else g, c])
+
+    def o_core(self, incoming=False):
+        c = self.c
+        return self.copy("go_core", (), "core", 0, self.WO.at[:, :, c], self.WO.at[:, :, 1 - c if incoming else c])
+
+    def f_plane(self, j, k, incoming=False):
+        g, c, f = self.g, self.c, self.t ^ j
+        return self.copy("g2_plane", (j, k), "plane", k, self.W2.at[f, :, g, c], self.W2.at[f, :, g ^ k if incoming else g, c])
+
+    def f_core(self, j, incoming=False):
+        c, f = self.c, self.t ^ j
+        return self.copy("g2_core", (j,), "core", 0, self.W2.at[f, :, :, c], self.W2.at[f, :, :, 1 - c if incoming else c])
+
+    def rq(self, stage, x, k=0, incoming=False):
+        g, c, p = self.g, self.c, self.t ^ x
+        if stage == "core":
+            return self.copy("rq_core", (x,), "core", 0, self.DQ.at[p, :, 1 - c], self.CQ.at[x])
+        if stage == "plane":
+            return self.copy("rq_plane", (x, k), "plane", k, self.DQ.at[p, g ^ k, c], self.XQ.at[x, k])
+        return self.copy("rq_z", (x,), "z", x, self.DQ.at[p, g, c], self.ZQ.at[x])
+
+    def r2(self, stage, x, k=0):
+        g, c, p = self.g, self.c, self.t ^ x
+        if stage == "core":
+            return self.copy("r2_core", (x,), "core", 0, self.D2.at[p, :, :, 1 - c], self.C2.at[x])
+        if stage == "plane":
+            return self.copy("r2_plane", (x, k), "plane", k, self.D2.at[p, :, g ^ k, c], self.X2.at[x, k])
+        return self.copy("r2_z", (x,), "z", x, self.D2.at[p, :, g, c], self.Z2.at[x])
+
+    def ro(self, stage, k=0):
+        g, c, t = self.g, self.c, self.t
+        if stage == "core":
+            return self.copy("ro_core", (), "core", 0, self.DO.at[:, :, 1 - c], self.CO)
+        if stage == "plane":
+            return self.copy("ro_plane", (k,), "plane", k, self.DO.at[:, g ^ k, c], self.XO.at[k])
+        return self.copy("ro_z", (k,), "z", k, self.DO.at[t ^ k, g, c], self.ZO.at[k])
+
+    def q_after_core(self, x):
+        p, c = self.t ^ x, self.c
+        self.rq("core", x).wait_recv()
+        self.DQ[p, :, c] = (self.DQ[p, :, c].astype(f32) + self.CQ[x].astype(f32)).astype(bf16)
+        for k in range(1, self.ng):
+            self.rq("plane", x, k).start()
+
+    def q_after_plane(self, x):
+        p, c, g = self.t ^ x, self.c, self.g
+        acc = self.DQ[p, g, c].astype(f32)
+        for k in range(1, self.ng):
+            self.rq("plane", x, k).wait_recv()
+            acc = acc + self.XQ[x, k].astype(f32)
+        self.DQ[p, g, c] = acc.astype(bf16)
+
+    def f_after_core(self, x):
+        p, c = self.t ^ x, self.c
+        self.r2("core", x).wait_recv()
+        for u in range(2):
+            def step(i, _):
+                self.D2[p, u, i, c] = (self.D2[p, u, i, c].astype(f32) + self.C2[x, u, i].astype(f32)).astype(bf16)
+                return 0
+            lax.fori_loop(0, self.ng, step, 0)
+        for k in range(1, self.ng):
+            self.r2("plane", x, k).start()
+
+    def f_after_plane(self, x):
+        p, c, g = self.t ^ x, self.c, self.g
+        for k in range(1, self.ng):
+            self.r2("plane", x, k).wait_recv()
+        for u in range(2):
+            acc = self.D2[p, u, g, c].astype(f32)
+            for k in range(1, self.ng):
+                acc = acc + self.X2[x, k, u].astype(f32)
+            self.D2[p, u, g, c] = acc.astype(bf16)
+
+    def hook(self, place, j=None):
+        ng, nt, t, g, c = self.ng, self.nt, self.t, self.g, self.c
+        if place == "start":
+            rq = self.w_qkv.shape[1]
+            for k in range(3):
+                self.WQ[t, g, c, :, 128 * k:128 * k + 128] = self.w_qkv[k].astype(bf16)
+            self.WO[t, g, c] = self.w_out[...].astype(bf16)
+            self.W2[t, 0, g, c] = self.w_up[...].astype(bf16)
+            self.W2[t, 1, g, c] = self.w_down[...].astype(bf16)
+            self.enter()
+            for k in range(1, ng):
+                self.q_plane(k).start()
+        elif place == "normed":
+            for k in range(1, ng):
+                self.q_plane_in(k).wait_recv()
+            self.q_core(0).start()
+            for k in range(1, nt):
+                self.q_z(k).start()
+            for k in range(1, nt):
+                for x in self.r_z(k):
+                    x.start()
+        elif place == "pair":
+            self.q_core_in(j).wait_recv()
+        elif place == "pair_mid":
+            @pl.when(j < nt - 1)
+            def _():
+                self.q_z_in(j + 1).wait_recv()
+                self.q_core(j + 1).start()
+            @pl.when(j == nt // 2)
+            def _():
+                for k in range(1, nt):
+                    for x in self.r_z(k, t ^ k):
+                        x.wait_recv()
+                for k in range(1, ng):
+                    self.o_plane(k).start()
+                for x in range(nt):
+                    for k in range(1, ng):
+                        self.f_plane(x, k).start()
+        elif place == "mixed":
+            for k in range(1, ng):
+                self.o_plane(k, True).wait_recv()
+            self.o_core().start()
+            for k in range(1, ng):
+                self.f_plane(0, k, True).wait_recv()
+            self.f_core(0).start()
+            self.o_core(True).wait_recv()
+        elif place == "chunk":
+            self.f_core(j, True).wait_recv()
+        elif place == "chunk_mid":
+            @pl.when(j < nt - 1)
+            def _():
+                for k in range(1, ng):
+                    self.f_plane(j + 1, k, True).wait_recv()
+                self.f_core(j + 1).start()
+            @pl.when(j >= 1)
+            def _():
+                self.f_after_core(j - 1)
+            @pl.when(j >= 2)
+            def _():
+                self.f_after_plane(j - 2)
+                @pl.when(j >= 3)
+                def _():
+                    self.r2("z", j - 2).start()
+        elif place == "chunk_end":
+            self.r2("core", j).start()
+        elif place == "ffn_done":
+            self.f_after_core(nt - 1)
+            self.f_after_plane(nt - 2)
+            self.r2("z", nt - 2).start()
+        elif place == "out_grad":
+            self.ro("core").start()
+        elif place == "back_mid":
+            @pl.when(j == 0)
+            def _():
+                self.f_after_plane(nt - 1)
+                self.r2("z", nt - 1).start()
+                self.ro("core").wait_recv()
+                for p in range(nt):
+                    self.DO[p, :, c] = (self.DO[p, :, c].astype(f32) + self.CO[p].astype(f32)).astype(bf16)
+                for k in range(1, ng):
+                    self.ro("plane", k).start()
+            @pl.when(j == 1)
+            def _():
+                for k in range(1, ng):
+                    self.ro("plane", k).wait_recv()
+                for p in range(nt):
+                    acc = self.DO[p, g, c].astype(f32)
+                    for k in range(1, ng):
+                        acc = acc + self.XO[k, p].astype(f32)
+                    self.DO[p, g, c] = acc.astype(bf16)
+                for k in range(1, nt):
+                    self.ro("z", k).start()
+            @pl.when(j >= 1)
+            def _():
+                self.q_after_core(nt - j)
+            @pl.when(j >= 2)
+            def _():
+                self.q_after_plane(nt - j + 1)
+                self.rq("z", nt - j + 1).start()
+        elif place == "back_end":
+            self.rq("core", nt - 1 - j).start()
+        elif place == "back_done":
+            self.q_after_core(0)
+            self.q_after_plane(1)
+            self.rq("z", 1).start()
+        elif place == "finish":
+            for x in range(1, nt):
+                self.r2("z", x).wait_recv()
+                self.ro("z", x).wait_recv()
+            for u, o in enumerate((self.o_up, self.o_down)):
+                acc = self.D2[t, u, g, c].astype(f32)
+                for x in range(1, nt):
+                    acc = acc + self.Z2[x, u].astype(f32)
+                o[...] = acc
+            acc = self.DO[t, g, c].astype(f32)
+            for x in range(1, nt):
+                acc = acc + self.ZO[x].astype(f32)
+            self.o_out[...] = acc
+            acc = self.DQ[t, g, c].astype(f32)
+            for k in range(1, ng):
+                self.rq("plane", 0, k).wait_recv()
+                acc = acc + self.XQ[0, k].astype(f32)
+            for x in range(1, nt):
+                self.rq("z", x).wait_recv()
+                acc = acc + self.ZQ[x].astype(f32)
+            for k in range(3):
+                self.o_qkv[k] = acc[:, 128 * k:128 * k + 128]
+        elif place == "leave":
+            for k in range(1, ng):
+                self.q_plane(k).wait_send()
+                self.o_plane(k).wait_send()
+                self.ro("plane", k).wait_send()
+                for x in range(nt):
+                    self.f_plane(x, k).wait_send()
+                    self.r2("plane", x, k).wait_send()
+                    self.rq("plane", x, k).wait_send()
+            for k in range(nt):
+                self.q_core(k).wait_send()
+                self.f_core(k).wait_send()
+                self.r2("core", k).wait_send()
+                self.rq("core", k).wait_send()
+            self.o_core().wait_send()
+            self.ro("core").wait_send()
+            for k in range(1, nt):
+                self.q_z(k).wait_send()
+                for x in self.r_z(k):
+                    x.wait_send()
+                self.r2("z", k).wait_send()
+                self.rq("z", k).wait_send()
+                self.ro("z", k).wait_send()
+
+    def v(self, name, stage, k):
+        B = getattr(self, name)
+        Z, X, C = B
+        if stage == "z":
+            return self.copy(name + "_z", (k,), "z", k, Z.at[self.t], Z.at[self.t])
+        if stage == "plane":
+            return self.copy(name + "_plane", (k,), "plane", k, X.at[self.g], X.at[self.g])
+        return self.copy(name + "_core", (), "core", 0, C.at[self.c], C.at[self.c])
+
+    def v_in(self, name, stage, k):
+        Z, X, C = getattr(self, name)
+        if stage == "z":
+            return self.copy(name + "_z", (k,), "z", k, Z.at[self.t], Z.at[self.t ^ k])
+        if stage == "plane":
+            return self.copy(name + "_plane", (k,), "plane", k, X.at[self.g], X.at[self.g ^ k])
+        return self.copy(name + "_core", (), "core", 0, C.at[self.c], C.at[1 - self.c])
+
+    def v_start(self, name, rows):
+        Z = getattr(self, name)[0]
+        for k, x in enumerate(rows):
+            Z[self.t, k:k + 1, :] = x
+        for k in range(1, self.nt):
+            self.v(name, "z", k).start()
+
+    def v_mid(self, name, m):
+        Z, X, C = getattr(self, name)
+        nt = self.nt
+        for k in range(1, nt):
+            self.v_in(name, "z", k).wait_recv()
+        for k in range(nt):
+            X[self.g, k:k + 1, :] = Z[k, 0:1, :]
+        s = Z[0, 1:m, :]
+        for k in range(1, nt):
+            s = s + Z[k, 1:m, :]
+        X[self.g, 8:8 + m - 1, :] = s
+        for k in range(1, self.ng):
+            self.v(name, "plane", k).start()
+
+    def v_last(self, name, m):
+        Z, X, C = getattr(self, name)
+        nt, ng = self.nt, self.ng
+        for k in range(1, ng):
+            self.v_in(name, "plane", k).wait_recv()
+        for k in range(ng):
+            C[self.c, k * nt:k * nt + nt, :] = X[k, 0:nt, :]
+        s = X[0, 8:8 + m - 1, :]
+        for k in range(1, ng):
+            s = s + X[k, 8:8 + m - 1, :]
+        C[self.c, ng * nt:ng * nt + m - 1, :] = s
+        self.v(name, "core", 0).start()
+
+    def v_done(self, name, m):
+        C = getattr(self, name)[2]
+        n = self.nt * self.ng
+        self.v_in(name, "core", 0).wait_recv()
+        kept = jnp.concatenate([C[0, 0:n, :], C[1, 0:n, :]], axis=0)
+        return kept, C[0, n:n + m - 1, :] + C[1, n:n + m - 1, :]
+
+    def v_leave(self, name):
+        for k in range(1, self.nt):
+            self.v(name, "z", k).wait_send()
+        for k in range(1, self.ng):
+            self.v(name, "plane", k).wait_send()
+        self.v(name, "core", 0).wait_send()
+
+
+def layer(cm, T, most, length, t, tok, cot, seg, wt, btime, g1, b1, g2, b2, bdown, bup, out, gtok, sc):
+    tp, n1, qkv, qaug, kaug, mixed, lse, qq, kk, vv, oo, dq, dkv, dqkv, mid, n2, ffn, gn, act, gu, gm, xT, xT2, bsum = sc
     seq, D = tok.shape
-    P = wq.shape[0]
+    P = qkv.shape[0]
+    NF, F = bsum.shape[0], bsum.shape[2]
     n = seq // TR
-    length = len_ref[T()]
-    t = ts_ref[0].astype(f32)
+    cm.hook("start")
     half = D // 2
     ang = t * jnp.exp(-math.log(10000.0) * lax.broadcasted_iota(jnp.int32, (8, half), 1).astype(f32) / half)
     emb = jnp.concatenate([jnp.sin(ang), jnp.cos(ang)], axis=1)
-    vec[0:1, :] = emb[0:1, :]
-    proj = jnp.dot(emb, wt[...], precision=lax.Precision.HIGHEST, preferred_element_type=f32)[0:1, :] + btime[...]
-    tp[...] = proj
+    tp[...] = jnp.dot(emb, wt[...], precision=lax.Precision.HIGHEST, preferred_element_type=f32)[0:1, :] + btime[...]
+
     def ln1(i, _):
         r = rows_of(i)
         xh, _r = normed(tok[r, :].astype(f32) + tp[...])
         n1[r, :] = (xh * g1[...] + b1[...]).astype(bf16)
         return 0
+
     lax.fori_loop(0, n, ln1, 0)
-    srow = seg[pl.ds(T(), 1), :].astype(f32)
+    cm.hook("normed")
+    srow = seg[pl.ds(T, 1), :].astype(f32)
     for b in range(seq // 128):
         col = jnp.broadcast_to(srow[:, 128 * b:128 * b + 128], (128, 128)).T
         spot = lane((128, 128)) % HS
@@ -231,56 +671,72 @@
         qaug[r, :] = jnp.where(same & (spot < 8), 1.0, 0.0).astype(bf16)
         ka = jnp.where(same & (pos < length), 0.0, -BIG)
         kaug[r, :] = jnp.where(spot < 8, ka, jnp.where(spot < 11, -1.0, 0.0)).astype(bf16)
-    def pair_fwd(hp, _):
+
+    def pair_fwd(j, _):
+        hp = cm.order(j)
+        cm.hook("pair", j)
+
         def proj(i, _):
             r = rows_of(i)
-            x = nn_dot(n1[r, :], wq[hp])
+            x = nn_dot(n1[r, :], cm.getq(hp))
             s = jnp.where(lane((1, 384)) < 128, SCALE * LOG2E, 1.0)
             qkv[hp, r, :] = (x * s).astype(bf16)
             return 0
+
         lax.fori_loop(0, n, proj, 0)
         attend_fwd(seq, most, length, qkv, qaug, kaug, mixed, lse, qq, kk, vv, hp)
+        cm.hook("pair_mid", j)
         return 0
+
     lax.fori_loop(0, P, pair_fwd, 0)
+    cm.hook("mixed")
+
     def ln2(i, _):
         r = rows_of(i)
         mx = jnp.concatenate([mixed[p, r, :] for p in range(P)], axis=1)
-        w = jnp.concatenate([wo[p] for p in range(P)], axis=1)
-        x = tok[r, :].astype(f32) + tp[...] + nt_dot(mx, w)
+        x = tok[r, :].astype(f32) + tp[...] + nt_dot(mx, cm.geto())
         mid[r, :] = x
         xh, _r = normed(x)
         n2[r, :] = (xh * g2[...] + b2[...]).astype(bf16)
+        ffn[r, :] = jnp.zeros((TR, D), f32)
+        gn[r, :] = jnp.zeros((TR, D), f32)
         return 0
+
     lax.fori_loop(0, n, ln2, 0)
     transpose_into(xT, cot, seq)
     transpose_into(xT2, n2, seq)
-    for f in range(wu.shape[0]):
-        F = wu.shape[2]
+
+    def chunk(j, _):
+        f = cm.order(j)
+        cm.hook("chunk", j)
+
         def tile(i, acc):
             r = rows_of(i)
-            u = nn_dot(n2[r, :], wu[f]) + bup[:, f * F:f * F + F]
+            u = nn_dot(n2[r, :], cm.getu(f)) + bup[f]
             a, ga = gelu_parts(u)
             a = a.astype(bf16)
-            g = (nn_dot(cot[r, :], wd[f]) * ga).astype(bf16)
+            g = (nn_dot(cot[r, :], cm.getd(f)) * ga).astype(bf16)
             act[r, :] = a
             gu[r, :] = g
-            fo = nt_dot(a, wd[f])
-            go = nt_dot(g, wu[f])
-            if f == 0:
-                ffn[r, :] = fo
-                gn[r, :] = go
-            else:
-                ffn[r, :] += fo
-                gn[r, :] += go
+            ffn[r, :] += nt_dot(a, cm.getd(f))
+            gn[r, :] += nt_dot(g, cm.getu(f))
             return acc + colsum(g.astype(f32))
-        acc = lax.fori_loop(0, n, tile, jnp.zeros((1, F), f32))
-        vec[7 + f:8 + f, :] = acc
+
+        bsum[f] = lax.fori_loop(0, n, tile, jnp.zeros((1, F), f32))
+        cm.hook("chunk_mid", j)
+
         def wgrad(i, _):
             r = rows_of(i)
-            dwd[f, r, :] = nn_dot(xT[r, :], act[...]).astype(bf16)
-            dwu[f, r, :] = nn_dot(xT2[r, :], gu[...]).astype(bf16)
+            cm.put2(f, 1, i, nn_dot(xT[r, :], act[...]).astype(bf16))
+            cm.put2(f, 0, i, nn_dot(xT2[r, :], gu[...]).astype(bf16))
             return 0
+
         lax.fori_loop(0, D // TR, wgrad, 0)
+        cm.hook("chunk_end", j)
+        return 0
+
+    lax.fori_loop(0, NF, chunk, 0)
+
     def ln2b(i, acc):
         r = rows_of(i)
         c = cot[r, :].astype(f32)
@@ -291,43 +747,59 @@
         gmid = c + norm_back(xh, rr, g2[...], gy)
         mid[r, :] = gmid
         n2[r, :] = gmid.astype(bf16)
+        gn[r, :] = jnp.zeros((TR, D), f32)
         return acc[0] + colsum(gy * xh), acc[1] + colsum(gy), acc[2] + colsum(c)
+
     z = jnp.zeros((1, D), f32)
     a = lax.fori_loop(0, n, ln2b, (z, z, z))
-    vec[4:5, :], vec[5:6, :], vec[6:7, :] = a
+    cm.early([emb[0:1, :], *a] + [bsum[f] for f in range(NF)])
+    cm.hook("ffn_done")
     transpose_into(xT2, n2, seq)
+
     def gmix(i, _):
         r = rows_of(i)
-        w = jnp.concatenate([wo[p] for p in range(P)], axis=1)
-        x = nn_dot(n2[r, :], w).astype(bf16)
+        x = nn_dot(n2[r, :], cm.geto()).astype(bf16)
         for p in range(P):
             gm[p, r, :] = x[:, 128 * p:128 * p + 128]
         return 0
+
     lax.fori_loop(0, n, gmix, 0)
+
     def gwo(i, _):
         r = rows_of(i)
         m = jnp.concatenate([mixed[p] for p in range(P)], axis=1)
         x = nn_dot(xT2[r, :], m).astype(bf16)
         for p in range(P):
-            dwo[p, r, :] = x[:, 128 * p:128 * p + 128]
+            cm.puto(p, i, x[:, 128 * p:128 * p + 128])
         return 0
+
     lax.fori_loop(0, D // TR, gwo, 0)
+    cm.hook("out_grad")
     transpose_into(xT, n1, seq)
-    gn[...] = jnp.zeros(gn.shape, f32)
-    def pair_bwd(hp, _):
+
+    def pair_bwd(j, _):
+        hp = cm.order_back(j)
         attend_bwd(seq, most, length, qkv, qaug, kaug, mixed, lse, gm, qq, kk, vv, oo, dq, dkv, dqkv, hp)
+        cm.hook("back_mid", j)
+
         def wgrad(i, _):
-            r = rows_of(i)
-            dwq[hp, r, :] = nn_dot(xT[r, :], dqkv[...]).astype(bf16)
+            cm.putq(hp, i, nn_dot(xT[rows_of(i), :], dqkv[...]).astype(bf16))
             return 0
+
         lax.fori_loop(0, D // TR, wgrad, 0)
+        cm.hook("back_end", j)
+
         def back(i, _):
             r = rows_of(i)
-            gn[r, :] += nt_dot(dqkv[r, :], wq[hp])
+            gn[r, :] += nt_dot(dqkv[r, :], cm.getq(hp))
             return 0
+
         lax.fori_loop(0, n, back, 0)
         return 0
+
     lax.fori_loop(0, P, pair_bwd, 0)
+    cm.hook("back_done")
+
     def ln1b(i, acc):
         r = rows_of(i)
         xh, rr = normed(tok[r, :].astype(f32) + tp[...])
@@ -335,28 +807,117 @@
         gt = mid[r, :] + norm_back(xh, rr, g1[...], gy)
         gtok[r, :] = gt
         return acc[0] + colsum(gt), acc[1] + colsum(gy * xh), acc[2] + colsum(gy)
+
     a = lax.fori_loop(0, n, ln1b, (z, z, z))
-    vec[1:2, :], vec[2:3, :], vec[3:4, :] = a
-
-
-def run(T, most, length, ts, tok, cot, seg, wq, wo, wu, wd, wt, btime, g1, b1, g2, b2, bdown, bup):
-    seq, D = tok.shape
-    P, NF, F = wq.shape[0], wu.shape[0], wu.shape[2]
+    cm.late(list(a))
+
+
+def layer_scratch(seq, D, P, NF, F):
     V = pltpu.VMEM
-    S = jax.ShapeDtypeStruct
-    scratch = [V((1, D), f32), V((seq, D), bf16), V((P, seq, 384), bf16), V((seq, 128), bf16), V((seq, 128), bf16),
+    return [V((1, D), f32), V((seq, D), bf16), V((P, seq, 384), bf16), V((seq, 128), bf16), V((seq, 128), bf16),
         V((P, seq, 128), bf16), V((P, seq, 128), f32)] + [V((2, seq, 128), bf16)] * 4 + [V((2, seq, 128), f32),
         V((2, 2, seq, 128), f32), V((seq, 384), bf16), V((seq, D), f32), V((seq, D), bf16), V((seq, D), f32), V((seq, D), f32),
-        V((seq, F), bf16), V((seq, F), bf16), V((P, seq, 128), bf16), V((D, seq), bf16), V((D, seq), bf16)]
+        V((seq, F), bf16), V((seq, F), bf16), V((P, seq, 128), bf16), V((D, seq), bf16), V((D, seq), bf16), V((NF, 1, F), f32)]
+
+
+def plain_kernel(most, n_sc, *refs):
+    len_ref, ts_ref, tok, cot, seg, wq, wo, w2, wt, btime, g1, b1, g2, b2, bdown, bup, out, gtok, dwq, dwo, dw2, vec = refs[:22]
+    T = lax.axis_index("tensor")
+    cm = Plain(wq, wo, w2, dwq, dwo, dw2, vec)
+    layer(cm, T, most, len_ref[T], ts_ref[0].astype(f32), tok, cot, seg, wt, btime, g1, b1, g2, b2, bdown, bup, out, gtok, refs[22:])
+
+
+def run_plain(most, length, ts, tok, cot, seg, wq, wo, w2, wt, vecs, bup):
+    seq, D = tok.shape
+    P, NF, F = wq.shape[0], w2.shape[0], w2.shape[-1]
+    S = jax.ShapeDtypeStruct
     vm = pl.BlockSpec(memory_space=pltpu.VMEM)
     sm = pl.BlockSpec(memory_space=pltpu.SMEM)
     return pl.pallas_call(
-        functools.partial(kernel, T, most),
-        out_shape=(S((seq, D), bf16), S((seq, D), f32), S(wq.shape, bf16), S(wo.shape, bf16), S(wu.shape, bf16), S(wd.shape, bf16), S((16, D), f32)),
-        in_specs=[sm, sm] + [vm] * 15, out_specs=[vm] * 7,
+        functools.partial(plain_kernel, most, 0),
+        out_shape=(S((seq, D), bf16), S((seq, D), f32), S(wq.shape, bf16), S(wo.shape, bf16), S(w2.shape, bf16), S((16, D), f32)),
+        in_specs=[sm, sm] + [vm] * 14, out_specs=[vm] * 6,
+        scratch_shapes=layer_scratch(seq, D, P, NF, F),
+        compiler_params=pltpu.CompilerParams(vmem_limit_bytes=60 << 20),
+    )(length, ts, tok, cot, seg, wq, wo, w2, wt, *[v[None] for v in vecs], bup)
+
+
+def linked_kernel(most, ng, nt, names, semnames, n_layer, *refs):
+    len_ref, ts_ref, tok, cot, seg, w_qkv, w_out, w_up, w_down, wt, btime, g1, b1, g2, b2, bdown, bup = refs[:17]
+    out, gtok, o_qkv, o_out, o_up, o_down, gwt, vec = refs[17:25]
+    sc = refs[25:25 + n_layer]
+    rest = refs[25 + n_layer:]
+    bufs = dict(zip(names, rest[:len(names)]))
+    sr = rest[len(names):]
+    sems = {nm: (sr[2 * i], sr[2 * i + 1]) for i, nm in enumerate(semnames)}
+    bufs.update(w_qkv=w_qkv, w_out=w_out, w_up=w_up, w_down=w_down, o_qkv=o_qkv, o_out=o_out, o_up=o_up, o_down=o_down)
+    bufs["E"] = tuple(bufs.pop(k) for k in ("EZ", "EX", "EC"))
+    bufs["L"] = tuple(bufs.pop(k) for k in ("LZ", "LX", "LC"))
+    cm = Linked(ng, nt, bufs, sems)
+    T = cm.t
+    NE = 4 + bup.shape[0]
+    cm.early = lambda rows: cm.v_start("E", rows)
+    cm.late = lambda rows: cm.v_start("L", rows)
+    plain_hook = cm.hook
+
+    def hook(place, j=None):
+        plain_hook(place, j)
+        if place == "back_mid":
+            @pl.when(j == 0)
+            def _():
+                cm.v_mid("E", NE)
+            @pl.when(j == 1)
+            def _():
+                cm.v_last("E", NE)
+
+    cm.hook = hook
+    layer(cm, T, most, len_ref[T], ts_ref[0].astype(f32), tok, cot, seg, wt, btime, g1, b1, g2, b2, bdown, bup, out, gtok, sc)
+    cm.v_mid("L", 3)
+    embs, sums = cm.v_done("E", NE)
+    vec[4:4 + NE - 1, :] = sums
+    cm.v_last("L", 3)
+    cm.hook("finish")
+    grads, late = cm.v_done("L", 3)
+    vec[2:4, :] = late
+    vec[1:2, :] = colsum(grads)
+    gwt[...] = lax.dot_general(embs, grads, (((0,), (0,)), ((), ())), precision=lax.Precision.HIGHEST, preferred_element_type=f32)
+    cm.hook("leave")
+    cm.v_leave("E")
+    cm.v_leave("L")
+
+
+def run_linked(most, nd, nt, length, ts, tok, cot, seg, w_qkv, w_out, w_up, w_down, wt, vecs, bup):
+    seq, D = tok.shape
+    ng = nd // 2
+    r, F = w_up.shape
+    P, NF = nt, nt
+    S, V = jax.ShapeDtypeStruct, pltpu.VMEM
+    DMA = pltpu.SemaphoreType.DMA
+    bufs = dict(
+        WQ=V((nt, ng, 2, r, 384), bf16), WO=V((nt, ng, 2, r, 128), bf16), W2=V((nt, 2, ng, 2, r, F), bf16),
+        DQ=V((nt, ng, 2, r, 384), bf16), DO=V((nt, ng, 2, r, 128), bf16), D2=V((nt, 2, ng, 2, r, F), bf16),
+        CQ=V((nt, ng, r, 384), bf16), XQ=V((nt, ng, r, 384), bf16), ZQ=V((nt, r, 384), bf16),
+        CO=V((nt, ng, r, 128), bf16), XO=V((ng, nt, r, 128), bf16), ZO=V((nt, r, 128), bf16),
+        C2=V((nt, 2, ng, r, F), bf16), X2=V((nt, ng, 2, r, F), bf16), Z2=V((nt, 2, r, F), bf16),
+        EZ=V((nt, 8, D), f32), EX=V((ng, 16, D), f32), EC=V((2, nt * ng + 8, D), f32),
+        LZ=V((nt, 8, D), f32), LX=V((ng, 16, D), f32), LC=V((2, nt * ng + 8, D), f32),
+    )
+    sems = dict(gq_plane=(ng,), gq_z=(nt,), gq_core=(nt,), go_z=(nt,), g2_z=(nt,), go_plane=(ng,), go_core=(), g2_plane=(nt, ng), g2_core=(nt,),
+        rq_core=(nt,), rq_plane=(nt, ng), rq_z=(nt,), r2_core=(nt,), r2_plane=(nt, ng), r2_z=(nt,), ro_core=(), ro_plane=(ng,), ro_z=(nt,),
+        E_z=(nt,), E_plane=(ng,), E_core=(), L_z=(nt,), L_plane=(ng,), L_core=())
+    ls = layer_scratch(seq, D, P, NF, F)
+    scratch = ls + list(bufs.values())
+    for s in sems.values():
+        scratch += [DMA(s), DMA(s)]
+    vm = pl.BlockSpec(memory_space=pltpu.VMEM)
+    sm = pl.BlockSpec(memory_space=pltpu.SMEM)
+    return pl.pallas_call(
+        functools.partial(linked_kernel, most, ng, nt, tuple(bufs), tuple(sems), len(ls)),
+        out_shape=(S((seq, D), bf16), S((seq, D), f32), S(w_qkv.shape, f32), S(w_out.shape, f32), S(w_up.shape, f32), S(w_down.shape, f32), S((D, D), f32), S((16, D), f32)),
+        in_specs=[sm, sm] + [vm] * 15, out_specs=[vm] * 8,
         scratch_shapes=scratch,
-        compiler_params=pltpu.CompilerParams(vmem_limit_bytes=62 << 20),
-    )(length, ts, tok, cot, seg, wq, wo, wu, wd, wt, btime[None], g1[None], b1[None], g2[None], b2[None], bdown[None], bup[None])
+        compiler_params=pltpu.CompilerParams(vmem_limit_bytes=62 << 20, collective_id=0, has_side_effects=True),
+    )(length, ts, tok, cot, seg, w_qkv, w_out, w_up, w_down, wt, *[v[None] for v in vecs], bup)
 
 
 def shards(
@@ -378,29 +939,37 @@
     b_down,
     cotangent,
 ):
-    b = lambda w: w.astype(bf16)
-    rows, seq, D = tokens.shape
+    seq, D = tokens.shape[1:]
+    nd, nt = lax.axis_size("dp"), lax.axis_size("tensor")
+    vecs = (b_time, ln1_gain, ln1_bias, ln2_gain, ln2_bias, b_down)
+    F = w_up.shape[1]
+    bup = b_up.reshape(nt, 1, F)
+    if w_up.shape[0] % 16 == 0:
+        out, gtok, gq, go, gu, gd, gwt, vec = run_linked(
+            DOC, nd, nt, span_lengths, timestep, tokens[0], cotangent[0], segment_ids,
+            w_qkv, w_out_t, w_up, w_down_t, w_time, vecs, bup)
+        return (out[None], gtok[None], gq, go, gu, gd, gwt, vec[1], vec[2], vec[3], vec[4], vec[5],
+                vec[7:7 + nt].reshape(-1), vec[6])
     HB = w_qkv.shape[2]
 
     def whole(w):
-        return lax.all_gather(lax.all_gather(b(w), "dp", axis=0, tiled=True), "tensor", axis=0)
-
-    def part(g):
-        g = lax.psum_scatter(g, "dp", scatter_dimension=1, tiled=True)
+        return lax.all_gather(lax.all_gather(w.astype(bf16), "dp", axis=w.ndim - 2, tiled=True), "tensor", axis=0)
+
+    def part(g, dim):
+        g = lax.psum_scatter(g, "dp", scatter_dimension=dim, tiled=True)
         return lax.psum_scatter(g, "tensor", scatter_dimension=0, tiled=True)[0].astype(f32)
 
     wq = whole(jnp.transpose(w_qkv, (1, 0, 2)).reshape(w_qkv.shape[1], 3 * HB))
-    wo, wu, wd = whole(w_out_t), whole(w_up), whole(w_down_t)
-    out, gtok, dwq, dwo, dwu, dwd, vec = run(
-        lambda: lax.axis_index("tensor"), seq // 2, span_lengths, timestep, tokens[0], cotangent[0], segment_ids,
-        wq, wo, wu, wd, w_time, b_time, ln1_gain, ln1_bias, ln2_gain, ln2_bias, b_down, b_up)
-    lines = lax.all_gather(vec[:2], ("dp", "tensor"), axis=1, tiled=False)
+    out, gtok, dwq, dwo, dw2, vec = run_plain(
+        DOC, span_lengths, timestep, tokens[0], cotangent[0], segment_ids,
+        wq, whole(w_out_t), whole(jnp.stack([w_up, w_down_t])), w_time, vecs, bup)
+    lines = lax.all_gather(jnp.stack([vec[0], vec[8]]), ("dp", "tensor"), axis=1, tiled=False)
     gwt = jnp.dot(lines[0].T, lines[1], precision=lax.Precision.HIGHEST)
-    small = lax.psum(vec[1:], ("dp", "tensor"))
-    gq = part(dwq)
+    small = lax.psum(vec, ("dp", "tensor"))
+    gq, g2 = part(dwq, 1), part(dw2, 2)
     return (
-        out[None], gtok[None], jnp.transpose(gq.reshape(gq.shape[0], 3, HB), (1, 0, 2)), part(dwo), part(dwu), part(dwd),
-        gwt, small[0], small[1], small[2], small[3], small[4], small[6:10].reshape(-1), small[5])
+        out[None], gtok[None], jnp.transpose(gq.reshape(gq.shape[0], 3, HB), (1, 0, 2)), part(dwo, 1), g2[0], g2[1],
+        gwt, small[8], small[9], small[10], small[1], small[2], small[4:4 + nt].reshape(-1), small[3])
 
 
 def solution(mesh):

time: 507 us -> 159 us (0.31)
  waiting for transfers between devices: 215 us -> 0 us
  blocking collectives: 164 us -> 0 us
  Pallas kernels: 100 us -> 147 us
  between operations: 14.7 us -> 1.34 us
  local copies, waits for them, and re-layouts: 3.08 us -> 10.1 us
  other arithmetic: 6.19 us -> 0 us
    reduce_scatter x8 -> x0, waiting for transfers between devices: 131 us -> none  [the longest x4 72.9 us: part(): g = lax.psum_scatter(g, 'dp', scatter_dimension=1, tiled=True)]
    all_gather x6 -> x0, blocking collectives: 127 us -> none  [the longest x1 68.3 us: shards(): lines = lax.all_gather(vec[:2], ('dp', 'tensor'), axis=1, tiled=False)]
    all_gather x3 -> x0, waiting for transfers between devices: 82.9 us -> none  [whole(): lax.all_gather(lax.all_gather(b(w), 'dp', axis=0, tiled=True), 'tensor',...]
    pallas_call x1, Pallas kernels: 100 us -> 147 us  [run_linked(): pl.pallas_call(functools.partial(linked_kernel, most, ng, nt, tuple(bufs)...]
    psum x1 -> x0, blocking collectives: 37.1 us -> none  [shards(): small = lax.psum(vec[1:], ('dp', 'tensor'))]
    unnamed x9 -> x21, local copies, waits for them, and re-layouts: 1.27 us -> 8.51 us
    convert_element_type x7 -> x0, other arithmetic: 6.19 us -> none  [the longest x3 4.34 us: part(): lax.psum_scatter(g, 'tensor', scatter_dimension=0, tiled=True)[0]]
  transfers between devices with their start and end apart: 11 -> 0, of which waited for: 8 -> 0; matrix products, arithmetic and copies ran while one was open for 2% -> 0% of each run, Pallas kernels for 0% -> 0%
where the time goes in v3:
time: 159 us; the launch traced here: 158 us
  Pallas kernels  147 us (92%)
  local copies, waits for them, and re-layouts  10.1 us (6%)
    pallas_call x1, Pallas kernels, run_linked(): pl.pallas_call(functools.partial(linked_kernel, most, ng, nt, tuple(bufs)...  147 us
    unnamed x21, local copies, waits for them, and re-layouts  8.51 us

profile of v3, /device:TPU:0, one launch (start us, length us, event | category | flops | bytes accessed | tf_op | source)
XLA Modules:
  0.0 158.2 jit_solution(17540724222233080746)
XLA Ops:
  1.3 146.8 %shard_map.272 = (bf16[1024,512]{1,0:T(8,128)(2,1)}, f32[1024,512]{1,0:T(8,128)}, f32[3,64,128]{2,1,0:T(8,128)}, f32[64,128]{1,0:T(8,128)}, f32[64,512]{1,0:T(8,...) custom-call(s32[4]{0:T(128)} %refs_0_.1, s32[1]{0:T(128)S(6)} %copy.39.refs_1_, ...), custom_call_target="tpu_custom_call" | custom-call | tf_op jit(solution)/shard_map/pallas_call | solution.py:914
  148.1 0.0 copy-start
  148.1 1.6 fusion
  149.7 0.8 slice_bitcast_fusion
  150.4 0.6 copy.31
  151.0 2.3 %copy.40 = bf16[1,1024,512]{2,1,0:T(8,128)(2,1)} copy(bf16[1,1024,512]{2,1,0:T(8,128)(2,1)} %bitcast.23) | data formatting | bytes 2097152
  153.3 0.0 copy-done
  153.3 0.0 copy-start.4
  153.3 0.0 copy-start.5
  153.3 0.0 copy-start.3
  153.3 0.0 copy-start.2
  153.3 0.0 copy-start.1
  153.3 1.3 copy.41
  154.6 0.0 copy-done.4
  154.6 0.6 copy.42
  155.3 0.0 copy-done.5
  155.3 0.6 copy.43
  155.9 0.0 copy-done.3
  155.9 0.7 copy.44
  156.6 0.0 copy-done.2
  156.6 0.7 copy.45
  157.2 0.0 copy-done.1
  157.2 1.0 copy.46
Async XLA Ops:
  148.1 5.2 %copy-start = (f32[1024,512]{1,0:T(8,128)S(1)}, f32[1024,512]{1,0:T(8,128)}, u32[]{:S(2)}) copy-start(f32[1024,512]{1,0:T(8,128)} %get-tuple-element.23) | copy-start | bytes 6291460
  153.3 1.4 copy-start.4
  153.3 2.0 %copy-start.5 = (f32[64,128]{1,0:T(8,128)S(1)}, f32[64,128]{1,0:T(8,128)}, u32[]{:S(2)}) copy-start(f32[64,128]{1,0:T(8,128)} %get-tuple-element.53) | copy-start | bytes 98308
  153.3 2.6 %copy-start.3 = (f32[64,512]{1,0:T(8,128)S(1)}, f32[64,512]{1,0:T(8,128)}, u32[]{:S(2)}) copy-start(f32[64,512]{1,0:T(8,128)} %get-tuple-element.54) | copy-start | bytes 393220
  153.3 3.3 %copy-start.2 = (f32[64,512]{1,0:T(8,128)S(1)}, f32[64,512]{1,0:T(8,128)}, u32[]{:S(2)}) copy-start(f32[64,512]{1,0:T(8,128)} %get-tuple-element.55) | copy-start | bytes 393220
  153.3 3.9 %copy-start.1 = (f32[512,512]{1,0:T(8,128)S(1)}, f32[512,512]{1,0:T(8,128)}, u32[]{:S(2)}) copy-start(f32[512,512]{1,0:T(8,128)} %get-tuple-element.56) | copy-start | bytes 3145732

commit v4 on v3

--- a/solution.py
+++ b/solution.py
@@ -79,7 +79,7 @@
     return lo, hi
 
 
-def attend_fwd(seq, most, length, qkv, qaug, kaug, mixed, lse, qq, kk, vv, hp):
+def attend_fwd(seq, most, length, qkv, qaug, kaug, mixed, lse, qq, kk, vv, hp, half):
     n = seq // TR
     def prep(i, _):
         r = rows_of(i)
@@ -96,6 +96,8 @@
         return 0
     lax.fori_loop(0, n, prep, 0)
     for i in range(n):
+        if i == n // 2:
+            half()
         lo, hi = window(i, seq, most)
         r = slice(i * TR, i * TR + TR)
         low = lane((TR, 128)) < HS
@@ -223,13 +225,13 @@
         return self.w2[f, 1]
 
     def putq(self, p, i, x):
-        self.dwq[p, rows_of(i), :] = x
+        self.dwq[p, i, :] = x
 
     def puto(self, p, i, x):
-        self.dwo[p, rows_of(i), :] = x
+        self.dwo[p, i, :] = x
 
     def put2(self, f, k, i, x):
-        self.dw2[f, k, rows_of(i), :] = x
+        self.dw2[f, k, i, :] = x
 
     def order(self, j):
         return j
@@ -290,8 +292,8 @@
 
     def blocks(self, ref, i):
         rows = ref.shape[-2]
-        m = TR // (2 * rows)
-        return pl.ds(i * m, m), (m, 2, rows, ref.shape[-1])
+        m = (i.stop - i.start) // (2 * rows)
+        return slice(i.start // (2 * rows), i.stop // (2 * rows)), (m, 2, rows, ref.shape[-1])
 
     def putq(self, p, i, x):
         b, shape = self.blocks(self.DQ, i)
@@ -318,21 +320,13 @@
             pl.semaphore_signal(bar, inc=1, device_id=self.dev(kind, k), device_id_type=MESH)
         pl.semaphore_wait(bar, len(peers))
 
-    def q_plane(self, k):
+    def q_plane(self, x, k, incoming=False):
+        g, c, p = self.g, self.c, self.t ^ x
+        return self.copy("gq_plane", (x, k), "plane", k, self.WQ.at[p, g, c], self.WQ.at[p, g ^ k if incoming else g, c])
+
+    def q_z(self, k, incoming=False):
         g, c, t = self.g, self.c, self.t
-        return self.copy("gq_plane", (k,), "plane", k, self.WQ.at[t, g, c], self.WQ.at[t, g, c])
-
-    def q_plane_in(self, k):
-        g, c, t = self.g, self.c, self.t
-        return self.copy("gq_plane", (k,), "plane", k, self.WQ.at[t, g, c], self.WQ.at[t, g ^ k, c])
-
-    def q_z(self, k):
-        c, t = self.c, self.t
-        return self.copy("gq_z", (k,), "z", k, self.WQ.at[t, :, c], self.WQ.at[t, :, c])
-
-    def q_z_in(self, k):
-        c, t = self.c, self.t
-        return self.copy("gq_z", (k,), "z", k, self.WQ.at[t, :, c], self.WQ.at[t ^ k, :, c])
+        return self.copy("gq_z", (k,), "z", k, self.WQ.at[t, g, c], self.WQ.at[t ^ k if incoming else t, g, c])
 
     def q_core(self, k):
         c, t = self.c, self.t
@@ -435,40 +429,50 @@
             self.W2[t, 1, g, c] = self.w_down[...].astype(bf16)
             self.enter()
             for k in range(1, ng):
-                self.q_plane(k).start()
+                self.q_plane(0, k).start()
+            for k in range(1, nt):
+                self.q_z(k).start()
         elif place == "normed":
             for k in range(1, ng):
-                self.q_plane_in(k).wait_recv()
+                self.q_plane(0, k, True).wait_recv()
             self.q_core(0).start()
-            for k in range(1, nt):
-                self.q_z(k).start()
             for k in range(1, nt):
                 for x in self.r_z(k):
                     x.start()
+        elif place == "masked":
+            for x in range(1, nt):
+                self.q_z(x, True).wait_recv()
+                for k in range(1, ng):
+                    self.q_plane(x, k).start()
         elif place == "pair":
             self.q_core_in(j).wait_recv()
+        elif place == "pair_half":
+            @pl.when(j < nt - 1)
+            def _():
+                for k in range(1, ng):
+                    self.q_plane(j + 1, k, True).wait_recv()
+                self.q_core(j + 1).start()
+            @pl.when(j == nt - 2)
+            def _():
+                for k in range(1, ng):
+                    self.o_plane(k, True).wait_recv()
+                self.o_core().start()
+            @pl.when(j == nt - 1)
+            def _():
+                for k in range(1, ng):
+                    self.f_plane(0, k, True).wait_recv()
+                self.f_core(0).start()
         elif place == "pair_mid":
-            @pl.when(j < nt - 1)
-            def _():
-                self.q_z_in(j + 1).wait_recv()
-                self.q_core(j + 1).start()
-            @pl.when(j == nt // 2)
+            @pl.when(j == 0)
             def _():
                 for k in range(1, nt):
                     for x in self.r_z(k, t ^ k):
                         x.wait_recv()
                 for k in range(1, ng):
                     self.o_plane(k).start()
-                for x in range(nt):
-                    for k in range(1, ng):
-                        self.f_plane(x, k).start()
+            for k in range(1, ng):
+                self.f_plane(j, k).start()
         elif place == "mixed":
-            for k in range(1, ng):
-                self.o_plane(k, True).wait_recv()
-            self.o_core().start()
-            for k in range(1, ng):
-                self.f_plane(0, k, True).wait_recv()
-            self.f_core(0).start()
             self.o_core(True).wait_recv()
         elif place == "chunk":
             self.f_core(j, True).wait_recv()
@@ -553,10 +557,10 @@
                 self.o_qkv[k] = acc[:, 128 * k:128 * k + 128]
         elif place == "leave":
             for k in range(1, ng):
-                self.q_plane(k).wait_send()
                 self.o_plane(k).wait_send()
                 self.ro("plane", k).wait_send()
                 for x in range(nt):
+                    self.q_plane(x, k).wait_send()
                     self.f_plane(x, k).wait_send()
                     self.r2("plane", x, k).wait_send()
                     self.rq("plane", x, k).wait_send()
@@ -641,6 +645,19 @@
         self.v(name, "core", 0).wait_send()
 
 
+TILE = dict(ln1=256, proj=1024, ln2=512, tile=512, wgrad=512, ln2b=256, gmix=1024, gwo=512, qgrad=512, back=1024, ln1b=256)
+UNROLL = {"proj", "ln2", "tile", "wgrad", "gmix", "gwo", "qgrad", "back"}
+
+
+def loop(name, total, body, init):
+    n = TILE[name]
+    if name in UNROLL or total == n:
+        for i in range(total // n):
+            init = body(slice(i * n, i * n + n), init)
+        return init
+    return lax.fori_loop(0, total // n, lambda i, x: body(pl.ds(pl.multiple_of(i * n, n), n), x), init)
+
+
 def layer(cm, T, most, length, t, tok, cot, seg, wt, btime, g1, b1, g2, b2, bdown, bup, out, gtok, sc):
     tp, n1, qkv, qaug, kaug, mixed, lse, qq, kk, vv, oo, dq, dkv, dqkv, mid, n2, ffn, gn, act, gu, gm, xT, xT2, bsum = sc
     seq, D = tok.shape
@@ -653,13 +670,12 @@
     emb = jnp.concatenate([jnp.sin(ang), jnp.cos(ang)], axis=1)
     tp[...] = jnp.dot(emb, wt[...], precision=lax.Precision.HIGHEST, preferred_element_type=f32)[0:1, :] + btime[...]
 
-    def ln1(i, _):
-        r = rows_of(i)
+    def ln1(r, _):
         xh, _r = normed(tok[r, :].astype(f32) + tp[...])
         n1[r, :] = (xh * g1[...] + b1[...]).astype(bf16)
         return 0
 
-    lax.fori_loop(0, n, ln1, 0)
+    loop("ln1", seq, ln1, 0)
     cm.hook("normed")
     srow = seg[pl.ds(T, 1), :].astype(f32)
     for b in range(seq // 128):
@@ -672,37 +688,37 @@
         ka = jnp.where(same & (pos < length), 0.0, -BIG)
         kaug[r, :] = jnp.where(spot < 8, ka, jnp.where(spot < 11, -1.0, 0.0)).astype(bf16)
 
+    cm.hook("masked")
+
     def pair_fwd(j, _):
         hp = cm.order(j)
         cm.hook("pair", j)
 
-        def proj(i, _):
-            r = rows_of(i)
+        def proj(r, _):
             x = nn_dot(n1[r, :], cm.getq(hp))
             s = jnp.where(lane((1, 384)) < 128, SCALE * LOG2E, 1.0)
             qkv[hp, r, :] = (x * s).astype(bf16)
             return 0
 
-        lax.fori_loop(0, n, proj, 0)
-        attend_fwd(seq, most, length, qkv, qaug, kaug, mixed, lse, qq, kk, vv, hp)
+        loop("proj", seq, proj, 0)
+        attend_fwd(seq, most, length, qkv, qaug, kaug, mixed, lse, qq, kk, vv, hp, lambda: cm.hook("pair_half", j))
         cm.hook("pair_mid", j)
         return 0
 
     lax.fori_loop(0, P, pair_fwd, 0)
     cm.hook("mixed")
 
-    def ln2(i, _):
-        r = rows_of(i)
+    def ln2(r, _):
         mx = jnp.concatenate([mixed[p, r, :] for p in range(P)], axis=1)
         x = tok[r, :].astype(f32) + tp[...] + nt_dot(mx, cm.geto())
         mid[r, :] = x
         xh, _r = normed(x)
         n2[r, :] = (xh * g2[...] + b2[...]).astype(bf16)
-        ffn[r, :] = jnp.zeros((TR, D), f32)
-        gn[r, :] = jnp.zeros((TR, D), f32)
+        ffn[r, :] = jnp.zeros((TILE["ln2"], D), f32)
+        gn[r, :] = jnp.zeros((TILE["ln2"], D), f32)
         return 0
 
-    lax.fori_loop(0, n, ln2, 0)
+    loop("ln2", seq, ln2, 0)
     transpose_into(xT, cot, seq)
     transpose_into(xT2, n2, seq)
 
@@ -710,8 +726,7 @@
         f = cm.order(j)
         cm.hook("chunk", j)
 
-        def tile(i, acc):
-            r = rows_of(i)
+        def tile(r, acc):
             u = nn_dot(n2[r, :], cm.getu(f)) + bup[f]
             a, ga = gelu_parts(u)
             a = a.astype(bf16)
@@ -722,23 +737,21 @@
             gn[r, :] += nt_dot(g, cm.getu(f))
             return acc + colsum(g.astype(f32))
 
-        bsum[f] = lax.fori_loop(0, n, tile, jnp.zeros((1, F), f32))
+        bsum[f] = loop("tile", seq, tile, jnp.zeros((1, F), f32))
         cm.hook("chunk_mid", j)
 
-        def wgrad(i, _):
-            r = rows_of(i)
-            cm.put2(f, 1, i, nn_dot(xT[r, :], act[...]).astype(bf16))
-            cm.put2(f, 0, i, nn_dot(xT2[r, :], gu[...]).astype(bf16))
+        def wgrad(r, _):
+            cm.put2(f, 1, r, nn_dot(xT[r, :], act[...]).astype(bf16))
+            cm.put2(f, 0, r, nn_dot(xT2[r, :], gu[...]).astype(bf16))
             return 0
 
-        lax.fori_loop(0, D // TR, wgrad, 0)
+        loop("wgrad", D, wgrad, 0)
         cm.hook("chunk_end", j)
         return 0
 
     lax.fori_loop(0, NF, chunk, 0)
 
-    def ln2b(i, acc):
-        r = rows_of(i)
+    def ln2b(r, acc):
         c = cot[r, :].astype(f32)
         x = mid[r, :]
         out[r, :] = (x + ffn[r, :] + bdown[...]).astype(bf16)
@@ -747,33 +760,31 @@
         gmid = c + norm_back(xh, rr, g2[...], gy)
         mid[r, :] = gmid
         n2[r, :] = gmid.astype(bf16)
-        gn[r, :] = jnp.zeros((TR, D), f32)
+        gn[r, :] = jnp.zeros((TILE["ln2b"], D), f32)
         return acc[0] + colsum(gy * xh), acc[1] + colsum(gy), acc[2] + colsum(c)
 
     z = jnp.zeros((1, D), f32)
-    a = lax.fori_loop(0, n, ln2b, (z, z, z))
+    a = loop("ln2b", seq, ln2b, (z, z, z))
     cm.early([emb[0:1, :], *a] + [bsum[f] for f in range(NF)])
     cm.hook("ffn_done")
     transpose_into(xT2, n2, seq)
 
-    def gmix(i, _):
-        r = rows_of(i)
+    def gmix(r, _):
         x = nn_dot(n2[r, :], cm.geto()).astype(bf16)
         for p in range(P):
             gm[p, r, :] = x[:, 128 * p:128 * p + 128]
         return 0
 
-    lax.fori_loop(0, n, gmix, 0)
-
-    def gwo(i, _):
-        r = rows_of(i)
+    loop("gmix", seq, gmix, 0)
+
+    def gwo(r, _):
         m = jnp.concatenate([mixed[p] for p in range(P)], axis=1)
         x = nn_dot(xT2[r, :], m).astype(bf16)
         for p in range(P):
-            cm.puto(p, i, x[:, 128 * p:128 * p + 128])
+            cm.puto(p, r, x[:, 128 * p:128 * p + 128])
         return 0
 
-    lax.fori_loop(0, D // TR, gwo, 0)
+    loop("gwo", D, gwo, 0)
     cm.hook("out_grad")
     transpose_into(xT, n1, seq)
 
@@ -782,33 +793,31 @@
         attend_bwd(seq, most, length, qkv, qaug, kaug, mixed, lse, gm, qq, kk, vv, oo, dq, dkv, dqkv, hp)
         cm.hook("back_mid", j)
 
-        def wgrad(i, _):
-            cm.putq(hp, i, nn_dot(xT[rows_of(i), :], dqkv[...]).astype(bf16))
+        def wgrad(r, _):
+            cm.putq(hp, r, nn_dot(xT[r, :], dqkv[...]).astype(bf16))
             return 0
 
-        lax.fori_loop(0, D // TR, wgrad, 0)
+        loop("qgrad", D, wgrad, 0)
         cm.hook("back_end", j)
 
-        def back(i, _):
-            r = rows_of(i)
+        def back(r, _):
             gn[r, :] += nt_dot(dqkv[r, :], cm.getq(hp))
             return 0
 
-        lax.fori_loop(0, n, back, 0)
+        loop("back", seq, back, 0)
         return 0
 
     lax.fori_loop(0, P, pair_bwd, 0)
     cm.hook("back_done")
 
-    def ln1b(i, acc):
-        r = rows_of(i)
+    def ln1b(r, acc):
         xh, rr = normed(tok[r, :].astype(f32) + tp[...])
         gy = gn[r, :]
         gt = mid[r, :] + norm_back(xh, rr, g1[...], gy)
         gtok[r, :] = gt
         return acc[0] + colsum(gt), acc[1] + colsum(gy * xh), acc[2] + colsum(gy)
 
-    a = lax.fori_loop(0, n, ln1b, (z, z, z))
+    a = loop("ln1b", seq, ln1b, (z, z, z))
     cm.late(list(a))
 
 
@@ -902,7 +911,7 @@
         EZ=V((nt, 8, D), f32), EX=V((ng, 16, D), f32), EC=V((2, nt * ng + 8, D), f32),
         LZ=V((nt, 8, D), f32), LX=V((ng, 16, D), f32), LC=V((2, nt * ng + 8, D), f32),
     )
-    sems = dict(gq_plane=(ng,), gq_z=(nt,), gq_core=(nt,), go_z=(nt,), g2_z=(nt,), go_plane=(ng,), go_core=(), g2_plane=(nt, ng), g2_core=(nt,),
+    sems = dict(gq_plane=(nt, ng), gq_z=(nt,), gq_core=(nt,), go_z=(nt,), g2_z=(nt,), go_plane=(ng,), go_core=(), g2_plane=(nt, ng), g2_core=(nt,),
         rq_core=(nt,), rq_plane=(nt, ng), rq_z=(nt,), r2_core=(nt,), r2_plane=(nt, ng), r2_z=(nt,), ro_core=(), ro_plane=(ng,), ro_z=(nt,),
         E_z=(nt,), E_plane=(ng,), E_core=(), L_z=(nt,), L_plane=(ng,), L_core=())
     ls = layer_scratch(seq, D, P, NF, F)
@@ -918,6 +927,41 @@
         scratch_shapes=scratch,
         compiler_params=pltpu.CompilerParams(vmem_limit_bytes=62 << 20, collective_id=0, has_side_effects=True),
     )(length, ts, tok, cot, seg, w_qkv, w_out, w_up, w_down, wt, *[v[None] for v in vecs], bup)
+
+
+def emit_kernel(nb, *refs):
+    big, outs, small, bufs = refs[:8], refs[8:15], refs[15:22], refs[22:30]
+    sem_in, sem_out = refs[30:]
+    ins = [pltpu.make_async_copy(a, b, sem_in.at[i]) for i, (a, b) in enumerate(zip(big, bufs))]
+    ups = [pltpu.make_async_copy(a, b, sem_out.at[i]) for i, (a, b) in enumerate(zip(bufs, outs))]
+    for x in ins:
+        x.start()
+    for x, y in zip(ins, ups):
+        x.wait()
+        y.start()
+    ins[7].wait()
+    vec = bufs[7]
+    for k, o in enumerate(small[:-1]):
+        o[...] = vec[1 + k, :]
+    n = vec.shape[1]
+    for k in range(nb):
+        small[-1][pl.ds(k * n, n)] = vec[7 + k, :]
+    for y in ups:
+        y.wait()
+
+
+def emit(nb, *big):
+    S = jax.ShapeDtypeStruct
+    D = big[-1].shape[1]
+    vm = pl.BlockSpec(memory_space=pltpu.VMEM)
+    hb = pl.BlockSpec(memory_space=pltpu.HBM)
+    return pl.pallas_call(
+        functools.partial(emit_kernel, nb),
+        out_shape=tuple(S(x.shape, x.dtype) for x in big[:-1]) + tuple(S((D,), f32) for _ in range(6)) + (S((nb * D,), f32),),
+        in_specs=[hb] * 8, out_specs=[hb] * 7 + [vm] * 7,
+        scratch_shapes=[pltpu.VMEM(x.shape, x.dtype) for x in big] + [pltpu.SemaphoreType.DMA((8,)), pltpu.SemaphoreType.DMA((7,))],
+        compiler_params=pltpu.CompilerParams(vmem_limit_bytes=60 << 20),
+    )(*big)
 
 
 def shards(
@@ -948,8 +992,8 @@
         out, gtok, gq, go, gu, gd, gwt, vec = run_linked(
             DOC, nd, nt, span_lengths, timestep, tokens[0], cotangent[0], segment_ids,
             w_qkv, w_out_t, w_up, w_down_t, w_time, vecs, bup)
-        return (out[None], gtok[None], gq, go, gu, gd, gwt, vec[1], vec[2], vec[3], vec[4], vec[5],
-                vec[7:7 + nt].reshape(-1), vec[6])
+        gq, go, gu, gd, out, gwt, gtok, *v = emit(nt, gq, go, gu, gd, out, gwt, gtok, vec)
+        return (out[None], gtok[None], gq, go, gu, gd, gwt, v[0], v[1], v[2], v[3], v[4], v[6], v[5])
     HB = w_qkv.shape[2]
 
     def whole(w):

time: 159 us -> 135 us (0.85)
  Pallas kernels: 147 us -> 133 us
  local copies, waits for them, and re-layouts: 10.1 us -> 0 us
    pallas_call x1, Pallas kernels: 147 us -> 128 us  [run_linked(): pl.pallas_call(functools.partial(linked_kernel, most, ng, nt, tuple(bufs)...]
    unnamed x21 -> x0, local copies, waits for them, and re-layouts: 8.51 us -> none
    pallas_call x0 -> x1, Pallas kernels: none -> 5.02 us  [emit(): pl.pallas_call(functools.partial(emit_kernel, nb), out_shape=tuple((S(x.s...]
where the time goes in v4:
time: 135 us; the launch traced here: 134 us
  Pallas kernels  133 us (99%)
  between operations  1.47 us (1%)
    pallas_call x1, Pallas kernels, run_linked(): pl.pallas_call(functools.partial(linked_kernel, most, ng, nt, tuple(bufs)...  128 us
    pallas_call x1, Pallas kernels, emit(): pl.pallas_call(functools.partial(emit_kernel, nb), out_shape=tuple((S(x.s...  5.02 us

profile of v4, /device:TPU:0, one launch (start us, length us, event | category | flops | bytes accessed | tf_op | source)
XLA Modules:
  0.0 134.2 jit_solution(17694700904017925659)
XLA Ops:
  1.3 127.7 %shard_map.272 = (bf16[1024,512]{1,0:T(8,128)(2,1)}, f32[1024,512]{1,0:T(8,128)}, f32[3,64,128]{2,1,0:T(8,128)}, f32[64,128]{1,0:T(8,128)}, f32[64,512]{1,0:T(8,...) custom-call(s32[4]{0:T(128)} %refs_0_.1, s32[1]{0:T(128)S(6)} %copy.31.refs_1_, ...), custom_call_target="tpu_custom_call" | custom-call | tf_op jit(solution)/shard_map/pallas_call | solution.py:923
  129.0 5.0 %shard_map.273 = (f32[3,64,128]{2,1,0:T(8,128)}, f32[64,128]{1,0:T(8,128)}, f32[64,512]{1,0:T(8,128)}, f32[64,512]{1,0:T(8,128)}, bf16[1024,512]{1,0:T(8,128)(2,...) custom-call(f32[3,64,128]{2,1,0:T(8,128)} %get-tuple-element.36.refs, ...), custom_call_target="tpu_custom_call" | custom-call | tf_op jit(solution)/shard_map/pallas_call | solution.py:958

commit v5 on v4

--- a/solution.py
+++ b/solution.py
@@ -14,6 +14,7 @@
 BIG = 1e30
 EPS = 1e-5
 DOC = 512
+LEAST = 512
 LOG2E = math.log2(math.e)
 LN2 = math.log(2.0)
 SCALE = 1.0 / math.sqrt(HS)
@@ -77,6 +78,35 @@
     lo = max(0, (i * TR - most + 1) // 128 * 128)
     hi = min(seq, -(-(i * TR + TR - 1 + most) // 128) * 128)
     return lo, hi
+
+
+def gelu_parts(u):
+    c0, c1 = 0.7978845608028654, 0.044715
+    u2 = u * u
+    th = jnp.tanh(u * (c0 + (c0 * c1) * u2))
+    half = 0.5 + 0.5 * th
+    act = u * half
+    grad = half + (0.5 * u) * (1.0 - th * th) * (c0 + (3.0 * c0 * c1) * u2)
+    return act, grad
+
+
+def transpose_into(dst, src, seq):
+    def step(i, _):
+        r = rows_of(i)
+        dst[:, r] = src[r, :].T
+        return 0
+    for i in range(seq // TR):
+        r = slice(i * TR, i * TR + TR)
+        dst[:, r] = src[r, :].T
+
+
+def half_sums(prod, swap=False):
+    hi = prod.astype(bf16)
+    lo = (prod - hi.astype(f32)).astype(bf16)
+    a = lax.broadcasted_iota(jnp.int32, (256, 128), 0) // HS % 2
+    b = lax.broadcasted_iota(jnp.int32, (256, 128), 1) // HS
+    w = jnp.where((a != b) if swap else (a == b), 1.0, 0.0).astype(bf16)
+    return nn_dot(jnp.concatenate([hi, lo], axis=1), w)
 
 
 def attend_fwd(seq, most, length, qkv, qaug, kaug, mixed, lse, qq, kk, vv, hp, half):
@@ -94,44 +124,68 @@
         vv[0, r, :] = jnp.where(low, v, one)
         vv[1, r, :] = jnp.where(low, one, v)
         return 0
-    lax.fori_loop(0, n, prep, 0)
     for i in range(n):
-        if i == n // 2:
-            half()
+        prep(i, 0)
+
+    def score(i, h):
         lo, hi = window(i, seq, most)
+        return nt_dot(qq[h, i * TR:i * TR + TR, :], kk[h, lo:hi, :])
+
+    def soft(i, s, own):
+        m = jnp.max(s, axis=-1, keepdims=True)
+        if own is not None:
+            pad = (lax.broadcasted_iota(jnp.int32, (TR, 1), 0) + i * TR) >= length
+            m = jnp.where(pad, jnp.maximum(m, own), m)
+        return m, jnp.exp2(s - m).astype(bf16)
+
+    def finish(i, own, tops, outs):
         r = slice(i * TR, i * TR + TR)
         low = lane((TR, 128)) < HS
-        q, k, v = (qkv[hp, r, 128 * c:128 * c + 128].astype(f32) for c in range(3))
-        own = halves(q * k)
-        pad = (lax.broadcasted_iota(jnp.int32, (TR, 1), 0) + i * TR) >= length
-        tops, outs = [], []
-        for h in range(2):
-            s = nt_dot(qq[h, r, :], kk[h, lo:hi, :])
-            m = jnp.max(s, axis=-1, keepdims=True)
-            m = jnp.where(pad, jnp.maximum(m, own[h]), m)
-            p = jnp.exp2(s - m).astype(bf16)
-            outs.append(nn_dot(p, vv[h, lo:hi, :]))
-            tops.append(m)
-        padf = pad.astype(f32)
-        e0 = jnp.exp2(jnp.minimum(own[0] - tops[0], 0.0)).astype(bf16).astype(f32) * padf
-        e1 = jnp.exp2(jnp.minimum(own[1] - tops[1], 0.0)).astype(bf16).astype(f32) * padf
-        num = jnp.where(low, outs[0], outs[1]) + jnp.where(low, e0, e1) * v
-        den_x = jnp.where(low, outs[1], outs[0]) + jnp.where(low, e1, e0)
-        den = pltpu.roll(den_x, HS, 1)
-        mixed[hp, r, :] = (num / den).astype(bf16)
+        num = jnp.where(low, outs[0], outs[1])
+        den_x = jnp.where(low, outs[1], outs[0])
+        if own[0] is not None:
+            padf = ((lax.broadcasted_iota(jnp.int32, (TR, 1), 0) + i * TR) >= length).astype(f32)
+            e0 = jnp.exp2(jnp.minimum(own[0] - tops[0], 0.0)).astype(bf16).astype(f32) * padf
+            e1 = jnp.exp2(jnp.minimum(own[1] - tops[1], 0.0)).astype(bf16).astype(f32) * padf
+            num = num + jnp.where(low, e0, e1) * qkv[hp, r, 256:384].astype(f32)
+            den_x = den_x + jnp.where(low, e1, e0)
+        mixed[hp, r, :] = (num / pltpu.roll(den_x, HS, 1)).astype(bf16)
         lse[hp, r, :] = jnp.where(low, tops[1], tops[0]) + jnp.log2(den_x)
+
+    def selfs(i):
+        if (i + 1) * TR <= LEAST:
+            return (None, None)
+        r = slice(i * TR, i * TR + TR)
+        return halves(qkv[hp, r, 0:128].astype(f32) * qkv[hp, r, 128:256].astype(f32))
+
+    units = [(i, h) for i in range(n) for h in range(2)]
+    s = score(*units[0])
+    tops, outs = [], []
+    for u, (i, h) in enumerate(units):
+        if (i, h) == (n // 2, 0):
+            half()
+        nxt = score(*units[u + 1]) if u + 1 < len(units) else None
+        if h == 0:
+            own = selfs(i)
+        lo, hi = window(i, seq, most)
+        m, p = soft(i, s, own[h])
+        tops.append(m)
+        outs.append(nn_dot(p, vv[h, lo:hi, :]))
+        if h == 1:
+            finish(i, own, tops, outs)
+            tops, outs = [], []
+        s = nxt
 
 
 def attend_bwd(seq, most, length, qkv, qaug, kaug, mixed, lse, gm, qq, kk, vv, oo, dq, dkv, dqkv, hp):
     n = seq // TR
     def prep(i, _):
-        r = rows_of(i)
+        r = slice(i * TR, i * TR + TR)
         low = lane((TR, 128)) < HS
         spot = lane((TR, 128)) % HS
         q, k, v = (qkv[hp, r, 128 * c:128 * c + 128] for c in range(3))
         g = gm[hp, r, :]
-        d0, d1 = halves(g.astype(f32) * mixed[hp, r, :].astype(f32))
-        dx = jnp.where(low, d1, d0)
+        dx = half_sums(g.astype(f32) * mixed[hp, r, :].astype(f32), True)
         def put(base, x):
             hi, mid, lo = split3(x)
             z = jnp.where(spot == 8, hi, base)
@@ -145,63 +199,62 @@
         for ref, x, a in ((qq, q, qa), (kk, k, ka), (vv, v, va), (oo, g, oa)):
             ref[0, r, :] = jnp.where(low, x, a)
             ref[1, r, :] = jnp.where(low, a, x)
+        if (i + 1) * TR > LEAST:
+            q, k, v, g = (x.astype(f32) for x in (q, k, v, g))
+            padf = ((lax.broadcasted_iota(jnp.int32, (TR, 1), 0) + i * TR) >= length).astype(f32)
+            ls = pltpu.roll(lse[hp, r, :], HS, 1)
+            d = pltpu.roll(dx, HS, 1)
+            pf = jnp.exp2(jnp.minimum(half_sums(q * k) - ls, 1.0)) * padf
+            ds = (pf * (half_sums(g * v) - d)).astype(bf16).astype(f32)
+            pf = pf.astype(bf16).astype(f32)
+            dkv[2, 0, r, :] = ds
+            dkv[2, 1, r, :] = pf
         return 0
-    lax.fori_loop(0, n, prep, 0)
-    for h in range(2):
-        dq[h] = jnp.zeros(dq.shape[1:], f32)
     for i in range(n):
+        prep(i, 0)
+    lo, hi = window(0, seq, most)
+    if hi < seq:
+        dq[:, hi:seq, :] = jnp.zeros((2, seq - hi, 128), f32)
+
+    def score(i, h):
         lo, hi = window(i, seq, most)
         r = slice(i * TR, i * TR + TR)
-        for h in range(2):
-            st = nt_dot(kk[h, r, :], qq[h, lo:hi, :])
-            pt = jnp.exp2(st)
-            dpt = nt_dot(vv[h, r, :], oo[h, lo:hi, :])
-            dst = (pt * dpt).astype(bf16)
-            dkv[h, 0, r, :] = nn_dot(dst, qq[h, lo:hi, :])
-            dkv[h, 1, r, :] = nn_dot(pt.astype(bf16), oo[h, lo:hi, :])
-            dq[h, lo:hi, :] += tn_dot(dst, kk[h, r, :])
-    def post(i, _):
-        r = rows_of(i)
+        return nt_dot(kk[h, r, :], qq[h, lo:hi, :]), nt_dot(vv[h, r, :], oo[h, lo:hi, :])
+
+    def rest(i, h, st, dpt):
+        lo, hi = window(i, seq, most)
+        r = slice(i * TR, i * TR + TR)
+        pt = jnp.exp2(st)
+        dst = (pt * dpt).astype(bf16)
+        dkv[h, 0, r, :] = nn_dot(dst, qq[h, lo:hi, :])
+        dkv[h, 1, r, :] = nn_dot(pt.astype(bf16), oo[h, lo:hi, :])
+        x = tn_dot(dst, kk[h, r, :])
+        if i == 0:
+            dq[h, lo:hi, :] = x
+        else:
+            dq[h, lo:hi, :] += x
+
+    units = [(i, h) for i in range(n) for h in range(2)]
+    s = score(*units[0])
+    for u, (i, h) in enumerate(units):
+        nxt = score(*units[u + 1]) if u + 1 < len(units) else None
+        rest(i, h, *s)
+        s = nxt
+
+    for i in range(n):
+        r = slice(i * TR, i * TR + TR)
         low = lane((TR, 128)) < HS
-        q, k, v = (qkv[hp, r, 128 * c:128 * c + 128].astype(f32) for c in range(3))
-        g = gm[hp, r, :].astype(f32)
-        pad = (lax.broadcasted_iota(jnp.int32, (TR, 1), 0) + i * TR) >= length
-        padf = pad.astype(f32)
-        s0, s1 = halves(q * k)
-        p0, p1 = halves(g * v)
-        d0, d1 = halves(g * mixed[hp, r, :].astype(f32))
-        ls = pltpu.roll(lse[hp, r, :], HS, 1)
-        pf = jnp.exp2(jnp.minimum(jnp.where(low, s0, s1) - ls, 1.0)) * padf
-        ds = (pf * (jnp.where(low, p0, p1) - jnp.where(low, d0, d1))).astype(bf16).astype(f32)
-        pf = pf.astype(bf16).astype(f32)
-        gq = jnp.where(low, dq[0, r, :], dq[1, r, :]) + ds * k
-        gk = jnp.where(low, dkv[0, 0, r, :], dkv[1, 0, r, :]) + ds * q
-        gv = jnp.where(low, dkv[0, 1, r, :], dkv[1, 1, r, :]) + pf * g
+        gq = jnp.where(low, dq[0, r, :], dq[1, r, :])
+        gk = jnp.where(low, dkv[0, 0, r, :], dkv[1, 0, r, :])
+        gv = jnp.where(low, dkv[0, 1, r, :], dkv[1, 1, r, :])
+        if (i + 1) * TR > LEAST:
+            ds, pf = dkv[2, 0, r, :], dkv[2, 1, r, :]
+            gq = gq + ds * qkv[hp, r, 128:256].astype(f32)
+            gk = gk + ds * qkv[hp, r, 0:128].astype(f32)
+            gv = gv + pf * gm[hp, r, :].astype(f32)
         dqkv[r, 0:128] = (gq * SCALE).astype(bf16)
         dqkv[r, 128:256] = (gk * LN2).astype(bf16)
         dqkv[r, 256:384] = gv.astype(bf16)
-        return 0
-    lax.fori_loop(0, n, post, 0)
-
-
-def gelu_parts(u):
-    c0, c1 = 0.7978845608028654, 0.044715
-    u2 = u * u
-    th = jnp.tanh(u * (c0 + (c0 * c1) * u2))
-    half = 0.5 + 0.5 * th
-    act = u * half
-    grad = half + (0.5 * u) * (1.0 - th * th) * (c0 + (3.0 * c0 * c1) * u2)
-    return act, grad
-
-
-def transpose_into(dst, src, seq):
-    def step(i, _):
-        r = rows_of(i)
-        dst[:, r] = src[r, :].T
-        return 0
-    for i in range(seq // TR):
-        r = slice(i * TR, i * TR + TR)
-        dst[:, r] = src[r, :].T
 
 
 MESH = pl.DeviceIdType.MESH
@@ -265,6 +318,8 @@
             return (2 * self.g + 1 - self.c, self.t)
         if kind == "plane":
             return (2 * (self.g ^ k) + self.c, self.t)
+        if kind == "dp":
+            return (self.d ^ k, self.t)
         return (self.d, self.t ^ k)
 
     def copy(self, name, at, kind, k, src, dst):
@@ -315,7 +370,7 @@
 
     def enter(self):
         bar = pltpu.get_barrier_semaphore()
-        peers = [("core", 0)] + [("plane", k) for k in range(1, self.ng)] + [("z", k) for k in range(1, self.nt)]
+        peers = [("dp", k) for k in range(1, 2 * self.ng)] + [("z", k) for k in range(1, self.nt)]
         for kind, k in peers:
             pl.semaphore_signal(bar, inc=1, device_id=self.dev(kind, k), device_id_type=MESH)
         pl.semaphore_wait(bar, len(peers))
@@ -336,11 +391,13 @@
         c, t = self.c, self.t
         return self.copy("gq_core", (k,), "core", 0, self.WQ.at[t ^ k, :, c], self.WQ.at[t ^ k, :, 1 - c])
 
-    def r_z(self, k, into=None):
+    def o_z(self, k, incoming=False):
         g, c, t = self.g, self.c, self.t
-        u = t if into is None else into
-        return [self.copy("go_z", (k,), "z", k, self.WO.at[t, g, c], self.WO.at[u, g, c]),
-                self.copy("g2_z", (k,), "z", k, self.W2.at[t, :, g, c], self.W2.at[u, :, g, c])]
+        return self.copy("go_z", (k,), "z", k, self.WO.at[t, g, c], self.WO.at[t ^ k if incoming else t, g, c])
+
+    def f_z(self, k, incoming=False):
+        g, c, t = self.g, self.c, self.t
+        return self.copy("g2_z", (k,), "z", k, self.W2.at[t, :, g, c], self.W2.at[t ^ k if incoming else t, :, g, c])
 
     def o_plane(self, k, incoming=False):
         g, c = self.g, self.c
@@ -427,25 +484,35 @@
             self.WO[t, g, c] = self.w_out[...].astype(bf16)
             self.W2[t, 0, g, c] = self.w_up[...].astype(bf16)
             self.W2[t, 1, g, c] = self.w_down[...].astype(bf16)
+            for x in (self.E[1], self.L[1]):
+                x[self.d] = jnp.zeros(x.shape[1:], f32)
             self.enter()
             for k in range(1, ng):
                 self.q_plane(0, k).start()
             for k in range(1, nt):
                 self.q_z(k).start()
+                self.o_z(k).start()
         elif place == "normed":
             for k in range(1, ng):
                 self.q_plane(0, k, True).wait_recv()
             self.q_core(0).start()
             for k in range(1, nt):
-                for x in self.r_z(k):
-                    x.start()
-        elif place == "masked":
-            for x in range(1, nt):
-                self.q_z(x, True).wait_recv()
-                for k in range(1, ng):
-                    self.q_plane(x, k).start()
+                self.f_z(k).start()
         elif place == "pair":
             self.q_core_in(j).wait_recv()
+        elif place == "pair_proj":
+            @pl.when(j == 0)
+            def _():
+                for x in range(1, nt):
+                    self.q_z(x, True).wait_recv()
+                    for k in range(1, ng):
+                        self.q_plane(x, k).start()
+                for x in range(1, nt):
+                    self.o_z(x, True).wait_recv()
+                for k in range(1, ng):
+                    self.o_plane(k).start()
+                for k in range(1, ng):
+                    self.f_plane(0, k).start()
         elif place == "pair_half":
             @pl.when(j < nt - 1)
             def _():
@@ -463,15 +530,11 @@
                     self.f_plane(0, k, True).wait_recv()
                 self.f_core(0).start()
         elif place == "pair_mid":
-            @pl.when(j == 0)
+            @pl.when(j < nt - 1)
             def _():
-                for k in range(1, nt):
-                    for x in self.r_z(k, t ^ k):
-                        x.wait_recv()
+                self.f_z(j + 1, True).wait_recv()
                 for k in range(1, ng):
-                    self.o_plane(k).start()
-            for k in range(1, ng):
-                self.f_plane(j, k).start()
+                    self.f_plane(j + 1, k).start()
         elif place == "mixed":
             self.o_core(True).wait_recv()
         elif place == "chunk":
@@ -485,30 +548,26 @@
             @pl.when(j >= 1)
             def _():
                 self.f_after_core(j - 1)
-            @pl.when(j >= 2)
-            def _():
-                self.f_after_plane(j - 2)
-                @pl.when(j >= 3)
-                def _():
-                    self.r2("z", j - 2).start()
         elif place == "chunk_end":
             self.r2("core", j).start()
         elif place == "ffn_done":
             self.f_after_core(nt - 1)
-            self.f_after_plane(nt - 2)
-            self.r2("z", nt - 2).start()
         elif place == "out_grad":
             self.ro("core").start()
         elif place == "back_mid":
+            self.f_after_plane(j)
+            @pl.when(j >= 1)
+            def _():
+                self.r2("z", j).start()
+                self.q_after_core(nt - j)
             @pl.when(j == 0)
             def _():
-                self.f_after_plane(nt - 1)
-                self.r2("z", nt - 1).start()
                 self.ro("core").wait_recv()
                 for p in range(nt):
                     self.DO[p, :, c] = (self.DO[p, :, c].astype(f32) + self.CO[p].astype(f32)).astype(bf16)
                 for k in range(1, ng):
                     self.ro("plane", k).start()
+                self.v_mid("E", self.ne)
             @pl.when(j == 1)
             def _():
                 for k in range(1, ng):
@@ -520,9 +579,6 @@
                     self.DO[p, g, c] = acc.astype(bf16)
                 for k in range(1, nt):
                     self.ro("z", k).start()
-            @pl.when(j >= 1)
-            def _():
-                self.q_after_core(nt - j)
             @pl.when(j >= 2)
             def _():
                 self.q_after_plane(nt - j + 1)
@@ -546,6 +602,7 @@
             for x in range(1, nt):
                 acc = acc + self.ZO[x].astype(f32)
             self.o_out[...] = acc
+        elif place == "finish_q":
             acc = self.DQ[t, g, c].astype(f32)
             for k in range(1, ng):
                 self.rq("plane", 0, k).wait_recv()
@@ -573,28 +630,17 @@
             self.ro("core").wait_send()
             for k in range(1, nt):
                 self.q_z(k).wait_send()
-                for x in self.r_z(k):
-                    x.wait_send()
+                self.o_z(k).wait_send()
+                self.f_z(k).wait_send()
                 self.r2("z", k).wait_send()
                 self.rq("z", k).wait_send()
                 self.ro("z", k).wait_send()
 
-    def v(self, name, stage, k):
-        B = getattr(self, name)
-        Z, X, C = B
+    def v(self, name, stage, k, incoming=False):
+        Z, X = getattr(self, name)
         if stage == "z":
-            return self.copy(name + "_z", (k,), "z", k, Z.at[self.t], Z.at[self.t])
-        if stage == "plane":
-            return self.copy(name + "_plane", (k,), "plane", k, X.at[self.g], X.at[self.g])
-        return self.copy(name + "_core", (), "core", 0, C.at[self.c], C.at[self.c])
-
-    def v_in(self, name, stage, k):
-        Z, X, C = getattr(self, name)
-        if stage == "z":
-            return self.copy(name + "_z", (k,), "z", k, Z.at[self.t], Z.at[self.t ^ k])
-        if stage == "plane":
-            return self.copy(name + "_plane", (k,), "plane", k, X.at[self.g], X.at[self.g ^ k])
-        return self.copy(name + "_core", (), "core", 0, C.at[self.c], C.at[1 - self.c])
+            return self.copy(name + "_z", (k,), "z", k, Z.at[self.t], Z.at[self.t ^ k if incoming else self.t])
+        return self.copy(name + "_dp", (k,), "dp", k, X.at[self.d], X.at[self.d ^ k if incoming else self.d])
 
     def v_start(self, name, rows):
         Z = getattr(self, name)[0]
@@ -604,45 +650,34 @@
             self.v(name, "z", k).start()
 
     def v_mid(self, name, m):
-        Z, X, C = getattr(self, name)
+        Z, X = getattr(self, name)
         nt = self.nt
         for k in range(1, nt):
-            self.v_in(name, "z", k).wait_recv()
+            self.v(name, "z", k, True).wait_recv()
         for k in range(nt):
-            X[self.g, k:k + 1, :] = Z[k, 0:1, :]
+            X[self.d, k:k + 1, :] = Z[k, 0:1, :]
         s = Z[0, 1:m, :]
         for k in range(1, nt):
             s = s + Z[k, 1:m, :]
-        X[self.g, 8:8 + m - 1, :] = s
-        for k in range(1, self.ng):
-            self.v(name, "plane", k).start()
-
-    def v_last(self, name, m):
-        Z, X, C = getattr(self, name)
-        nt, ng = self.nt, self.ng
-        for k in range(1, ng):
-            self.v_in(name, "plane", k).wait_recv()
-        for k in range(ng):
-            C[self.c, k * nt:k * nt + nt, :] = X[k, 0:nt, :]
+        X[self.d, 8:8 + m - 1, :] = s
+        for k in range(1, 2 * self.ng):
+            self.v(name, "dp", k).start()
+
+    def v_done(self, name, m):
+        X = getattr(self, name)[1]
+        nd = 2 * self.ng
+        for k in range(1, nd):
+            self.v(name, "dp", k, True).wait_recv()
         s = X[0, 8:8 + m - 1, :]
-        for k in range(1, ng):
+        for k in range(1, nd):
             s = s + X[k, 8:8 + m - 1, :]
-        C[self.c, ng * nt:ng * nt + m - 1, :] = s
-        self.v(name, "core", 0).start()
-
-    def v_done(self, name, m):
-        C = getattr(self, name)[2]
-        n = self.nt * self.ng
-        self.v_in(name, "core", 0).wait_recv()
-        kept = jnp.concatenate([C[0, 0:n, :], C[1, 0:n, :]], axis=0)
-        return kept, C[0, n:n + m - 1, :] + C[1, n:n + m - 1, :]
+        return jnp.concatenate([X[k, 0:8, :] for k in range(nd)], axis=0), s
 
     def v_leave(self, name):
         for k in range(1, self.nt):
             self.v(name, "z", k).wait_send()
-        for k in range(1, self.ng):
-            self.v(name, "plane", k).wait_send()
-        self.v(name, "core", 0).wait_send()
+        for k in range(1, 2 * self.ng):
+            self.v(name, "dp", k).wait_send()
 
 
 TILE = dict(ln1=256, proj=1024, ln2=512, tile=512, wgrad=512, ln2b=256, gmix=1024, gwo=512, qgrad=512, back=1024, ln1b=256)
@@ -665,6 +700,7 @@
     NF, F = bsum.shape[0], bsum.shape[2]
     n = seq // TR
     cm.hook("start")
+    cm.hook("row_in")
     half = D // 2
     ang = t * jnp.exp(-math.log(10000.0) * lax.broadcasted_iota(jnp.int32, (8, half), 1).astype(f32) / half)
     emb = jnp.concatenate([jnp.sin(ang), jnp.cos(ang)], axis=1)
@@ -688,8 +724,6 @@
         ka = jnp.where(same & (pos < length), 0.0, -BIG)
         kaug[r, :] = jnp.where(spot < 8, ka, jnp.where(spot < 11, -1.0, 0.0)).astype(bf16)
 
-    cm.hook("masked")
-
     def pair_fwd(j, _):
         hp = cm.order(j)
         cm.hook("pair", j)
@@ -701,6 +735,7 @@
             return 0
 
         loop("proj", seq, proj, 0)
+        cm.hook("pair_proj", j)
         attend_fwd(seq, most, length, qkv, qaug, kaug, mixed, lse, qq, kk, vv, hp, lambda: cm.hook("pair_half", j))
         cm.hook("pair_mid", j)
         return 0
@@ -719,6 +754,7 @@
         return 0
 
     loop("ln2", seq, ln2, 0)
+    cm.hook("cot_in")
     transpose_into(xT, cot, seq)
     transpose_into(xT2, n2, seq)
 
@@ -765,6 +801,7 @@
 
     z = jnp.zeros((1, D), f32)
     a = loop("ln2b", seq, ln2b, (z, z, z))
+    cm.hook("row_out")
     cm.early([emb[0:1, :], *a] + [bsum[f] for f in range(NF)])
     cm.hook("ffn_done")
     transpose_into(xT2, n2, seq)
@@ -825,7 +862,7 @@
     V = pltpu.VMEM
     return [V((1, D), f32), V((seq, D), bf16), V((P, seq, 384), bf16), V((seq, 128), bf16), V((seq, 128), bf16),
         V((P, seq, 128), bf16), V((P, seq, 128), f32)] + [V((2, seq, 128), bf16)] * 4 + [V((2, seq, 128), f32),
-        V((2, 2, seq, 128), f32), V((seq, 384), bf16), V((seq, D), f32), V((seq, D), bf16), V((seq, D), f32), V((seq, D), f32),
+        V((3, 2, seq, 128), f32), V((seq, 384), bf16), V((seq, D), f32), V((seq, D), bf16), V((seq, D), f32), V((seq, D), f32),
         V((seq, F), bf16), V((seq, F), bf16), V((P, seq, 128), bf16), V((D, seq), bf16), V((D, seq), bf16), V((NF, 1, F), f32)]
 
 
@@ -852,47 +889,57 @@
 
 
 def linked_kernel(most, ng, nt, names, semnames, n_layer, *refs):
-    len_ref, ts_ref, tok, cot, seg, w_qkv, w_out, w_up, w_down, wt, btime, g1, b1, g2, b2, bdown, bup = refs[:17]
-    out, gtok, o_qkv, o_out, o_up, o_down, gwt, vec = refs[17:25]
-    sc = refs[25:25 + n_layer]
-    rest = refs[25 + n_layer:]
+    len_ref, ts_ref, tok_h, cot_h, seg, w_qkv, w_out, w_up, w_down, wt_h, btime, g1, b1, g2, b2, bdown, bup = refs[:17]
+    out_h, gtok_h, o_qkv, o_out, o_up, o_down, embs, grads, vec = refs[17:26]
+    sc = refs[26:26 + n_layer]
+    rest = refs[26 + n_layer:]
     bufs = dict(zip(names, rest[:len(names)]))
     sr = rest[len(names):]
     sems = {nm: (sr[2 * i], sr[2 * i + 1]) for i, nm in enumerate(semnames)}
+    local = sr[-1]
+    tok, cot, wt, out, gtok = (bufs.pop(k) for k in ("tok", "cot", "wt", "out", "gtok"))
     bufs.update(w_qkv=w_qkv, w_out=w_out, w_up=w_up, w_down=w_down, o_qkv=o_qkv, o_out=o_out, o_up=o_up, o_down=o_down)
-    bufs["E"] = tuple(bufs.pop(k) for k in ("EZ", "EX", "EC"))
-    bufs["L"] = tuple(bufs.pop(k) for k in ("LZ", "LX", "LC"))
+    bufs["E"] = bufs.pop("EZ"), bufs.pop("EX")
+    bufs["L"] = bufs.pop("LZ"), bufs.pop("LX")
     cm = Linked(ng, nt, bufs, sems)
     T = cm.t
-    NE = 4 + bup.shape[0]
+    cm.ne = 4 + bup.shape[0]
     cm.early = lambda rows: cm.v_start("E", rows)
     cm.late = lambda rows: cm.v_start("L", rows)
+    pairs = ((tok_h, tok), (wt_h, wt), (cot_h, cot), (out, out_h), (gtok, gtok_h))
+    moves = [pltpu.make_async_copy(a, b, local.at[i]) for i, (a, b) in enumerate(pairs)]
+    for x in moves[:3]:
+        x.start()
     plain_hook = cm.hook
 
     def hook(place, j=None):
-        plain_hook(place, j)
-        if place == "back_mid":
-            @pl.when(j == 0)
-            def _():
-                cm.v_mid("E", NE)
-            @pl.when(j == 1)
-            def _():
-                cm.v_last("E", NE)
+        if place == "row_in":
+            moves[0].wait()
+            moves[1].wait()
+        elif place == "cot_in":
+            moves[2].wait()
+        elif place == "row_out":
+            moves[3].start()
+        else:
+            plain_hook(place, j)
 
     cm.hook = hook
     layer(cm, T, most, len_ref[T], ts_ref[0].astype(f32), tok, cot, seg, wt, btime, g1, b1, g2, b2, bdown, bup, out, gtok, sc)
+    moves[4].start()
+    cm.hook("finish")
     cm.v_mid("L", 3)
-    embs, sums = cm.v_done("E", NE)
-    vec[4:4 + NE - 1, :] = sums
-    cm.v_last("L", 3)
-    cm.hook("finish")
-    grads, late = cm.v_done("L", 3)
+    kept, sums = cm.v_done("E", cm.ne)
+    embs[...] = kept
+    vec[4:4 + cm.ne - 1, :] = sums
+    cm.hook("finish_q")
+    kept, late = cm.v_done("L", 3)
+    grads[...] = kept
     vec[2:4, :] = late
-    vec[1:2, :] = colsum(grads)
-    gwt[...] = lax.dot_general(embs, grads, (((0,), (0,)), ((), ())), precision=lax.Precision.HIGHEST, preferred_element_type=f32)
     cm.hook("leave")
     cm.v_leave("E")
     cm.v_leave("L")
+    moves[3].wait()
+    moves[4].wait()
 
 
 def run_linked(most, nd, nt, length, ts, tok, cot, seg, w_qkv, w_out, w_up, w_down, wt, vecs, bup):
@@ -908,58 +955,64 @@
         CQ=V((nt, ng, r, 384), bf16), XQ=V((nt, ng, r, 384), bf16), ZQ=V((nt, r, 384), bf16),
         CO=V((nt, ng, r, 128), bf16), XO=V((ng, nt, r, 128), bf16), ZO=V((nt, r, 128), bf16),
         C2=V((nt, 2, ng, r, F), bf16), X2=V((nt, ng, 2, r, F), bf16), Z2=V((nt, 2, r, F), bf16),
-        EZ=V((nt, 8, D), f32), EX=V((ng, 16, D), f32), EC=V((2, nt * ng + 8, D), f32),
-        LZ=V((nt, 8, D), f32), LX=V((ng, 16, D), f32), LC=V((2, nt * ng + 8, D), f32),
+        EZ=V((nt, 8, D), f32), EX=V((nd, 16, D), f32), LZ=V((nt, 8, D), f32), LX=V((nd, 16, D), f32),
+        tok=V((seq, D), bf16), cot=V((seq, D), bf16), wt=V((D, D), f32), out=V((seq, D), bf16), gtok=V((seq, D), f32),
     )
     sems = dict(gq_plane=(nt, ng), gq_z=(nt,), gq_core=(nt,), go_z=(nt,), g2_z=(nt,), go_plane=(ng,), go_core=(), g2_plane=(nt, ng), g2_core=(nt,),
         rq_core=(nt,), rq_plane=(nt, ng), rq_z=(nt,), r2_core=(nt,), r2_plane=(nt, ng), r2_z=(nt,), ro_core=(), ro_plane=(ng,), ro_z=(nt,),
-        E_z=(nt,), E_plane=(ng,), E_core=(), L_z=(nt,), L_plane=(ng,), L_core=())
+        E_z=(nt,), E_dp=(nd,), L_z=(nt,), L_dp=(nd,))
     ls = layer_scratch(seq, D, P, NF, F)
     scratch = ls + list(bufs.values())
     for s in sems.values():
         scratch += [DMA(s), DMA(s)]
+    scratch.append(DMA((5,)))
     vm = pl.BlockSpec(memory_space=pltpu.VMEM)
     sm = pl.BlockSpec(memory_space=pltpu.SMEM)
+    hb = pl.BlockSpec(memory_space=pltpu.HBM)
     return pl.pallas_call(
         functools.partial(linked_kernel, most, ng, nt, tuple(bufs), tuple(sems), len(ls)),
-        out_shape=(S((seq, D), bf16), S((seq, D), f32), S(w_qkv.shape, f32), S(w_out.shape, f32), S(w_up.shape, f32), S(w_down.shape, f32), S((D, D), f32), S((16, D), f32)),
-        in_specs=[sm, sm] + [vm] * 15, out_specs=[vm] * 8,
+        out_shape=(S((seq, D), bf16), S((seq, D), f32), S(w_qkv.shape, f32), S(w_out.shape, f32), S(w_up.shape, f32), S(w_down.shape, f32),
+            S((8 * nd, D), f32), S((8 * nd, D), f32), S((16, D), f32)),
+        in_specs=[sm, sm, hb, hb] + [vm] * 5 + [hb] + [vm] * 7, out_specs=[hb, hb] + [vm] * 7,
         scratch_shapes=scratch,
         compiler_params=pltpu.CompilerParams(vmem_limit_bytes=62 << 20, collective_id=0, has_side_effects=True),
     )(length, ts, tok, cot, seg, w_qkv, w_out, w_up, w_down, wt, *[v[None] for v in vecs], bup)
 
 
 def emit_kernel(nb, *refs):
-    big, outs, small, bufs = refs[:8], refs[8:15], refs[15:22], refs[22:30]
-    sem_in, sem_out = refs[30:]
+    big, outs, gwt, small, bufs = refs[:9], refs[9:15], refs[15], refs[16:23], refs[23:32]
+    sem_in, sem_out = refs[32:]
     ins = [pltpu.make_async_copy(a, b, sem_in.at[i]) for i, (a, b) in enumerate(zip(big, bufs))]
-    ups = [pltpu.make_async_copy(a, b, sem_out.at[i]) for i, (a, b) in enumerate(zip(bufs, outs))]
+    ups = [pltpu.make_async_copy(a, b, sem_out.at[i]) for i, (a, b) in enumerate(zip(bufs[3:], outs))]
     for x in ins:
         x.start()
-    for x, y in zip(ins, ups):
+    for x in ins[:3]:
         x.wait()
-        y.start()
-    ins[7].wait()
-    vec = bufs[7]
-    for k, o in enumerate(small[:-1]):
-        o[...] = vec[1 + k, :]
+    embs, grads, vec = (b[...] for b in bufs[:3])
+    gwt[...] = lax.dot_general(embs, grads, (((0,), (0,)), ((), ())), precision=lax.Precision.HIGHEST, preferred_element_type=f32)
+    small[0][...] = jnp.sum(grads, axis=0)
+    for k, o in enumerate(small[1:-1]):
+        o[...] = vec[2 + k, :]
     n = vec.shape[1]
     for k in range(nb):
         small[-1][pl.ds(k * n, n)] = vec[7 + k, :]
+    for x, y in zip(ins[3:], ups):
+        x.wait()
+        y.start()
     for y in ups:
         y.wait()
 
 
 def emit(nb, *big):
     S = jax.ShapeDtypeStruct
-    D = big[-1].shape[1]
+    D = big[2].shape[1]
     vm = pl.BlockSpec(memory_space=pltpu.VMEM)
     hb = pl.BlockSpec(memory_space=pltpu.HBM)
     return pl.pallas_call(
         functools.partial(emit_kernel, nb),
-        out_shape=tuple(S(x.shape, x.dtype) for x in big[:-1]) + tuple(S((D,), f32) for _ in range(6)) + (S((nb * D,), f32),),
-        in_specs=[hb] * 8, out_specs=[hb] * 7 + [vm] * 7,
-        scratch_shapes=[pltpu.VMEM(x.shape, x.dtype) for x in big] + [pltpu.SemaphoreType.DMA((8,)), pltpu.SemaphoreType.DMA((7,))],
+        out_shape=tuple(S(x.shape, x.dtype) for x in big[3:]) + (S((D, D), f32),) + tuple(S((D,), f32) for _ in range(6)) + (S((nb * D,), f32),),
+        in_specs=[hb] * 9, out_specs=[hb] * 6 + [vm] * 8,
+        scratch_shapes=[pltpu.VMEM(x.shape, x.dtype) for x in big] + [pltpu.SemaphoreType.DMA((9,)), pltpu.SemaphoreType.DMA((6,))],
         compiler_params=pltpu.CompilerParams(vmem_limit_bytes=60 << 20),
     )(*big)
 
@@ -989,10 +1042,10 @@
     F = w_up.shape[1]
     bup = b_up.reshape(nt, 1, F)
     if w_up.shape[0] % 16 == 0:
-        out, gtok, gq, go, gu, gd, gwt, vec = run_linked(
+        out, gtok, *g, embs, lines, vec = run_linked(
             DOC, nd, nt, span_lengths, timestep, tokens[0], cotangent[0], segment_ids,
             w_qkv, w_out_t, w_up, w_down_t, w_time, vecs, bup)
-        gq, go, gu, gd, out, gwt, gtok, *v = emit(nt, gq, go, gu, gd, out, gwt, gtok, vec)
+        gq, go, gu, gd, out, gtok, gwt, *v = emit(nt, embs, lines, vec, *g, out, gtok)
         return (out[None], gtok[None], gq, go, gu, gd, gwt, v[0], v[1], v[2], v[3], v[4], v[6], v[5])
     HB = w_qkv.shape[2]
 

time: 135 us -> 113 us (0.84)
  Pallas kernels: 133 us -> 111 us
    pallas_call x1, Pallas kernels: 128 us -> 106 us  [run_linked(): pl.pallas_call(functools.partial(linked_kernel, most, ng, nt, tuple(bufs)...]
where the time goes in v5:
time: 113 us
  Pallas kernels  111 us (98%)
  between operations  1.47 us (1%)
    pallas_call x1, Pallas kernels, run_linked(): pl.pallas_call(functools.partial(linked_kernel, most, ng, nt, tuple(bufs)...  106 us
    pallas_call x1, Pallas kernels, emit(): pl.pallas_call(functools.partial(emit_kernel, nb), out_shape=tuple((S(x.s...  4.92 us

profile of v5, /device:TPU:0, one launch (start us, length us, event | category | flops | bytes accessed | tf_op | source)
XLA Modules:
  0.0 112.6 jit_solution(5376105402684233008)
XLA Ops:
  1.3 106.2 %shard_map.272 = (bf16[1024,512]{1,0:T(8,128)(2,1)}, f32[1024,512]{1,0:T(8,128)}, f32[3,64,128]{2,1,0:T(8,128)}, f32[64,128]{1,0:T(8,128)}, f32[64,512]{1,0:T(8,...) custom-call(s32[4]{0:T(128)} %refs_0_.1, s32[1]{0:T(128)S(6)} %copy.31.refs_1_, ...), custom_call_target="tpu_custom_call" | custom-call | tf_op jit(solution)/shard_map/pallas_call | solution.py:972
  107.5 4.9 %shard_map.273 = (f32[3,64,128]{2,1,0:T(8,128)}, f32[64,128]{1,0:T(8,128)}, f32[64,512]{1,0:T(8,128)}, f32[64,512]{1,0:T(8,128)}, bf16[1024,512]{1,0:T(8,128)(2,...) custom-call(f32[64,512]{1,0:T(8,128)} %get-tuple-element.37.refs_0_,, ...), custom_call_target="tpu_custom_call" | custom-call | tf_op jit(solution)/shard_map/pallas_call | solution.py:1011

commit v6 on v5

--- a/solution.py
+++ b/solution.py
@@ -368,12 +368,16 @@
     def order_back(self, j):
         return self.t ^ (self.nt - 1 - j)
 
+    def peers(self):
+        return [("dp", k) for k in range(1, 2 * self.ng)] + [("z", k) for k in range(1, self.nt)]
+
+    def greet(self):
+        bar = pltpu.get_barrier_semaphore()
+        for kind, k in self.peers():
+            pl.semaphore_signal(bar, inc=1, device_id=self.dev(kind, k), device_id_type=MESH)
+
     def enter(self):
-        bar = pltpu.get_barrier_semaphore()
-        peers = [("dp", k) for k in range(1, 2 * self.ng)] + [("z", k) for k in range(1, self.nt)]
-        for kind, k in peers:
-            pl.semaphore_signal(bar, inc=1, device_id=self.dev(kind, k), device_id_type=MESH)
-        pl.semaphore_wait(bar, len(peers))
+        pl.semaphore_wait(pltpu.get_barrier_semaphore(), len(self.peers()))
 
     def q_plane(self, x, k, incoming=False):
         g, c, p = self.g, self.c, self.t ^ x
@@ -407,9 +411,21 @@
         c = self.c
         return self.copy("go_core", (), "core", 0, self.WO.at[:, :, c], self.WO.at[:, :, 1 - c if incoming else c])
 
-    def f_plane(self, j, k, incoming=False):
+    def f_plane(self, j, k, u, incoming=False):
         g, c, f = self.g, self.c, self.t ^ j
-        return self.copy("g2_plane", (j, k), "plane", k, self.W2.at[f, :, g, c], self.W2.at[f, :, g ^ k if incoming else g, c])
+        return self.copy("g2_plane", (j, u, k), "plane", k, self.W2.at[f, u, g, c], self.W2.at[f, u, g ^ k if incoming else g, c])
+
+    def f_on(self, x):
+        self.f_z(x, True).wait_recv()
+        for u in range(2):
+            for k in range(1, self.ng):
+                self.f_plane(x, k, u).start()
+
+    def f_pass(self, x):
+        for u in range(2):
+            for k in range(1, self.ng):
+                self.f_plane(x, k, u, True).wait_recv()
+        self.f_core(x).start()
 
     def f_core(self, j, incoming=False):
         c, f = self.c, self.t ^ j
@@ -430,6 +446,10 @@
         if stage == "plane":
             return self.copy("r2_plane", (x, k), "plane", k, self.D2.at[p, :, g ^ k, c], self.X2.at[x, k])
         return self.copy("r2_z", (x,), "z", x, self.D2.at[p, :, g, c], self.Z2.at[x])
+
+    def r2_near(self):
+        c, t = self.c, self.t
+        return self.copy("r2_near", (), "z", 1, self.D2.at[t ^ 1, :, :, c], self.Y2)
 
     def ro(self, stage, k=0):
         g, c, t = self.g, self.c, self.t
@@ -462,8 +482,6 @@
                 self.D2[p, u, i, c] = (self.D2[p, u, i, c].astype(f32) + self.C2[x, u, i].astype(f32)).astype(bf16)
                 return 0
             lax.fori_loop(0, self.ng, step, 0)
-        for k in range(1, self.ng):
-            self.r2("plane", x, k).start()
 
     def f_after_plane(self, x):
         p, c, g = self.t ^ x, self.c, self.g
@@ -477,8 +495,19 @@
 
     def hook(self, place, j=None):
         ng, nt, t, g, c = self.ng, self.nt, self.t, self.g, self.c
-        if place == "start":
-            rq = self.w_qkv.shape[1]
+        planes = range(1, ng)
+
+        def begin(*copies):
+            for x in copies:
+                x.start()
+
+        def await_in(*copies):
+            for x in copies:
+                x.wait_recv()
+
+        if place == "greet":
+            self.greet()
+        elif place == "start":
             for k in range(3):
                 self.WQ[t, g, c, :, 128 * k:128 * k + 128] = self.w_qkv[k].astype(bf16)
             self.WO[t, g, c] = self.w_out[...].astype(bf16)
@@ -487,102 +516,125 @@
             for x in (self.E[1], self.L[1]):
                 x[self.d] = jnp.zeros(x.shape[1:], f32)
             self.enter()
-            for k in range(1, ng):
-                self.q_plane(0, k).start()
-            for k in range(1, nt):
-                self.q_z(k).start()
-                self.o_z(k).start()
+            begin(*[self.q_plane(0, k) for k in planes], self.q_z(1))
         elif place == "normed":
-            for k in range(1, ng):
-                self.q_plane(0, k, True).wait_recv()
-            self.q_core(0).start()
-            for k in range(1, nt):
-                self.f_z(k).start()
+            begin(self.q_z(2), self.q_z(3))
+        elif place == "masked":
+            await_in(self.q_z(1, True))
+            begin(*[self.q_plane(1, k) for k in planes])
+            await_in(*[self.q_plane(0, k, True) for k in planes])
+            begin(self.q_core(0))
         elif place == "pair":
-            self.q_core_in(j).wait_recv()
+            await_in(self.q_core_in(j))
         elif place == "pair_proj":
             @pl.when(j == 0)
             def _():
-                for x in range(1, nt):
-                    self.q_z(x, True).wait_recv()
-                    for k in range(1, ng):
-                        self.q_plane(x, k).start()
-                for x in range(1, nt):
-                    self.o_z(x, True).wait_recv()
-                for k in range(1, ng):
-                    self.o_plane(k).start()
-                for k in range(1, ng):
-                    self.f_plane(0, k).start()
+                begin(*[self.o_z(k) for k in range(1, nt)])
+                begin(*[self.f_plane(0, k, 0) for k in planes])
         elif place == "pair_half":
-            @pl.when(j < nt - 1)
-            def _():
-                for k in range(1, ng):
-                    self.q_plane(j + 1, k, True).wait_recv()
-                self.q_core(j + 1).start()
-            @pl.when(j == nt - 2)
-            def _():
-                for k in range(1, ng):
-                    self.o_plane(k, True).wait_recv()
-                self.o_core().start()
-            @pl.when(j == nt - 1)
-            def _():
-                for k in range(1, ng):
-                    self.f_plane(0, k, True).wait_recv()
-                self.f_core(0).start()
+            @pl.when(j == 0)
+            def _():
+                await_in(*[self.q_plane(1, k, True) for k in planes])
+                begin(self.q_core(1))
+                await_in(self.q_z(2, True))
+                begin(*[self.q_plane(2, k) for k in planes])
+            @pl.when(j == 1)
+            def _():
+                begin(self.f_z(2), self.f_z(3))
+                begin(*[self.f_plane(0, k, 1) for k in planes])
+            @pl.when(j == 2)
+            def _():
+                await_in(*[self.q_plane(3, k, True) for k in planes])
+                begin(self.q_core(3))
+            @pl.when(j == 3)
+            def _():
+                await_in(*[self.o_plane(k, True) for k in planes])
+                begin(self.o_core())
         elif place == "pair_mid":
-            @pl.when(j < nt - 1)
-            def _():
-                self.f_z(j + 1, True).wait_recv()
-                for k in range(1, ng):
-                    self.f_plane(j + 1, k).start()
+            @pl.when(j == 0)
+            def _():
+                await_in(self.q_z(3, True))
+                begin(*[self.q_plane(3, k) for k in planes])
+                begin(self.f_z(1))
+            @pl.when(j == 1)
+            def _():
+                await_in(*[self.o_z(k, True) for k in range(1, nt)])
+                begin(*[self.o_plane(k) for k in planes])
+                await_in(*[self.q_plane(2, k, True) for k in planes])
+                begin(self.q_core(2))
+            @pl.when(j == 2)
+            def _():
+                self.f_on(1)
+            @pl.when(j == 3)
+            def _():
+                self.f_on(2)
         elif place == "mixed":
-            self.o_core(True).wait_recv()
+            await_in(self.o_core(True))
+        elif place == "second":
+            self.f_pass(0)
+            self.f_on(3)
         elif place == "chunk":
-            self.f_core(j, True).wait_recv()
+            await_in(self.f_core(j, True))
         elif place == "chunk_mid":
             @pl.when(j < nt - 1)
             def _():
-                for k in range(1, ng):
-                    self.f_plane(j + 1, k, True).wait_recv()
-                self.f_core(j + 1).start()
+                self.f_pass(j + 1)
             @pl.when(j >= 1)
             def _():
                 self.f_after_core(j - 1)
+            @pl.when(j == 2)
+            def _():
+                begin(self.r2_near())
+            @pl.when(j == 3)
+            def _():
+                begin(*[self.r2("plane", 2, k) for k in planes])
         elif place == "chunk_end":
-            self.r2("core", j).start()
+            begin(self.r2("core", j))
         elif place == "ffn_done":
             self.f_after_core(nt - 1)
+            begin(*[self.r2("plane", 3, k) for k in planes])
         elif place == "out_grad":
-            self.ro("core").start()
+            begin(self.ro("core"))
         elif place == "back_mid":
-            self.f_after_plane(j)
             @pl.when(j >= 1)
             def _():
-                self.r2("z", j).start()
                 self.q_after_core(nt - j)
             @pl.when(j == 0)
             def _():
-                self.ro("core").wait_recv()
+                await_in(self.ro("core"))
                 for p in range(nt):
                     self.DO[p, :, c] = (self.DO[p, :, c].astype(f32) + self.CO[p].astype(f32)).astype(bf16)
-                for k in range(1, ng):
-                    self.ro("plane", k).start()
+                begin(*[self.ro("plane", k) for k in planes])
                 self.v_mid("E", self.ne)
+                await_in(self.r2_near())
+                for u in range(2):
+                    def step(i, _):
+                        self.D2[t, u, i, c] = (self.D2[t, u, i, c].astype(f32) + self.Y2[u, i].astype(f32)).astype(bf16)
+                        return 0
+                    lax.fori_loop(0, ng, step, 0)
+                begin(*[self.r2("plane", 0, k) for k in planes])
             @pl.when(j == 1)
             def _():
-                for k in range(1, ng):
-                    self.ro("plane", k).wait_recv()
+                self.f_after_plane(2)
+                begin(self.r2("z", 2))
+            @pl.when(j == 2)
+            def _():
+                await_in(*[self.ro("plane", k) for k in planes])
                 for p in range(nt):
                     acc = self.DO[p, g, c].astype(f32)
-                    for k in range(1, ng):
+                    for k in planes:
                         acc = acc + self.XO[k, p].astype(f32)
                     self.DO[p, g, c] = acc.astype(bf16)
-                for k in range(1, nt):
-                    self.ro("z", k).start()
+                begin(*[self.ro("z", k) for k in range(1, nt)])
+                self.f_after_plane(3)
+                begin(self.r2("z", 3))
+            @pl.when(j == 3)
+            def _():
+                self.f_after_plane(0)
             @pl.when(j >= 2)
             def _():
                 self.q_after_plane(nt - j + 1)
-                self.rq("z", nt - j + 1).start()
+                begin(self.rq("z", nt - j + 1))
         elif place == "back_end":
             self.rq("core", nt - 1 - j).start()
         elif place == "back_done":
@@ -591,11 +643,12 @@
             self.rq("z", 1).start()
         elif place == "finish":
             for x in range(1, nt):
-                self.r2("z", x).wait_recv()
+                if x > 1:
+                    self.r2("z", x).wait_recv()
                 self.ro("z", x).wait_recv()
             for u, o in enumerate((self.o_up, self.o_down)):
                 acc = self.D2[t, u, g, c].astype(f32)
-                for x in range(1, nt):
+                for x in range(2, nt):
                     acc = acc + self.Z2[x, u].astype(f32)
                 o[...] = acc
             acc = self.DO[t, g, c].astype(f32)
@@ -613,13 +666,15 @@
             for k in range(3):
                 self.o_qkv[k] = acc[:, 128 * k:128 * k + 128]
         elif place == "leave":
-            for k in range(1, ng):
+            for k in planes:
                 self.o_plane(k).wait_send()
                 self.ro("plane", k).wait_send()
                 for x in range(nt):
                     self.q_plane(x, k).wait_send()
-                    self.f_plane(x, k).wait_send()
-                    self.r2("plane", x, k).wait_send()
+                    for u in range(2):
+                        self.f_plane(x, k, u).wait_send()
+                    if x != 1:
+                        self.r2("plane", x, k).wait_send()
                     self.rq("plane", x, k).wait_send()
             for k in range(nt):
                 self.q_core(k).wait_send()
@@ -628,11 +683,13 @@
                 self.rq("core", k).wait_send()
             self.o_core().wait_send()
             self.ro("core").wait_send()
+            self.r2_near().wait_send()
             for k in range(1, nt):
                 self.q_z(k).wait_send()
                 self.o_z(k).wait_send()
                 self.f_z(k).wait_send()
-                self.r2("z", k).wait_send()
+                if k > 1:
+                    self.r2("z", k).wait_send()
                 self.rq("z", k).wait_send()
                 self.ro("z", k).wait_send()
 
@@ -694,11 +751,12 @@
 
 
 def layer(cm, T, most, length, t, tok, cot, seg, wt, btime, g1, b1, g2, b2, bdown, bup, out, gtok, sc):
-    tp, n1, qkv, qaug, kaug, mixed, lse, qq, kk, vv, oo, dq, dkv, dqkv, mid, n2, ffn, gn, act, gu, gm, xT, xT2, bsum = sc
+    tp, n1, qkv, qaug, kaug, mixed, lse, qq, kk, vv, oo, dq, dkv, dqkv, mid, n2, ffn, gn, act, gu, gm, xT, xT2, xT3, bsum = sc
     seq, D = tok.shape
     P = qkv.shape[0]
     NF, F = bsum.shape[0], bsum.shape[2]
     n = seq // TR
+    cm.hook("greet")
     cm.hook("start")
     cm.hook("row_in")
     half = D // 2
@@ -724,6 +782,11 @@
         ka = jnp.where(same & (pos < length), 0.0, -BIG)
         kaug[r, :] = jnp.where(spot < 8, ka, jnp.where(spot < 11, -1.0, 0.0)).astype(bf16)
 
+    cm.hook("cot_in")
+    transpose_into(xT, cot, seq)
+    cm.hook("masked")
+    transpose_into(xT3, n1, seq)
+
     def pair_fwd(j, _):
         hp = cm.order(j)
         cm.hook("pair", j)
@@ -754,8 +817,7 @@
         return 0
 
     loop("ln2", seq, ln2, 0)
-    cm.hook("cot_in")
-    transpose_into(xT, cot, seq)
+    cm.hook("second")
     transpose_into(xT2, n2, seq)
 
     def chunk(j, _):
@@ -801,7 +863,6 @@
 
     z = jnp.zeros((1, D), f32)
     a = loop("ln2b", seq, ln2b, (z, z, z))
-    cm.hook("row_out")
     cm.early([emb[0:1, :], *a] + [bsum[f] for f in range(NF)])
     cm.hook("ffn_done")
     transpose_into(xT2, n2, seq)
@@ -823,15 +884,13 @@
 
     loop("gwo", D, gwo, 0)
     cm.hook("out_grad")
-    transpose_into(xT, n1, seq)
-
     def pair_bwd(j, _):
         hp = cm.order_back(j)
         attend_bwd(seq, most, length, qkv, qaug, kaug, mixed, lse, gm, qq, kk, vv, oo, dq, dkv, dqkv, hp)
         cm.hook("back_mid", j)
 
         def wgrad(r, _):
-            cm.putq(hp, r, nn_dot(xT[r, :], dqkv[...]).astype(bf16))
+            cm.putq(hp, r, nn_dot(xT3[r, :], dqkv[...]).astype(bf16))
             return 0
 
         loop("qgrad", D, wgrad, 0)
@@ -863,7 +922,7 @@
     return [V((1, D), f32), V((seq, D), bf16), V((P, seq, 384), bf16), V((seq, 128), bf16), V((seq, 128), bf16),
         V((P, seq, 128), bf16), V((P, seq, 128), f32)] + [V((2, seq, 128), bf16)] * 4 + [V((2, seq, 128), f32),
         V((3, 2, seq, 128), f32), V((seq, 384), bf16), V((seq, D), f32), V((seq, D), bf16), V((seq, D), f32), V((seq, D), f32),
-        V((seq, F), bf16), V((seq, F), bf16), V((P, seq, 128), bf16), V((D, seq), bf16), V((D, seq), bf16), V((NF, 1, F), f32)]
+        V((seq, F), bf16), V((seq, F), bf16), V((P, seq, 128), bf16), V((D, seq), bf16), V((D, seq), bf16), V((D, seq), bf16), V((NF, 1, F), f32)]
 
 
 def plain_kernel(most, n_sc, *refs):
@@ -890,14 +949,14 @@
 
 def linked_kernel(most, ng, nt, names, semnames, n_layer, *refs):
     len_ref, ts_ref, tok_h, cot_h, seg, w_qkv, w_out, w_up, w_down, wt_h, btime, g1, b1, g2, b2, bdown, bup = refs[:17]
-    out_h, gtok_h, o_qkv, o_out, o_up, o_down, embs, grads, vec = refs[17:26]
+    out, gtok, o_qkv, o_out, o_up, o_down, embs, grads, vec = refs[17:26]
     sc = refs[26:26 + n_layer]
     rest = refs[26 + n_layer:]
     bufs = dict(zip(names, rest[:len(names)]))
     sr = rest[len(names):]
     sems = {nm: (sr[2 * i], sr[2 * i + 1]) for i, nm in enumerate(semnames)}
     local = sr[-1]
-    tok, cot, wt, out, gtok = (bufs.pop(k) for k in ("tok", "cot", "wt", "out", "gtok"))
+    tok, cot, wt = (bufs.pop(k) for k in ("tok", "cot", "wt"))
     bufs.update(w_qkv=w_qkv, w_out=w_out, w_up=w_up, w_down=w_down, o_qkv=o_qkv, o_out=o_out, o_up=o_up, o_down=o_down)
     bufs["E"] = bufs.pop("EZ"), bufs.pop("EX")
     bufs["L"] = bufs.pop("LZ"), bufs.pop("LX")
@@ -906,26 +965,25 @@
     cm.ne = 4 + bup.shape[0]
     cm.early = lambda rows: cm.v_start("E", rows)
     cm.late = lambda rows: cm.v_start("L", rows)
-    pairs = ((tok_h, tok), (wt_h, wt), (cot_h, cot), (out, out_h), (gtok, gtok_h))
+    pairs = ((tok_h, tok), (wt_h, wt), (cot_h, cot))
     moves = [pltpu.make_async_copy(a, b, local.at[i]) for i, (a, b) in enumerate(pairs)]
-    for x in moves[:3]:
-        x.start()
     plain_hook = cm.hook
 
     def hook(place, j=None):
-        if place == "row_in":
+        if place == "greet":
+            plain_hook(place)
+            for x in moves:
+                x.start()
+        elif place == "row_in":
             moves[0].wait()
             moves[1].wait()
         elif place == "cot_in":
             moves[2].wait()
-        elif place == "row_out":
-            moves[3].start()
         else:
             plain_hook(place, j)
 
     cm.hook = hook
     layer(cm, T, most, len_ref[T], ts_ref[0].astype(f32), tok, cot, seg, wt, btime, g1, b1, g2, b2, bdown, bup, out, gtok, sc)
-    moves[4].start()
     cm.hook("finish")
     cm.v_mid("L", 3)
     kept, sums = cm.v_done("E", cm.ne)
@@ -938,8 +996,6 @@
     cm.hook("leave")
     cm.v_leave("E")
     cm.v_leave("L")
-    moves[3].wait()
-    moves[4].wait()
 
 
 def run_linked(most, nd, nt, length, ts, tok, cot, seg, w_qkv, w_out, w_up, w_down, wt, vecs, bup):
@@ -954,41 +1010,38 @@
         DQ=V((nt, ng, 2, r, 384), bf16), DO=V((nt, ng, 2, r, 128), bf16), D2=V((nt, 2, ng, 2, r, F), bf16),
         CQ=V((nt, ng, r, 384), bf16), XQ=V((nt, ng, r, 384), bf16), ZQ=V((nt, r, 384), bf16),
         CO=V((nt, ng, r, 128), bf16), XO=V((ng, nt, r, 128), bf16), ZO=V((nt, r, 128), bf16),
-        C2=V((nt, 2, ng, r, F), bf16), X2=V((nt, ng, 2, r, F), bf16), Z2=V((nt, 2, r, F), bf16),
+        C2=V((nt, 2, ng, r, F), bf16), X2=V((nt, ng, 2, r, F), bf16), Z2=V((nt, 2, r, F), bf16), Y2=V((2, ng, r, F), bf16),
         EZ=V((nt, 8, D), f32), EX=V((nd, 16, D), f32), LZ=V((nt, 8, D), f32), LX=V((nd, 16, D), f32),
-        tok=V((seq, D), bf16), cot=V((seq, D), bf16), wt=V((D, D), f32), out=V((seq, D), bf16), gtok=V((seq, D), f32),
+        tok=V((seq, D), bf16), cot=V((seq, D), bf16), wt=V((D, D), f32),
     )
-    sems = dict(gq_plane=(nt, ng), gq_z=(nt,), gq_core=(nt,), go_z=(nt,), g2_z=(nt,), go_plane=(ng,), go_core=(), g2_plane=(nt, ng), g2_core=(nt,),
-        rq_core=(nt,), rq_plane=(nt, ng), rq_z=(nt,), r2_core=(nt,), r2_plane=(nt, ng), r2_z=(nt,), ro_core=(), ro_plane=(ng,), ro_z=(nt,),
+    sems = dict(gq_plane=(nt, ng), gq_z=(nt,), gq_core=(nt,), go_z=(nt,), g2_z=(nt,), go_plane=(ng,), go_core=(), g2_plane=(nt, 2, ng), g2_core=(nt,),
+        rq_core=(nt,), rq_plane=(nt, ng), rq_z=(nt,), r2_core=(nt,), r2_plane=(nt, ng), r2_z=(nt,), r2_near=(), ro_core=(), ro_plane=(ng,), ro_z=(nt,),
         E_z=(nt,), E_dp=(nd,), L_z=(nt,), L_dp=(nd,))
     ls = layer_scratch(seq, D, P, NF, F)
     scratch = ls + list(bufs.values())
     for s in sems.values():
         scratch += [DMA(s), DMA(s)]
-    scratch.append(DMA((5,)))
+    scratch.append(DMA((3,)))
     vm = pl.BlockSpec(memory_space=pltpu.VMEM)
     sm = pl.BlockSpec(memory_space=pltpu.SMEM)
     hb = pl.BlockSpec(memory_space=pltpu.HBM)
+    an = pl.BlockSpec(memory_space=pl.ANY)
     return pl.pallas_call(
         functools.partial(linked_kernel, most, ng, nt, tuple(bufs), tuple(sems), len(ls)),
-        out_shape=(S((seq, D), bf16), S((seq, D), f32), S(w_qkv.shape, f32), S(w_out.shape, f32), S(w_up.shape, f32), S(w_down.shape, f32),
-            S((8 * nd, D), f32), S((8 * nd, D), f32), S((16, D), f32)),
-        in_specs=[sm, sm, hb, hb] + [vm] * 5 + [hb] + [vm] * 7, out_specs=[hb, hb] + [vm] * 7,
+        out_shape=(V((seq, D), bf16), V((seq, D), f32), V(w_qkv.shape, f32), V(w_out.shape, f32), V(w_up.shape, f32), V(w_down.shape, f32),
+            V((8 * nd, D), f32), V((8 * nd, D), f32), V((16, D), f32)),
+        in_specs=[sm, sm, hb, hb] + [vm] * 5 + [hb] + [vm] * 7, out_specs=[vm] * 9,
         scratch_shapes=scratch,
-        compiler_params=pltpu.CompilerParams(vmem_limit_bytes=62 << 20, collective_id=0, has_side_effects=True),
+        compiler_params=pltpu.CompilerParams(vmem_limit_bytes=56 << 20, collective_id=0, has_side_effects=True),
     )(length, ts, tok, cot, seg, w_qkv, w_out, w_up, w_down, wt, *[v[None] for v in vecs], bup)
 
 
 def emit_kernel(nb, *refs):
-    big, outs, gwt, small, bufs = refs[:9], refs[9:15], refs[15], refs[16:23], refs[23:32]
-    sem_in, sem_out = refs[32:]
-    ins = [pltpu.make_async_copy(a, b, sem_in.at[i]) for i, (a, b) in enumerate(zip(big, bufs))]
-    ups = [pltpu.make_async_copy(a, b, sem_out.at[i]) for i, (a, b) in enumerate(zip(bufs[3:], outs))]
-    for x in ins:
+    big, outs, gwt, small, sem = refs[:9], refs[9:15], refs[15], refs[16:23], refs[23]
+    ups = [pltpu.make_async_copy(a, b, sem.at[i]) for i, (a, b) in enumerate(zip(big[3:], outs))]
+    for x in ups:
         x.start()
-    for x in ins[:3]:
-        x.wait()
-    embs, grads, vec = (b[...] for b in bufs[:3])
+    embs, grads, vec = (b[...] for b in big[:3])
     gwt[...] = lax.dot_general(embs, grads, (((0,), (0,)), ((), ())), precision=lax.Precision.HIGHEST, preferred_element_type=f32)
     small[0][...] = jnp.sum(grads, axis=0)
     for k, o in enumerate(small[1:-1]):
@@ -996,9 +1049,6 @@
     n = vec.shape[1]
     for k in range(nb):
         small[-1][pl.ds(k * n, n)] = vec[7 + k, :]
-    for x, y in zip(ins[3:], ups):
-        x.wait()
-        y.start()
     for y in ups:
         y.wait()
 
@@ -1007,13 +1057,14 @@
     S = jax.ShapeDtypeStruct
     D = big[2].shape[1]
     vm = pl.BlockSpec(memory_space=pltpu.VMEM)
+    an = pl.BlockSpec(memory_space=pl.ANY)
     hb = pl.BlockSpec(memory_space=pltpu.HBM)
     return pl.pallas_call(
         functools.partial(emit_kernel, nb),
         out_shape=tuple(S(x.shape, x.dtype) for x in big[3:]) + (S((D, D), f32),) + tuple(S((D,), f32) for _ in range(6)) + (S((nb * D,), f32),),
-        in_specs=[hb] * 9, out_specs=[hb] * 6 + [vm] * 8,
-        scratch_shapes=[pltpu.VMEM(x.shape, x.dtype) for x in big] + [pltpu.SemaphoreType.DMA((9,)), pltpu.SemaphoreType.DMA((6,))],
-        compiler_params=pltpu.CompilerParams(vmem_limit_bytes=60 << 20),
+        in_specs=[vm] * 3 + [an] * 6, out_specs=[hb] * 6 + [vm] * 8,
+        scratch_shapes=[pltpu.SemaphoreType.DMA((6,))],
+        compiler_params=pltpu.CompilerParams(vmem_limit_bytes=16 << 20),
     )(*big)
 
 
@@ -1041,7 +1092,7 @@
     vecs = (b_time, ln1_gain, ln1_bias, ln2_gain, ln2_bias, b_down)
     F = w_up.shape[1]
     bup = b_up.reshape(nt, 1, F)
-    if w_up.shape[0] % 16 == 0:
+    if w_up.shape[0] % 16 == 0 and (nd, nt) == (8, 4):
         out, gtok, *g, embs, lines, vec = run_linked(
             DOC, nd, nt, span_lengths, timestep, tokens[0], cotangent[0], segment_ids,
             w_qkv, w_out_t, w_up, w_down_t, w_time, vecs, bup)

time: 113 us -> 106 us (0.938)
  Pallas kernels: 111 us -> 104 us
    pallas_call x1, Pallas kernels: 106 us -> 102 us  [run_linked(): pl.pallas_call(functools.partial(linked_kernel, most, ng, nt, tuple(bufs)...]
    pallas_call x1, Pallas kernels: 4.92 us -> 2.86 us  [emit(): pl.pallas_call(functools.partial(emit_kernel, nb), out_shape=tuple((S(x.s...]
where the time goes in v6:
time: 106 us
  Pallas kernels  104 us (98%)
  between operations  1.47 us (1%)
    pallas_call x1, Pallas kernels, run_linked(): pl.pallas_call(functools.partial(linked_kernel, most, ng, nt, tuple(bufs)...  102 us
    pallas_call x1, Pallas kernels, emit(): pl.pallas_call(functools.partial(emit_kernel, nb), out_shape=tuple((S(x.s...  2.86 us

profile of v6, /device:TPU:0, one launch (start us, length us, event | category | flops | bytes accessed | tf_op | source)
XLA Modules:
  0.0 105.9 jit_solution(5330197185384198883)
XLA Ops:
  1.3 101.6 %shard_map.272 = (bf16[1024,512]{1,0:T(8,128)(2,1)S(1)}, f32[1024,512]{1,0:T(8,128)S(1)}, f32[3,64,128]{2,1,0:T(8,128)S(1)}, f32[64,128]{1,0:T(8,128)S(1)}, f32[...) custom-call(s32[4]{0:T(128)} %refs_0_.1, ...), custom_call_target="tpu_custom_call" | custom-call | tf_op jit(solution)/shard_map/pallas_call | solution.py:1029
  102.9 2.9 %shard_map.273 = (f32[3,64,128]{2,1,0:T(8,128)}, f32[64,128]{1,0:T(8,128)}, f32[64,512]{1,0:T(8,128)}, f32[64,512]{1,0:T(8,128)}, bf16[1024,512]{1,0:T(8,128)(2,...) custom-call(f32[64,512]{1,0:T(8,128)S(1)} %get-tuple-element.37.refs, ...), custom_call_target="tpu_custom_call" | custom-call | tf_op jit(solution)/shard_map/pallas_call | solution.py:1062

commit v7 on v6

--- a/solution.py
+++ b/solution.py
@@ -11,6 +11,7 @@
 f32, bf16 = jnp.float32, jnp.bfloat16
 HS = 64
 TR = 256
+TB = 256
 BIG = 1e30
 EPS = 1e-5
 DOC = 512
@@ -74,9 +75,9 @@
     return hi, mid, lo
 
 
-def window(i, seq, most):
-    lo = max(0, (i * TR - most + 1) // 128 * 128)
-    hi = min(seq, -(-(i * TR + TR - 1 + most) // 128) * 128)
+def window(i, seq, most, tr):
+    lo = max(0, (i * tr - most + 1) // 128 * 128)
+    hi = min(seq, -(-(i * tr + tr - 1 + most) // 128) * 128)
     return lo, hi
 
 
@@ -128,7 +129,7 @@
         prep(i, 0)
 
     def score(i, h):
-        lo, hi = window(i, seq, most)
+        lo, hi = window(i, seq, most, TR)
         return nt_dot(qq[h, i * TR:i * TR + TR, :], kk[h, lo:hi, :])
 
     def soft(i, s, own):
@@ -167,7 +168,7 @@
         nxt = score(*units[u + 1]) if u + 1 < len(units) else None
         if h == 0:
             own = selfs(i)
-        lo, hi = window(i, seq, most)
+        lo, hi = window(i, seq, most, TR)
         m, p = soft(i, s, own[h])
         tops.append(m)
         outs.append(nn_dot(p, vv[h, lo:hi, :]))
@@ -178,11 +179,11 @@
 
 
 def attend_bwd(seq, most, length, qkv, qaug, kaug, mixed, lse, gm, qq, kk, vv, oo, dq, dkv, dqkv, hp):
-    n = seq // TR
+    n = seq // TB
     def prep(i, _):
-        r = slice(i * TR, i * TR + TR)
-        low = lane((TR, 128)) < HS
-        spot = lane((TR, 128)) % HS
+        r = slice(i * TB, i * TB + TB)
+        low = lane((TB, 128)) < HS
+        spot = lane((TB, 128)) % HS
         q, k, v = (qkv[hp, r, 128 * c:128 * c + 128] for c in range(3))
         g = gm[hp, r, :]
         dx = half_sums(g.astype(f32) * mixed[hp, r, :].astype(f32), True)
@@ -191,7 +192,7 @@
             z = jnp.where(spot == 8, hi, base)
             z = jnp.where(spot == 9, mid, z)
             return jnp.where(spot == 10, lo, z)
-        zero = jnp.zeros((TR, 128), bf16)
+        zero = jnp.zeros((TB, 128), bf16)
         qa = put(qaug[r, :], lse[hp, r, :])
         oa = put(zero, dx)
         ka = kaug[r, :]
@@ -199,9 +200,9 @@
         for ref, x, a in ((qq, q, qa), (kk, k, ka), (vv, v, va), (oo, g, oa)):
             ref[0, r, :] = jnp.where(low, x, a)
             ref[1, r, :] = jnp.where(low, a, x)
-        if (i + 1) * TR > LEAST:
+        if (i + 1) * TB > LEAST:
             q, k, v, g = (x.astype(f32) for x in (q, k, v, g))
-            padf = ((lax.broadcasted_iota(jnp.int32, (TR, 1), 0) + i * TR) >= length).astype(f32)
+            padf = ((lax.broadcasted_iota(jnp.int32, (TB, 1), 0) + i * TB) >= length).astype(f32)
             ls = pltpu.roll(lse[hp, r, :], HS, 1)
             d = pltpu.roll(dx, HS, 1)
             pf = jnp.exp2(jnp.minimum(half_sums(q * k) - ls, 1.0)) * padf
@@ -212,18 +213,18 @@
         return 0
     for i in range(n):
         prep(i, 0)
-    lo, hi = window(0, seq, most)
+    hi = window(0, seq, most, TB)[1]
     if hi < seq:
         dq[:, hi:seq, :] = jnp.zeros((2, seq - hi, 128), f32)
 
     def score(i, h):
-        lo, hi = window(i, seq, most)
-        r = slice(i * TR, i * TR + TR)
+        lo, hi = window(i, seq, most, TB)
+        r = slice(i * TB, i * TB + TB)
         return nt_dot(kk[h, r, :], qq[h, lo:hi, :]), nt_dot(vv[h, r, :], oo[h, lo:hi, :])
 
     def rest(i, h, st, dpt):
-        lo, hi = window(i, seq, most)
-        r = slice(i * TR, i * TR + TR)
+        lo, hi = window(i, seq, most, TB)
+        r = slice(i * TB, i * TB + TB)
         pt = jnp.exp2(st)
         dst = (pt * dpt).astype(bf16)
         dkv[h, 0, r, :] = nn_dot(dst, qq[h, lo:hi, :])
@@ -242,12 +243,12 @@
         s = nxt
 
     for i in range(n):
-        r = slice(i * TR, i * TR + TR)
-        low = lane((TR, 128)) < HS
+        r = slice(i * TB, i * TB + TB)
+        low = lane((TB, 128)) < HS
         gq = jnp.where(low, dq[0, r, :], dq[1, r, :])
         gk = jnp.where(low, dkv[0, 0, r, :], dkv[1, 0, r, :])
         gv = jnp.where(low, dkv[0, 1, r, :], dkv[1, 1, r, :])
-        if (i + 1) * TR > LEAST:
+        if (i + 1) * TB > LEAST:
             ds, pf = dkv[2, 0, r, :], dkv[2, 1, r, :]
             gq = gq + ds * qkv[hp, r, 128:256].astype(f32)
             gk = gk + ds * qkv[hp, r, 0:128].astype(f32)
@@ -290,6 +291,9 @@
         return j
 
     def order_back(self, j):
+        return j
+
+    def order_ffn(self, j):
         return j
 
     def hook(self, *_):
@@ -368,6 +372,12 @@
     def order_back(self, j):
         return self.t ^ (self.nt - 1 - j)
 
+    def turn(self, j):
+        return (2 * j) ^ (7 * (j // 2))
+
+    def order_ffn(self, j):
+        return self.t ^ self.turn(j)
+
     def peers(self):
         return [("dp", k) for k in range(1, 2 * self.ng)] + [("z", k) for k in range(1, self.nt)]
 
@@ -414,6 +424,10 @@
     def f_plane(self, j, k, u, incoming=False):
         g, c, f = self.g, self.c, self.t ^ j
         return self.copy("g2_plane", (j, u, k), "plane", k, self.W2.at[f, u, g, c], self.W2.at[f, u, g ^ k if incoming else g, c])
+
+    def f_near(self, u, incoming=False):
+        c, t = self.c, self.t
+        return self.copy("g2_near", (u,), "z", 1, self.W2.at[t, u, :, c], self.W2.at[t ^ 1 if incoming else t, u, :, c])
 
     def f_on(self, x):
         self.f_z(x, True).wait_recv()
@@ -462,9 +476,7 @@
     def q_after_core(self, x):
         p, c = self.t ^ x, self.c
         self.rq("core", x).wait_recv()
-        self.DQ[p, :, c] = (self.DQ[p, :, c].astype(f32) + self.CQ[x].astype(f32)).astype(bf16)
-        for k in range(1, self.ng):
-            self.rq("plane", x, k).start()
+        self.DQ[p, :, c] = self.DQ[p, :, c] + self.CQ[x]
 
     def q_after_plane(self, x):
         p, c, g = self.t ^ x, self.c, self.g
@@ -479,7 +491,7 @@
         self.r2("core", x).wait_recv()
         for u in range(2):
             def step(i, _):
-                self.D2[p, u, i, c] = (self.D2[p, u, i, c].astype(f32) + self.C2[x, u, i].astype(f32)).astype(bf16)
+                self.D2[p, u, i, c] = self.D2[p, u, i, c] + self.C2[x, u, i]
                 return 0
             lax.fori_loop(0, self.ng, step, 0)
 
@@ -513,8 +525,6 @@
             self.WO[t, g, c] = self.w_out[...].astype(bf16)
             self.W2[t, 0, g, c] = self.w_up[...].astype(bf16)
             self.W2[t, 1, g, c] = self.w_down[...].astype(bf16)
-            for x in (self.E[1], self.L[1]):
-                x[self.d] = jnp.zeros(x.shape[1:], f32)
             self.enter()
             begin(*[self.q_plane(0, k) for k in planes], self.q_z(1))
         elif place == "normed":
@@ -530,6 +540,7 @@
             @pl.when(j == 0)
             def _():
                 begin(*[self.o_z(k) for k in range(1, nt)])
+                begin(self.f_z(2))
                 begin(*[self.f_plane(0, k, 0) for k in planes])
         elif place == "pair_half":
             @pl.when(j == 0)
@@ -540,22 +551,25 @@
                 begin(*[self.q_plane(2, k) for k in planes])
             @pl.when(j == 1)
             def _():
-                begin(self.f_z(2), self.f_z(3))
                 begin(*[self.f_plane(0, k, 1) for k in planes])
             @pl.when(j == 2)
             def _():
                 await_in(*[self.q_plane(3, k, True) for k in planes])
                 begin(self.q_core(3))
+                await_in(*[self.f_plane(0, k, 0, True) for k in planes])
+                begin(self.f_near(0))
             @pl.when(j == 3)
             def _():
                 await_in(*[self.o_plane(k, True) for k in planes])
                 begin(self.o_core())
+                await_in(*[self.f_plane(0, k, 1, True) for k in planes])
+                begin(self.f_near(1), self.f_core(0))
         elif place == "pair_mid":
             @pl.when(j == 0)
             def _():
                 await_in(self.q_z(3, True))
                 begin(*[self.q_plane(3, k) for k in planes])
-                begin(self.f_z(1))
+                begin(self.f_z(3))
             @pl.when(j == 1)
             def _():
                 await_in(*[self.o_z(k, True) for k in range(1, nt)])
@@ -564,57 +578,57 @@
                 begin(self.q_core(2))
             @pl.when(j == 2)
             def _():
-                self.f_on(1)
+                self.f_on(2)
             @pl.when(j == 3)
             def _():
-                self.f_on(2)
+                self.f_on(3)
         elif place == "mixed":
             await_in(self.o_core(True))
-        elif place == "second":
-            self.f_pass(0)
-            self.f_on(3)
         elif place == "chunk":
-            await_in(self.f_core(j, True))
+            await_in(self.f_core(self.turn(j), True))
         elif place == "chunk_mid":
-            @pl.when(j < nt - 1)
-            def _():
-                self.f_pass(j + 1)
+            @pl.when(j < 2)
+            def _():
+                self.f_pass(j + 2)
+            @pl.when(j == 2)
+            def _():
+                await_in(self.f_near(0, True), self.f_near(1, True))
+                begin(self.f_core(1))
             @pl.when(j >= 1)
             def _():
-                self.f_after_core(j - 1)
-            @pl.when(j == 2)
-            def _():
-                begin(self.r2_near())
-            @pl.when(j == 3)
-            def _():
-                begin(*[self.r2("plane", 2, k) for k in planes])
+                x = self.turn(j - 1)
+                self.f_after_core(x)
+                @pl.when(j >= 2)
+                def _():
+                    begin(*[self.r2("plane", x, k) for k in planes])
         elif place == "chunk_end":
-            begin(self.r2("core", j))
+            begin(self.r2("core", self.turn(j)))
         elif place == "ffn_done":
-            self.f_after_core(nt - 1)
-            begin(*[self.r2("plane", 3, k) for k in planes])
+            self.f_after_core(1)
+            begin(self.r2_near())
         elif place == "out_grad":
             begin(self.ro("core"))
         elif place == "back_mid":
             @pl.when(j >= 1)
             def _():
                 self.q_after_core(nt - j)
+                begin(*[self.rq("plane", nt - j, k) for k in planes])
             @pl.when(j == 0)
             def _():
                 await_in(self.ro("core"))
                 for p in range(nt):
-                    self.DO[p, :, c] = (self.DO[p, :, c].astype(f32) + self.CO[p].astype(f32)).astype(bf16)
+                    self.DO[p, :, c] = self.DO[p, :, c] + self.CO[p]
                 begin(*[self.ro("plane", k) for k in planes])
                 self.v_mid("E", self.ne)
+            @pl.when(j == 1)
+            def _():
                 await_in(self.r2_near())
                 for u in range(2):
                     def step(i, _):
-                        self.D2[t, u, i, c] = (self.D2[t, u, i, c].astype(f32) + self.Y2[u, i].astype(f32)).astype(bf16)
+                        self.D2[t, u, i, c] = self.D2[t, u, i, c] + self.Y2[u, i]
                         return 0
                     lax.fori_loop(0, ng, step, 0)
                 begin(*[self.r2("plane", 0, k) for k in planes])
-            @pl.when(j == 1)
-            def _():
                 self.f_after_plane(2)
                 begin(self.r2("z", 2))
             @pl.when(j == 2)
@@ -628,26 +642,24 @@
                 begin(*[self.ro("z", k) for k in range(1, nt)])
                 self.f_after_plane(3)
                 begin(self.r2("z", 3))
-            @pl.when(j == 3)
-            def _():
-                self.f_after_plane(0)
             @pl.when(j >= 2)
             def _():
                 self.q_after_plane(nt - j + 1)
                 begin(self.rq("z", nt - j + 1))
         elif place == "back_end":
             self.rq("core", nt - 1 - j).start()
-        elif place == "back_done":
+        elif place == "finish":
             self.q_after_core(0)
-            self.q_after_plane(1)
-            self.rq("z", 1).start()
-        elif place == "finish":
+            begin(*[self.rq("plane", 0, k) for k in planes])
             for x in range(1, nt):
                 if x > 1:
                     self.r2("z", x).wait_recv()
                 self.ro("z", x).wait_recv()
+            await_in(*[self.r2("plane", 0, k) for k in planes])
             for u, o in enumerate((self.o_up, self.o_down)):
                 acc = self.D2[t, u, g, c].astype(f32)
+                for k in planes:
+                    acc = acc + self.X2[0, k, u].astype(f32)
                 for x in range(2, nt):
                     acc = acc + self.Z2[x, u].astype(f32)
                 o[...] = acc
@@ -655,6 +667,9 @@
             for x in range(1, nt):
                 acc = acc + self.ZO[x].astype(f32)
             self.o_out[...] = acc
+        elif place == "finish_z":
+            self.q_after_plane(1)
+            begin(self.rq("z", 1))
         elif place == "finish_q":
             acc = self.DQ[t, g, c].astype(f32)
             for k in range(1, ng):
@@ -671,8 +686,9 @@
                 self.ro("plane", k).wait_send()
                 for x in range(nt):
                     self.q_plane(x, k).wait_send()
-                    for u in range(2):
-                        self.f_plane(x, k, u).wait_send()
+                    if x != 1:
+                        for u in range(2):
+                            self.f_plane(x, k, u).wait_send()
                     if x != 1:
                         self.r2("plane", x, k).wait_send()
                     self.rq("plane", x, k).wait_send()
@@ -684,11 +700,13 @@
             self.o_core().wait_send()
             self.ro("core").wait_send()
             self.r2_near().wait_send()
+            self.f_near(0).wait_send()
+            self.f_near(1).wait_send()
             for k in range(1, nt):
                 self.q_z(k).wait_send()
                 self.o_z(k).wait_send()
-                self.f_z(k).wait_send()
                 if k > 1:
+                    self.f_z(k).wait_send()
                     self.r2("z", k).wait_send()
                 self.rq("z", k).wait_send()
                 self.ro("z", k).wait_send()
@@ -701,34 +719,39 @@
 
     def v_start(self, name, rows):
         Z = getattr(self, name)[0]
+        n = rows[0].shape[1]
         for k, x in enumerate(rows):
-            Z[self.t, k:k + 1, :] = x
+            Z[self.t, :, k * n:k * n + n] = x
         for k in range(1, self.nt):
             self.v(name, "z", k).start()
 
     def v_mid(self, name, m):
         Z, X = getattr(self, name)
-        nt = self.nt
+        nt, n = self.nt, Z.shape[2] // m
         for k in range(1, nt):
             self.v(name, "z", k, True).wait_recv()
         for k in range(nt):
-            X[self.d, k:k + 1, :] = Z[k, 0:1, :]
-        s = Z[0, 1:m, :]
+            X[self.d, :, k * n:k * n + n] = Z[k, :, 0:n]
+        s = Z[0, :, n:m * n]
         for k in range(1, nt):
-            s = s + Z[k, 1:m, :]
-        X[self.d, 8:8 + m - 1, :] = s
+            s = s + Z[k, :, n:m * n]
+        X[self.d, :, nt * n:(nt + m - 1) * n] = s
         for k in range(1, 2 * self.ng):
             self.v(name, "dp", k).start()
 
-    def v_done(self, name, m):
-        X = getattr(self, name)[1]
-        nd = 2 * self.ng
+    def v_done(self, name, m, kept, sums, at):
+        Z, X = getattr(self, name)
+        nd, nt, n = 2 * self.ng, self.nt, Z.shape[2] // m
         for k in range(1, nd):
             self.v(name, "dp", k, True).wait_recv()
-        s = X[0, 8:8 + m - 1, :]
+        for k in range(nd):
+            for i in range(nt):
+                kept[k * nt + i:k * nt + i + 1, :] = X[k, :, i * n:i * n + n]
+        s = X[0, :, nt * n:(nt + m - 1) * n]
         for k in range(1, nd):
-            s = s + X[k, 8:8 + m - 1, :]
-        return jnp.concatenate([X[k, 0:8, :] for k in range(nd)], axis=0), s
+            s = s + X[k, :, nt * n:(nt + m - 1) * n]
+        for i in range(m - 1):
+            sums[at + i:at + i + 1, :] = s[:, i * n:i * n + n]
 
     def v_leave(self, name):
         for k in range(1, self.nt):
@@ -751,7 +774,7 @@
 
 
 def layer(cm, T, most, length, t, tok, cot, seg, wt, btime, g1, b1, g2, b2, bdown, bup, out, gtok, sc):
-    tp, n1, qkv, qaug, kaug, mixed, lse, qq, kk, vv, oo, dq, dkv, dqkv, mid, n2, ffn, gn, act, gu, gm, xT, xT2, xT3, bsum = sc
+    tp, n1, qkv, qaug, kaug, mixed, lse, qq, kk, vv, oo, dq, dkv, dqkv, mid, n2, ffn, gn, act, gu, gm, xT, xT3, bsum = sc
     seq, D = tok.shape
     P = qkv.shape[0]
     NF, F = bsum.shape[0], bsum.shape[2]
@@ -818,10 +841,9 @@
 
     loop("ln2", seq, ln2, 0)
     cm.hook("second")
-    transpose_into(xT2, n2, seq)
 
     def chunk(j, _):
-        f = cm.order(j)
+        f = cm.order_ffn(j)
         cm.hook("chunk", j)
 
         def tile(r, acc):
@@ -840,7 +862,7 @@
 
         def wgrad(r, _):
             cm.put2(f, 1, r, nn_dot(xT[r, :], act[...]).astype(bf16))
-            cm.put2(f, 0, r, nn_dot(xT2[r, :], gu[...]).astype(bf16))
+            cm.put2(f, 0, r, tn_dot(n2[:, r], gu[...]).astype(bf16))
             return 0
 
         loop("wgrad", D, wgrad, 0)
@@ -865,7 +887,6 @@
     a = loop("ln2b", seq, ln2b, (z, z, z))
     cm.early([emb[0:1, :], *a] + [bsum[f] for f in range(NF)])
     cm.hook("ffn_done")
-    transpose_into(xT2, n2, seq)
 
     def gmix(r, _):
         x = nn_dot(n2[r, :], cm.geto()).astype(bf16)
@@ -877,7 +898,7 @@
 
     def gwo(r, _):
         m = jnp.concatenate([mixed[p] for p in range(P)], axis=1)
-        x = nn_dot(xT2[r, :], m).astype(bf16)
+        x = tn_dot(n2[:, r], m).astype(bf16)
         for p in range(P):
             cm.puto(p, r, x[:, 128 * p:128 * p + 128])
         return 0
@@ -904,7 +925,6 @@
         return 0
 
     lax.fori_loop(0, P, pair_bwd, 0)
-    cm.hook("back_done")
 
     def ln1b(r, acc):
         xh, rr = normed(tok[r, :].astype(f32) + tp[...])
@@ -922,7 +942,7 @@
     return [V((1, D), f32), V((seq, D), bf16), V((P, seq, 384), bf16), V((seq, 128), bf16), V((seq, 128), bf16),
         V((P, seq, 128), bf16), V((P, seq, 128), f32)] + [V((2, seq, 128), bf16)] * 4 + [V((2, seq, 128), f32),
         V((3, 2, seq, 128), f32), V((seq, 384), bf16), V((seq, D), f32), V((seq, D), bf16), V((seq, D), f32), V((seq, D), f32),
-        V((seq, F), bf16), V((seq, F), bf16), V((P, seq, 128), bf16), V((D, seq), bf16), V((D, seq), bf16), V((D, seq), bf16), V((NF, 1, F), f32)]
+        V((seq, F), bf16), V((seq, F), bf16), V((P, seq, 128), bf16), V((D, seq), bf16), V((D, seq), bf16), V((NF, 1, F), f32)]
 
 
 def plain_kernel(most, n_sc, *refs):
@@ -948,7 +968,8 @@
 
 
 def linked_kernel(most, ng, nt, names, semnames, n_layer, *refs):
-    len_ref, ts_ref, tok_h, cot_h, seg, w_qkv, w_out, w_up, w_down, wt_h, btime, g1, b1, g2, b2, bdown, bup = refs[:17]
+    len_ref, ts_ref = refs[:2]
+    held = refs[2:17]
     out, gtok, o_qkv, o_out, o_up, o_down, embs, grads, vec = refs[17:26]
     sc = refs[26:26 + n_layer]
     rest = refs[26 + n_layer:]
@@ -956,7 +977,8 @@
     sr = rest[len(names):]
     sems = {nm: (sr[2 * i], sr[2 * i + 1]) for i, nm in enumerate(semnames)}
     local = sr[-1]
-    tok, cot, wt = (bufs.pop(k) for k in ("tok", "cot", "wt"))
+    here = [bufs.pop("in%d" % i) for i in range(15)]
+    tok, cot, seg, w_qkv, w_out, w_up, w_down, wt, btime, g1, b1, g2, b2, bdown, bup = here
     bufs.update(w_qkv=w_qkv, w_out=w_out, w_up=w_up, w_down=w_down, o_qkv=o_qkv, o_out=o_out, o_up=o_up, o_down=o_down)
     bufs["E"] = bufs.pop("EZ"), bufs.pop("EX")
     bufs["L"] = bufs.pop("LZ"), bufs.pop("LX")
@@ -965,20 +987,21 @@
     cm.ne = 4 + bup.shape[0]
     cm.early = lambda rows: cm.v_start("E", rows)
     cm.late = lambda rows: cm.v_start("L", rows)
-    pairs = ((tok_h, tok), (wt_h, wt), (cot_h, cot))
-    moves = [pltpu.make_async_copy(a, b, local.at[i]) for i, (a, b) in enumerate(pairs)]
+    moves = [pltpu.make_async_copy(a, b, local.at[i]) for i, (a, b) in enumerate(zip(held, here))]
     plain_hook = cm.hook
 
     def hook(place, j=None):
         if place == "greet":
             plain_hook(place)
-            for x in moves:
-                x.start()
+            for i in (3, 4, 5, 6, 0, 7, 2, *range(8, 15), 1):
+                moves[i].start()
+            for i in range(3, 7):
+                moves[i].wait()
         elif place == "row_in":
-            moves[0].wait()
+            for i in (0, 7, 2, *range(8, 15)):
+                moves[i].wait()
+        elif place == "cot_in":
             moves[1].wait()
-        elif place == "cot_in":
-            moves[2].wait()
         else:
             plain_hook(place, j)
 
@@ -986,13 +1009,10 @@
     layer(cm, T, most, len_ref[T], ts_ref[0].astype(f32), tok, cot, seg, wt, btime, g1, b1, g2, b2, bdown, bup, out, gtok, sc)
     cm.hook("finish")
     cm.v_mid("L", 3)
-    kept, sums = cm.v_done("E", cm.ne)
-    embs[...] = kept
-    vec[4:4 + cm.ne - 1, :] = sums
+    cm.hook("finish_z")
+    cm.v_done("E", cm.ne, embs, vec, 4)
     cm.hook("finish_q")
-    kept, late = cm.v_done("L", 3)
-    grads[...] = kept
-    vec[2:4, :] = late
+    cm.v_done("L", 3, grads, vec, 2)
     cm.hook("leave")
     cm.v_leave("E")
     cm.v_leave("L")
@@ -1002,7 +1022,7 @@
     seq, D = tok.shape
     ng = nd // 2
     r, F = w_up.shape
-    P, NF = nt, nt
+    P, NF, ne = nt, nt, 4 + nt
     S, V = jax.ShapeDtypeStruct, pltpu.VMEM
     DMA = pltpu.SemaphoreType.DMA
     bufs = dict(
@@ -1011,17 +1031,19 @@
         CQ=V((nt, ng, r, 384), bf16), XQ=V((nt, ng, r, 384), bf16), ZQ=V((nt, r, 384), bf16),
         CO=V((nt, ng, r, 128), bf16), XO=V((ng, nt, r, 128), bf16), ZO=V((nt, r, 128), bf16),
         C2=V((nt, 2, ng, r, F), bf16), X2=V((nt, ng, 2, r, F), bf16), Z2=V((nt, 2, r, F), bf16), Y2=V((2, ng, r, F), bf16),
-        EZ=V((nt, 8, D), f32), EX=V((nd, 16, D), f32), LZ=V((nt, 8, D), f32), LX=V((nd, 16, D), f32),
-        tok=V((seq, D), bf16), cot=V((seq, D), bf16), wt=V((D, D), f32),
+        EZ=V((nt, 1, ne * D), f32), EX=V((nd, 1, (nt + ne - 1) * D), f32), LZ=V((nt, 1, 3 * D), f32), LX=V((nd, 1, (nt + 2) * D), f32),
     )
-    sems = dict(gq_plane=(nt, ng), gq_z=(nt,), gq_core=(nt,), go_z=(nt,), g2_z=(nt,), go_plane=(ng,), go_core=(), g2_plane=(nt, 2, ng), g2_core=(nt,),
+    held = (tok, cot, seg, w_qkv, w_out, w_up, w_down, wt, *[v[None] for v in vecs], bup)
+    for i, x in enumerate(held):
+        bufs["in%d" % i] = V(x.shape, x.dtype)
+    sems = dict(gq_plane=(nt, ng), gq_z=(nt,), gq_core=(nt,), go_z=(nt,), g2_z=(nt,), go_plane=(ng,), go_core=(), g2_plane=(nt, 2, ng), g2_core=(nt,), g2_near=(2,),
         rq_core=(nt,), rq_plane=(nt, ng), rq_z=(nt,), r2_core=(nt,), r2_plane=(nt, ng), r2_z=(nt,), r2_near=(), ro_core=(), ro_plane=(ng,), ro_z=(nt,),
         E_z=(nt,), E_dp=(nd,), L_z=(nt,), L_dp=(nd,))
     ls = layer_scratch(seq, D, P, NF, F)
     scratch = ls + list(bufs.values())
     for s in sems.values():
         scratch += [DMA(s), DMA(s)]
-    scratch.append(DMA((3,)))
+    scratch.append(DMA((15,)))
     vm = pl.BlockSpec(memory_space=pltpu.VMEM)
     sm = pl.BlockSpec(memory_space=pltpu.SMEM)
     hb = pl.BlockSpec(memory_space=pltpu.HBM)
@@ -1029,11 +1051,11 @@
     return pl.pallas_call(
         functools.partial(linked_kernel, most, ng, nt, tuple(bufs), tuple(sems), len(ls)),
         out_shape=(V((seq, D), bf16), V((seq, D), f32), V(w_qkv.shape, f32), V(w_out.shape, f32), V(w_up.shape, f32), V(w_down.shape, f32),
-            V((8 * nd, D), f32), V((8 * nd, D), f32), V((16, D), f32)),
-        in_specs=[sm, sm, hb, hb] + [vm] * 5 + [hb] + [vm] * 7, out_specs=[vm] * 9,
+            V((nd * nt, D), f32), V((nd * nt, D), f32), V((16, D), f32)),
+        in_specs=[sm, sm] + [hb] * 15, out_specs=[vm] * 9,
         scratch_shapes=scratch,
         compiler_params=pltpu.CompilerParams(vmem_limit_bytes=56 << 20, collective_id=0, has_side_effects=True),
-    )(length, ts, tok, cot, seg, w_qkv, w_out, w_up, w_down, wt, *[v[None] for v in vecs], bup)
+    )(length, ts, *held)
 
 
 def emit_kernel(nb, *refs):

time: 106 us -> 99.7 us (0.941)
  Pallas kernels: 104 us -> 98 us
    pallas_call x1, Pallas kernels: 102 us -> 95.2 us  [run_linked(): pl.pallas_call(functools.partial(linked_kernel, most, ng, nt, tuple(bufs)...]
where the time goes in v7:
time: 99.7 us; the launch traced here: 99.5 us
  Pallas kernels  98 us (98%)
  between operations  1.47 us (1%)
    pallas_call x1, Pallas kernels, run_linked(): pl.pallas_call(functools.partial(linked_kernel, most, ng, nt, tuple(bufs)...  95.2 us
    pallas_call x1, Pallas kernels, emit(): pl.pallas_call(functools.partial(emit_kernel, nb), out_shape=tuple((S(x.s...  2.86 us

profile of v7, /device:TPU:0, one launch (start us, length us, event | category | flops | bytes accessed | tf_op | source)
XLA Modules:
  0.0 99.5 jit_solution(11357541873526512481)
XLA Ops:
  1.3 95.2 %shard_map.272 = (bf16[1024,512]{1,0:T(8,128)(2,1)S(1)}, f32[1024,512]{1,0:T(8,128)S(1)}, f32[3,64,128]{2,1,0:T(8,128)S(1)}, f32[64,128]{1,0:T(8,128)S(1)}, f32[...) custom-call(s32[4]{0:T(128)} %refs_0_.1, ...), custom_call_target="tpu_custom_call" | custom-call | tf_op jit(solution)/shard_map/pallas_call | solution.py:1051
  96.5 2.9 %shard_map.273 = (f32[3,64,128]{2,1,0:T(8,128)}, f32[64,128]{1,0:T(8,128)}, f32[64,512]{1,0:T(8,128)}, f32[64,512]{1,0:T(8,128)}, bf16[1024,512]{1,0:T(8,128)(2,...) custom-call(f32[32,512]{1,0:T(8,128)S(1)} %get-tuple-element.37.refs, ...), custom_call_target="tpu_custom_call" | custom-call | tf_op jit(solution)/shard_map/pallas_call | solution.py:1084

commit v8 on v7

--- a/solution.py
+++ b/solution.py
@@ -41,18 +41,26 @@
     return pl.ds(pl.multiple_of(i * n, n), n)
 
 
-def normed(x):
+def normed_keep(x, stats, r):
     mean = jnp.mean(x, axis=-1, keepdims=True)
     c = x - mean
     var = jnp.mean(c * c, axis=-1, keepdims=True)
-    r = lax.rsqrt(var + EPS)
-    return c * r, r
-
-
-def norm_back(xhat, r, gain, gy):
+    f = lax.rsqrt(var + EPS)
+    stats[0, r, :] = jnp.broadcast_to(mean, (x.shape[0], 128))
+    stats[1, r, :] = jnp.broadcast_to(f, (x.shape[0], 128))
+    return c * f
+
+
+def normed_again(x, stats, r):
+    n = x.shape[1] // 128
+    f = jnp.concatenate([stats[1, r, :]] * n, axis=1)
+    return (x - jnp.concatenate([stats[0, r, :]] * n, axis=1)) * f, f
+
+
+def norm_back(gyx, xhat, r, gain, gy):
     gh = gy * gain
     a = jnp.mean(gh, axis=-1, keepdims=True)
-    b = jnp.mean(gh * xhat, axis=-1, keepdims=True)
+    b = jnp.mean(gyx * gain, axis=-1, keepdims=True)
     return r * (gh - a - xhat * b)
 
 
@@ -493,7 +501,8 @@
             def step(i, _):
                 self.D2[p, u, i, c] = self.D2[p, u, i, c] + self.C2[x, u, i]
                 return 0
-            lax.fori_loop(0, self.ng, step, 0)
+            for i in range(self.ng):
+                step(i, 0)
 
     def f_after_plane(self, x):
         p, c, g = self.t ^ x, self.c, self.g
@@ -528,10 +537,11 @@
             self.enter()
             begin(*[self.q_plane(0, k) for k in planes], self.q_z(1))
         elif place == "normed":
-            begin(self.q_z(2), self.q_z(3))
+            begin(self.q_z(2))
         elif place == "masked":
             await_in(self.q_z(1, True))
             begin(*[self.q_plane(1, k) for k in planes])
+            begin(self.q_z(3))
             await_in(*[self.q_plane(0, k, True) for k in planes])
             begin(self.q_core(0))
         elif place == "pair":
@@ -539,18 +549,20 @@
         elif place == "pair_proj":
             @pl.when(j == 0)
             def _():
+                await_in(self.q_z(2, True))
+                begin(*[self.q_plane(2, k) for k in planes])
                 begin(*[self.o_z(k) for k in range(1, nt)])
                 begin(self.f_z(2))
-                begin(*[self.f_plane(0, k, 0) for k in planes])
         elif place == "pair_half":
             @pl.when(j == 0)
             def _():
                 await_in(*[self.q_plane(1, k, True) for k in planes])
                 begin(self.q_core(1))
-                await_in(self.q_z(2, True))
-                begin(*[self.q_plane(2, k) for k in planes])
+                begin(*[self.f_plane(0, k, 0) for k in planes])
             @pl.when(j == 1)
             def _():
+                await_in(*[self.q_plane(2, k, True) for k in planes])
+                begin(self.q_core(2))
                 begin(*[self.f_plane(0, k, 1) for k in planes])
             @pl.when(j == 2)
             def _():
@@ -574,8 +586,6 @@
             def _():
                 await_in(*[self.o_z(k, True) for k in range(1, nt)])
                 begin(*[self.o_plane(k) for k in planes])
-                await_in(*[self.q_plane(2, k, True) for k in planes])
-                begin(self.q_core(2))
             @pl.when(j == 2)
             def _():
                 self.f_on(2)
@@ -627,7 +637,8 @@
                     def step(i, _):
                         self.D2[t, u, i, c] = self.D2[t, u, i, c] + self.Y2[u, i]
                         return 0
-                    lax.fori_loop(0, ng, step, 0)
+                    for i in range(ng):
+                        step(i, 0)
                 begin(*[self.r2("plane", 0, k) for k in planes])
                 self.f_after_plane(2)
                 begin(self.r2("z", 2))
@@ -761,7 +772,7 @@
 
 
 TILE = dict(ln1=256, proj=1024, ln2=512, tile=512, wgrad=512, ln2b=256, gmix=1024, gwo=512, qgrad=512, back=1024, ln1b=256)
-UNROLL = {"proj", "ln2", "tile", "wgrad", "gmix", "gwo", "qgrad", "back"}
+UNROLL = {"ln1", "ln1b", "ln2b", "proj", "ln2", "tile", "wgrad", "gmix", "gwo", "qgrad", "back"}
 
 
 def loop(name, total, body, init):
@@ -774,7 +785,7 @@
 
 
 def layer(cm, T, most, length, t, tok, cot, seg, wt, btime, g1, b1, g2, b2, bdown, bup, out, gtok, sc):
-    tp, n1, qkv, qaug, kaug, mixed, lse, qq, kk, vv, oo, dq, dkv, dqkv, mid, n2, ffn, gn, act, gu, gm, xT, xT3, bsum = sc
+    tp, n1, qkv, qaug, kaug, mixed, lse, qq, kk, vv, oo, dq, dkv, dqkv, mid, n2, ffn, gn, act, gu, gm, xT, xT3, bsum, stat1, stat2 = sc
     seq, D = tok.shape
     P = qkv.shape[0]
     NF, F = bsum.shape[0], bsum.shape[2]
@@ -788,7 +799,7 @@
     tp[...] = jnp.dot(emb, wt[...], precision=lax.Precision.HIGHEST, preferred_element_type=f32)[0:1, :] + btime[...]
 
     def ln1(r, _):
-        xh, _r = normed(tok[r, :].astype(f32) + tp[...])
+        xh = normed_keep(tok[r, :].astype(f32) + tp[...], stat1, r)
         n1[r, :] = (xh * g1[...] + b1[...]).astype(bf16)
         return 0
 
@@ -833,7 +844,7 @@
         mx = jnp.concatenate([mixed[p, r, :] for p in range(P)], axis=1)
         x = tok[r, :].astype(f32) + tp[...] + nt_dot(mx, cm.geto())
         mid[r, :] = x
-        xh, _r = normed(x)
+        xh = normed_keep(x, stat2, r)
         n2[r, :] = (xh * g2[...] + b2[...]).astype(bf16)
         ffn[r, :] = jnp.zeros((TILE["ln2"], D), f32)
         gn[r, :] = jnp.zeros((TILE["ln2"], D), f32)
@@ -875,13 +886,14 @@
         c = cot[r, :].astype(f32)
         x = mid[r, :]
         out[r, :] = (x + ffn[r, :] + bdown[...]).astype(bf16)
-        xh, rr = normed(x)
+        xh, rr = normed_again(x, stat2, r)
         gy = gn[r, :]
-        gmid = c + norm_back(xh, rr, g2[...], gy)
+        gyx = gy * xh
+        gmid = c + norm_back(gyx, xh, rr, g2[...], gy)
         mid[r, :] = gmid
         n2[r, :] = gmid.astype(bf16)
         gn[r, :] = jnp.zeros((TILE["ln2b"], D), f32)
-        return acc[0] + colsum(gy * xh), acc[1] + colsum(gy), acc[2] + colsum(c)
+        return acc[0] + colsum(gyx), acc[1] + colsum(gy), acc[2] + colsum(c)
 
     z = jnp.zeros((1, D), f32)
     a = loop("ln2b", seq, ln2b, (z, z, z))
@@ -927,11 +939,12 @@
     lax.fori_loop(0, P, pair_bwd, 0)
 
     def ln1b(r, acc):
-        xh, rr = normed(tok[r, :].astype(f32) + tp[...])
+        xh, rr = normed_again(tok[r, :].astype(f32) + tp[...], stat1, r)
         gy = gn[r, :]
-        gt = mid[r, :] + norm_back(xh, rr, g1[...], gy)
+        gyx = gy * xh
+        gt = mid[r, :] + norm_back(gyx, xh, rr, g1[...], gy)
         gtok[r, :] = gt
-        return acc[0] + colsum(gt), acc[1] + colsum(gy * xh), acc[2] + colsum(gy)
+        return acc[0] + colsum(gt), acc[1] + colsum(gyx), acc[2] + colsum(gy)
 
     a = loop("ln1b", seq, ln1b, (z, z, z))
     cm.late(list(a))
@@ -942,7 +955,7 @@
     return [V((1, D), f32), V((seq, D), bf16), V((P, seq, 384), bf16), V((seq, 128), bf16), V((seq, 128), bf16),
         V((P, seq, 128), bf16), V((P, seq, 128), f32)] + [V((2, seq, 128), bf16)] * 4 + [V((2, seq, 128), f32),
         V((3, 2, seq, 128), f32), V((seq, 384), bf16), V((seq, D), f32), V((seq, D), bf16), V((seq, D), f32), V((seq, D), f32),
-        V((seq, F), bf16), V((seq, F), bf16), V((P, seq, 128), bf16), V((D, seq), bf16), V((D, seq), bf16), V((NF, 1, F), f32)]
+        V((seq, F), bf16), V((seq, F), bf16), V((P, seq, 128), bf16), V((D, seq), bf16), V((D, seq), bf16), V((NF, 1, F), f32), V((2, seq, 128), f32), V((2, seq, 128), f32)]
 
 
 def plain_kernel(most, n_sc, *refs):

time: 99.7 us -> 98.8 us (level)
  no operation moved by 1% of the time
where the time goes in v8:
time: 98.8 us; the launch traced here: 98.6 us
  Pallas kernels  97.2 us (98%)
  between operations  1.47 us (1%)
    pallas_call x1, Pallas kernels, run_linked(): pl.pallas_call(functools.partial(linked_kernel, most, ng, nt, tuple(bufs)...  94.3 us
    pallas_call x1, Pallas kernels, emit(): pl.pallas_call(functools.partial(emit_kernel, nb), out_shape=tuple((S(x.s...  2.86 us

profile of v8, /device:TPU:0, one launch (start us, length us, event | category | flops | bytes accessed | tf_op | source)
XLA Modules:
  0.0 98.6 jit_solution(11132036468723617409)
XLA Ops:
  1.3 94.3 %shard_map.272 = (bf16[1024,512]{1,0:T(8,128)(2,1)S(1)}, f32[1024,512]{1,0:T(8,128)S(1)}, f32[3,64,128]{2,1,0:T(8,128)S(1)}, f32[64,128]{1,0:T(8,128)S(1)}, f32[...) custom-call(s32[4]{0:T(128)} %refs_0_.1, ...), custom_call_target="tpu_custom_call" | custom-call | tf_op jit(solution)/shard_map/pallas_call | solution.py:1064
  95.6 2.9 %shard_map.273 = (f32[3,64,128]{2,1,0:T(8,128)}, f32[64,128]{1,0:T(8,128)}, f32[64,512]{1,0:T(8,128)}, f32[64,512]{1,0:T(8,128)}, bf16[1024,512]{1,0:T(8,128)(2,...) custom-call(f32[32,512]{1,0:T(8,128)S(1)} %get-tuple-element.37.refs, ...), custom_call_target="tpu_custom_call" | custom-call | tf_op jit(solution)/shard_map/pallas_call | solution.py:1097

commit v9 on v8

--- a/solution.py
+++ b/solution.py
@@ -11,7 +11,7 @@
 f32, bf16 = jnp.float32, jnp.bfloat16
 HS = 64
 TR = 256
-TB = 256
+TB = 128
 BIG = 1e30
 EPS = 1e-5
 DOC = 512
@@ -857,18 +857,26 @@
         f = cm.order_ffn(j)
         cm.hook("chunk", j)
 
-        def tile(r, acc):
-            u = nn_dot(n2[r, :], cm.getu(f)) + bup[f]
-            a, ga = gelu_parts(u)
+        n = TILE["tile"]
+        spans = [slice(i * n, i * n + n) for i in range(seq // n)]
+
+        def lead(r):
+            return nn_dot(n2[r, :], cm.getu(f)) + bup[f], nn_dot(cot[r, :], cm.getd(f))
+
+        acc = jnp.zeros((1, F), f32)
+        ready = lead(spans[0])
+        for i, r in enumerate(spans):
+            ahead = lead(spans[i + 1]) if i + 1 < len(spans) else None
+            a, ga = gelu_parts(ready[0])
             a = a.astype(bf16)
-            g = (nn_dot(cot[r, :], cm.getd(f)) * ga).astype(bf16)
+            g = (ready[1] * ga).astype(bf16)
             act[r, :] = a
             gu[r, :] = g
             ffn[r, :] += nt_dot(a, cm.getd(f))
             gn[r, :] += nt_dot(g, cm.getu(f))
-            return acc + colsum(g.astype(f32))
-
-        bsum[f] = loop("tile", seq, tile, jnp.zeros((1, F), f32))
+            acc = acc + colsum(g.astype(f32))
+            ready = ahead
+        bsum[f] = acc
         cm.hook("chunk_mid", j)
 
         def wgrad(r, _):

time: 98.8 us -> 98 us (level)
  no operation moved by 1% of the time
where the time goes in v9:
time: 98 us; the launch traced here: 97.8 us
  Pallas kernels  96.4 us (98%)
  between operations  1.47 us (2%)
    pallas_call x1, Pallas kernels, run_linked(): pl.pallas_call(functools.partial(linked_kernel, most, ng, nt, tuple(bufs)...  93.5 us
    pallas_call x1, Pallas kernels, emit(): pl.pallas_call(functools.partial(emit_kernel, nb), out_shape=tuple((S(x.s...  2.86 us

profile of v9, /device:TPU:0, one launch (start us, length us, event | category | flops | bytes accessed | tf_op | source)
XLA Modules:
  0.0 97.8 jit_solution(11100977200621313999)
XLA Ops:
  1.3 93.5 %shard_map.272 = (bf16[1024,512]{1,0:T(8,128)(2,1)S(1)}, f32[1024,512]{1,0:T(8,128)S(1)}, f32[3,64,128]{2,1,0:T(8,128)S(1)}, f32[64,128]{1,0:T(8,128)S(1)}, f32[...) custom-call(s32[4]{0:T(128)} %refs_0_.1, ...), custom_call_target="tpu_custom_call" | custom-call | tf_op jit(solution)/shard_map/pallas_call | solution.py:1072
  94.8 2.9 %shard_map.273 = (f32[3,64,128]{2,1,0:T(8,128)}, f32[64,128]{1,0:T(8,128)}, f32[64,512]{1,0:T(8,128)}, f32[64,512]{1,0:T(8,128)}, bf16[1024,512]{1,0:T(8,128)(2,...) custom-call(f32[32,512]{1,0:T(8,128)S(1)} %get-tuple-element.37.refs, ...), custom_call_target="tpu_custom_call" | custom-call | tf_op jit(solution)/shard_map/pallas_call | solution.py:1105

commit v10 on v9

--- a/solution.py
+++ b/solution.py
@@ -531,11 +531,12 @@
         elif place == "start":
             for k in range(3):
                 self.WQ[t, g, c, :, 128 * k:128 * k + 128] = self.w_qkv[k].astype(bf16)
+            self.enter()
+            begin(*[self.q_plane(0, k) for k in planes], self.q_z(1))
+        elif place == "shards":
             self.WO[t, g, c] = self.w_out[...].astype(bf16)
             self.W2[t, 0, g, c] = self.w_up[...].astype(bf16)
             self.W2[t, 1, g, c] = self.w_down[...].astype(bf16)
-            self.enter()
-            begin(*[self.q_plane(0, k) for k in planes], self.q_z(1))
         elif place == "normed":
             begin(self.q_z(2))
         elif place == "masked":
@@ -1016,9 +1017,11 @@
             plain_hook(place)
             for i in (3, 4, 5, 6, 0, 7, 2, *range(8, 15), 1):
                 moves[i].start()
-            for i in range(3, 7):
+            moves[3].wait()
+        elif place == "row_in":
+            for i in range(4, 7):
                 moves[i].wait()
-        elif place == "row_in":
+            plain_hook("shards")
             for i in (0, 7, 2, *range(8, 15)):
                 moves[i].wait()
         elif place == "cot_in":

time: 98 us -> 98 us (level)
  no operation moved by 1% of the time
where the time goes in v10:
time: 98 us; the launch traced here: 97.8 us
  Pallas kernels  96.4 us (98%)
  between operations  1.47 us (2%)
    pallas_call x1, Pallas kernels, run_linked(): pl.pallas_call(functools.partial(linked_kernel, most, ng, nt, tuple(bufs)...  93.5 us
    pallas_call x1, Pallas kernels, emit(): pl.pallas_call(functools.partial(emit_kernel, nb), out_shape=tuple((S(x.s...  2.86 us

profile of v10, /device:TPU:0, one launch (start us, length us, event | category | flops | bytes accessed | tf_op | source)
XLA Modules:
  0.0 97.8 jit_solution(1630809450435791520)
XLA Ops:
  1.3 93.5 %shard_map.272 = (bf16[1024,512]{1,0:T(8,128)(2,1)S(1)}, f32[1024,512]{1,0:T(8,128)S(1)}, f32[3,64,128]{2,1,0:T(8,128)S(1)}, f32[64,128]{1,0:T(8,128)S(1)}, f32[...) custom-call(s32[4]{0:T(128)} %refs_0_.1, ...), custom_call_target="tpu_custom_call" | custom-call | tf_op jit(solution)/shard_map/pallas_call | solution.py:1075
  94.8 2.9 %shard_map.273 = (f32[3,64,128]{2,1,0:T(8,128)}, f32[64,128]{1,0:T(8,128)}, f32[64,512]{1,0:T(8,128)}, f32[64,512]{1,0:T(8,128)}, bf16[1024,512]{1,0:T(8,128)(2,...) custom-call(f32[32,512]{1,0:T(8,128)S(1)} %get-tuple-element.37.refs, ...), custom_call_target="tpu_custom_call" | custom-call | tf_op jit(solution)/shard_map/pallas_call | solution.py:1108
